TPU v7x, 32 devices: a whole 2x2x4 slice. The times are simulated.
32 devices in a mesh: gx: 4 (over x, core), gy: 4 (over z), sa: 2 (over y).
Axes of the slice: x: 2, y: 2, z: 4, core: 2. Of those that a mesh axis runs over, the one named last changes fastest.
Arguments:
- slab: float32 [2, 64, 512, 512], P(None, 'sa', 'gx', 'gy'), may hold values from -30 to 30, as said below
- factor_x: float32 [512, 256], P('gx'), may hold values from -1 to 1, as said below
- factor_y: float32 [512, 256], P('gy'), may hold values from -1 to 1, as said below
Outputs:
- gram_x: float32 [512, 512], P(('gx', 'gy', 'sa'))
- gram_y: float32 [512, 512], P('gy')
- core: float32 [2, 64, 256, 256], P(None, 'sa', 'gx', 'gy')
Inputs may be any that keep to these rules, and one draw needn't show every extreme that they name: `slab`: field values of a combustion state; rows of different x cells and species differ in scale. `factor_x`: the columns are orthonormal. `factor_y`: the columns are orthonormal.
All inputs are finite; a program needn't handle non-finite values.
Results may differ from a plain program's by a relative error of at most 0.000071.
Values sent between devices are 32-bit elements; how exact they have to be, the bound alone decides.
No kernel may reach another device: no remote copies, remote signals or barrier semaphores. Data moves between devices by JAX's collectives and lax.ppermute only.
A program may use at most 192 MiB of HBM per device.

v0:
```python
import jax
import jax.numpy as jnp
from jax import lax
from jax.sharding import PartitionSpec as P


def shards(slab, factor_x, factor_y):
    highest = lax.Precision.HIGHEST
    z_cells, s_local, x_local, y_local = slab.shape
    x_total = x_local * lax.axis_size("gx")
    y_total = y_local * lax.axis_size("gy")
    s_total = s_local * lax.axis_size("sa")
    core_rank = factor_x.shape[1]
    count_gx = lax.axis_size("gx")
    count_gy = lax.axis_size("gy")
    a_block = core_rank // count_gx
    b_block = core_rank // count_gy
    slice_rows = z_cells * s_local
    flat = slab.reshape((slice_rows, x_local, y_local))
    slices = lax.all_to_all(
        lax.all_to_all(flat, "gx", split_axis=0, concat_axis=1, tiled=True),
        "gy",
        split_axis=0,
        concat_axis=2,
        tiled=True,
    )
    whole_fx = lax.all_gather(factor_x, "gx", axis=0, tiled=True)
    whole_fy = lax.all_gather(factor_y, "gy", axis=0, tiled=True)
    local_gx = jnp.einsum(
        "rxy,rwy->xw", slices, slices, precision=highest, preferred_element_type=jnp.float32
    )
    local_gy = jnp.einsum(
        "rxy,rxw->yw", slices, slices, precision=highest, preferred_element_type=jnp.float32
    )
    gram_x = lax.psum_scatter(local_gx, ("gx", "gy", "sa"), scatter_dimension=0, tiled=True) / (
        y_total * z_cells * s_total
    )
    part_gy = lax.psum_scatter(local_gy, "gy", scatter_dimension=0, tiled=True)
    gram_y = lax.psum(part_gy, ("gx", "sa")) / (x_total * z_cells * s_total)
    along_x = jnp.einsum(
        "xa,rxy->ray", whole_fx, slices, precision=highest, preferred_element_type=jnp.float32
    )
    core_local = jnp.einsum(
        "ray,yb->rab", along_x, whole_fy, precision=highest, preferred_element_type=jnp.float32
    )
    returned = lax.all_to_all(
        lax.all_to_all(core_local, "gx", split_axis=1, concat_axis=0, tiled=True),
        "gy",
        split_axis=2,
        concat_axis=0,
        tiled=True,
    )
    per_slice = slice_rows // (count_gx * count_gy)
    ordered = returned.reshape((count_gy, count_gx, per_slice, a_block, b_block))
    ordered = jnp.transpose(ordered, (1, 0, 2, 3, 4))
    core = ordered.reshape((z_cells, s_local, a_block, b_block))
    return (gram_x, gram_y, core)


def solution(mesh):
    in_specs = (P(None, "sa", "gx", "gy"), P("gx", None), P("gy", None))
    out_specs = (P(("gx", "gy", "sa"), None), P("gy", None), P(None, "sa", "gx", "gy"))
    return jax.shard_map(shards, mesh=mesh, in_specs=in_specs, out_specs=out_specs, check_vma=False)
```

profile of v0, /device:TPU:0, one launch (start us, length us, event | category | flops | bytes accessed | tf_op | source)
XLA Modules:
  0.0 425.7 jit_solution(15394995978324955495)
XLA Ops:
  7.2 0.0 reduce-scatter.5.cloned.1.call-start
  7.2 52.6 %all_to_all.69 = f32[64,128,128]{2,1,0:T(8,128)S(1)} all-to-all(f32[64,128,128]{2,1,0:T(8,128)} %bitcast.55), channel_id=1, replica_groups=mesh['gx'=4,'gy'=4,'sa'=2] {'gx'}, dimensions={0} | all-to-all | bytes 8388608 | tf_op jit(solution)/shard_map/all_to_all | solution.py:21
  59.8 0.5 copy.28
  60.3 98.4 %all_to_all.70 = f32[16,512,128]{2,1,0:T(8,128)} all-to-all(f32[16,512,128]{2,1,0:T(8,128)S(1)} %bitcast.48), channel_id=1, replica_groups=mesh['gx'=4,'gy'=4,'sa'=2] {'gy'}, dimensions={0} | all-to-all | bytes 8388608 | tf_op jit(solution)/shard_map/all_to_all | solution.py:20
  158.6 5.2 %copy.30 = f32[4,512,4,128]{1,3,2,0:T(8,128)} copy(f32[4,512,4,128]{3,1,0,2:T(8,128)} %bitcast.46) | data formatting | bytes 8388608 | tf_op jit(solution)/shard_map/all_to_all | solution.py:20
  163.9 10.4 %convolution_bitcast_fusion = f32[512,512]{1,0:T(8,128)} fusion(f32[4,512,512]{1,2,0:T(8,128)} %bitcast.44), kind=kOutput, calls=%fused_computation.6 | convolution fusion | flops 6442450944 | bytes 5242880 | tf_op jit(solution)/shard_map/rxy,rxw->yw/dot_general | solution.py:32
  174.3 0.0 reduce-scatter.5.cloned.1.call-update
  174.3 0.0 reduce-scatter.3.cloned.1.call-start
  174.4 6.6 %all_gather.6 = f32[512,256]{1,0:T(8,128)S(1)} all-gather(f32[128,256]{1,0:T(8,128)S(1)} %copy-done.1), channel_id=1, replica_groups=mesh['gx'=4,'gy'=4,'sa'=2] {'gx'}, dimensions={0}, use_global_device_ids=true | all-gather | bytes 655360 | tf_op jit(solution)/shard_map/all_gather | solution.py:27
  181.0 22.1 %all_gather.7 = f32[512,256]{1,0:T(8,128)S(1)} all-gather(f32[128,256]{1,0:T(8,128)S(1)} %copy-done.2), channel_id=1, replica_groups=mesh['gx'=4,'gy'=4,'sa'=2] {'gy'}, dimensions={0}, use_global_device_ids=true | all-gather | bytes 655360 | tf_op jit(solution)/shard_map/all_gather | solution.py:28
  203.2 5.4 %fusion.9 = f32[4,512,256]{2,1,0:T(8,128)S(1)} fusion(f32[4,512,512]{1,2,0:T(8,128)} %bitcast.45, f32[512,256]{1,0:T(8,128)S(1)} %all_gather.6), kind=kOutput, calls=%fused_computation.8 | convolution fusion | flops 3221225472 | bytes 6815744 | tf_op jit(solution)/shard_map/xa,rxy->ray/dot_general | solution.py:40
  208.6 7.9 %fusion.5 = f32[512,512]{1,0:T(8,128)} fusion(f32[4,4,512,128]{3,2,1,0:T(8,128)S(1)} %bitcast.47), kind=kOutput, calls=%fused_computation.5 | convolution fusion | flops 6442450944 | bytes 5242880 | tf_op jit(solution)/shard_map/rxy,rwy->xw/dot_general | solution.py:29
  216.5 0.0 reduce-scatter.3.cloned.1.call-update
  216.5 3.4 fusion.3
  219.9 0.7 copy.33
  220.6 16.9 %all_to_all.71 = f32[4,256,256]{2,0,1:T(4,128)S(1)} all-to-all(f32[4,256,256]{2,0,1:T(4,128)S(1)} %copy.33), channel_id=1, replica_groups=mesh['gx'=4,'gy'=4,'sa'=2] {'gx'}, dimensions={1} | all-to-all | bytes 2097152 | tf_op jit(solution)/shard_map/all_to_all | solution.py:47
  237.5 0.2 copy.34
  237.7 0.1 copy.35
  237.8 1.3 copy.36
  239.1 2.4 reshape.23
  241.5 3.9 all-to-all-start.3
  245.4 0.7 all-reduce.2.cloned.1.call-update
  246.1 107.8 %reduce-scatter.3.cloned.1.call-done = f32[16,512]{1,0:T(8,128)} async-done(((f32[512,512]{1,0:T(8,128)}), f32[16,512]{1,0:T(8,128)}) %reduce-scatter.3.cloned.1.call-update) | async-done | bytes 32784 | tf_op jit(solution)/shard_map/reduce_scatter | solution.py:35
  353.9 1.4 broadcast_multiply_fusion.1
  355.3 51.8 %all-reduce.2.cloned.1.call-done = f32[128,512]{1,0:T(8,128)} async-done(((f32[128,512]{1,0:T(8,128)}), f32[128,512]{1,0:T(8,128)}) %all-reduce.2.cloned.1.call-update) | async-done | bytes 262160 | tf_op jit(solution)/shard_map/psum | solution.py:39
  407.1 1.7 broadcast_multiply_fusion
  408.8 0.5 broadcast.2
  409.3 3.7 reduce
  413.0 1.0 reshape.24
  414.0 1.8 copy.44
  415.8 1.9 copy.38
  417.7 1.5 copy.39
  (9 shorter events, 0.0 us)
Async XLA Ops:
  7.2 238.2 %reduce-scatter.5.cloned.1.call-start = ((), (), s32[]{:S(2)}) async-start(), calls=%async_computation.7 | async-start | bytes 1310720 | tf_op jit(solution)/shard_map/reduce_scatter | solution.py:38
  163.9 10.5 %copy-start.1 = (f32[128,256]{1,0:T(8,128)S(1)}, f32[128,256]{1,0:T(8,128)}, u32[]{:S(2)}) copy-start(f32[128,256]{1,0:T(8,128)} %param.4) | copy-start | bytes 393220
  163.9 17.1 %copy-start.2 = (f32[128,256]{1,0:T(8,128)S(1)}, f32[128,256]{1,0:T(8,128)}, u32[]{:S(2)}) copy-start(f32[128,256]{1,0:T(8,128)} %param.5) | copy-start | bytes 393220
  174.3 179.6 %reduce-scatter.3.cloned.1.call-start = ((), (), s32[]{:S(2)}) async-start(), calls=%async_computation.6 | async-start | bytes 1081344 | tf_op jit(solution)/shard_map/reduce_scatter | solution.py:35
  174.4 34.2 %copy-start = (f32[16,512,128]{2,1,0:T(8,128)S(1)}, f32[16,512,128]{2,1,0:T(8,128)}, u32[]{:S(2)}) copy-start(f32[16,512,128]{2,1,0:T(8,128)} %all_to_all.70) | copy-start | bytes 12582916
  241.5 167.3 %all-to-all-start.3 = ((f32[4,1,65536]{2,1,0:T(1,128)}), f32[4,1,65536]{2,1,0:T(1,128)S(1)}, u32[]{:S(2)}, u32[]{:S(2)}) async-start(f32[4,1,65536]{2,1,0:T(1,128)} %reshape.23), calls=%async_computation.5 | async-start | bytes 2097152 | tf_op jit(solution)/shard_map/all_to_all | solution.py:46
  245.4 161.7 %all-reduce.2.cloned.1.call-start = ((), (), s32[]{:S(2)}) async-start(), calls=%async_computation.8 | async-start | bytes 524288 | tf_op jit(solution)/shard_map/psum | solution.py:39
Sparse Core Ops, SparseCore 0:
  174.4 34.4 reduce-scatter.4
  216.6 137.2 reduce-scatter.2
  357.0 50.0 all-reduce.1
where the time goes:
time: 426 us
  blocking collectives  197 us (46%)
  waiting for transfers between devices  160 us (38%)
  matrix products  27.1 us (6%)
  local copies, waits for them, and re-layouts  17.1 us (4%)
  between operations  13.8 us (3%)
  other arithmetic  6.73 us (2%)
    reduce_scatter x1, waiting for transfers between devices, shards(): lax.psum_scatter(local_gx, ('gx', 'gy', 'sa'), scatter_dimension=0, tiled...  108 us
    all_to_all x1, blocking collectives, shards(): lax.all_to_all(lax.all_to_all(flat, 'gx', split_axis=0, concat_axis=1, ti...  98.4 us
    all_to_all x1, blocking collectives, shards(): lax.all_to_all(flat, 'gx', split_axis=0, concat_axis=1, tiled=True)  52.6 us
    psum x1, waiting for transfers between devices, shards(): gram_y = lax.psum(part_gy, ('gx', 'sa')) / (x_total * z_cells * s_total)  51.8 us
    all_gather x1, blocking collectives, shards(): whole_fy = lax.all_gather(factor_y, 'gy', axis=0, tiled=True)  22.1 us
    all_to_all x1, blocking collectives, shards(): lax.all_to_all(core_local, 'gx', split_axis=1, concat_axis=0, tiled=True)  16.9 us
    dot_general x1, matrix products, shards(): jnp.einsum('rxy,rxw->yw', slices, slices, precision=highest, preferred_el...  10.4 us
  transfers between devices with their start and end apart: 4, of which 2 were waited for; matrix products, arithmetic and copies ran while one was open for 6% of the time, Pallas kernels for 0%

commit v1 on v0

v1 whole, which is shorter than its diff:
```python
import functools

import jax
import jax.numpy as jnp
from jax import lax
from jax.experimental import pallas as pl
from jax.experimental.pallas import tpu as pltpu
from jax.sharding import PartitionSpec as P


CHUNKS = 4
F32 = jnp.float32
BF16 = jnp.bfloat16
ROWS = (((0,), (0,)), ((), ()))
LANES = (((1,), (1,)), ((), ()))
PLAIN = (((1,), (0,)), ((), ()))


def swap(value, axis, offset):
    size = lax.axis_size(axis)
    return lax.ppermute(value, axis, [(i, i ^ offset) for i in range(size)])


def far_first(size):
    return [k for k in range(1, size) if k >= size // 2] + [k for k in range(1, size // 2)]


def pick(value, index, axis):
    return lax.dynamic_index_in_dim(value, index, axis, keepdims=False)


def split(value):
    high = value.astype(BF16)
    return high, (value - high.astype(F32)).astype(BF16)


def dot3(left, right, dims):
    dot = functools.partial(lax.dot_general, dimension_numbers=dims, preferred_element_type=F32)
    return dot(left[0], right[0]) + (dot(left[0], right[1]) + dot(left[1], right[0]))


def whole_spec(shape):
    return pl.BlockSpec(shape, lambda i, s: (0,) * len(shape))


def fy_kernel(ny, nx, s_ref, own_ref, *refs):
    pieces, (high_ref, low_ref, scratch) = refs[:nx], refs[nx:]
    depth = own_ref.shape[0]
    small = depth // nx
    scratch[pl.ds(pl.multiple_of(s_ref[1] * depth, depth), depth), :] = own_ref[...]
    for o in range(nx):
        for k in range(1, ny):
            start = (s_ref[1] ^ k) * depth + (s_ref[0] ^ o) * small
            scratch[pl.ds(pl.multiple_of(start, small), small), :] = pieces[o][k - 1]
    high_ref[...], low_ref[...] = split(scratch[...])


def gather_fy(sizes, where, factor_y, pieces):
    nx, ny = sizes[:2]
    depth, rank = factor_y.shape
    shape = (ny * depth, rank)
    return pl.pallas_call(
        functools.partial(fy_kernel, ny, nx),
        grid_spec=pltpu.PrefetchScalarGridSpec(
            num_scalar_prefetch=1,
            grid=(1,),
            in_specs=[whole_spec(factor_y.shape)] + [whole_spec(p.shape) for p in pieces],
            out_specs=[whole_spec(shape)] * 2,
            scratch_shapes=[pltpu.VMEM(shape, F32)],
        ),
        out_shape=[jax.ShapeDtypeStruct(shape, BF16)] * 2,
        cost_estimate=pl.CostEstimate(flops=1000, bytes_accessed=1 << 20, transcendentals=0),
    )(where, factor_y, *pieces)


def chunk_kernel(sizes, first, last, s_ref, *refs):
    nx, ny, _ = sizes
    fields, refs = refs[:ny], refs[ny:]
    (fyh_ref, fyl_ref, fxt_ref), refs = refs[:3], refs[3:]
    if not first:
        gin_ref, refs = refs[0], refs[1:]
    keep_ref, sent_ref, refs = refs[0], refs[1], refs[2:]
    if last:
        gkeep_ref, gsent_ref, wide_ref, gram_ref = refs
    else:
        gram_ref, wide_ref = refs
    step = pl.program_id(0)
    pair, x_local, y_local = fields[0].shape
    me_x, me_y = s_ref[0], s_ref[1]
    for k in range(ny):
        start = pl.multiple_of((me_y ^ k) * y_local, y_local)
        wide_ref[:, pl.ds(start, y_local)] = fields[k][...].reshape(pair * x_local, y_local)
    wide = split(wide_ref[...])
    gram = dot3(wide, wide, ROWS)

    @pl.when(step == 0)
    def _():
        gram_ref[...] = gram if first else gin_ref[...] + gram

    @pl.when(step > 0)
    def _():
        gram_ref[...] += gram

    half = dot3(wide, (fyh_ref[...], fyl_ref[...]), PLAIN)
    b_block = half.shape[1] // ny
    paired = jnp.concatenate(
        [
            half[p * x_local : (p + 1) * x_local, q * b_block : (q + 1) * b_block]
            for q in range(ny)
            for p in range(pair)
        ],
        axis=1,
    )
    a_block = fxt_ref.shape[0] // nx
    fx = jnp.concatenate(
        [
            fxt_ref[pl.ds(pl.multiple_of((me_x ^ o) * a_block, a_block), a_block), :]
            for o in range(nx)
        ],
        axis=0,
    )
    full = dot3(split(fx), split(paired), PLAIN)
    lanes = pair * b_block
    for o in range(nx):
        target = sent_ref if o % 2 else keep_ref
        for q in range(ny):
            target[o // 2, q, 0] = full[
                o * a_block : (o + 1) * a_block, q * lanes : (q + 1) * lanes
            ]
    if last:

        @pl.when(step == pl.num_programs(0) - 1)
        def _():
            part = y_local // 2
            bit = me_x & 1
            for k in range(ny):
                mine = pl.multiple_of(k * y_local + bit * part, part)
                other = pl.multiple_of(k * y_local + (1 - bit) * part, part)
                gkeep_ref[k] = gram_ref[pl.ds(mine, part), :]
                gsent_ref[k] = gram_ref[pl.ds(other, part), :]


def chunk_terms(sizes, where, flat, offset, parts, fy, fxt, gram, last):
    nx, ny, _ = sizes
    n, x_local, y_local = parts[0].shape
    own = flat.shape[0] // ny
    rank = fxt.shape[0]
    pairs = n // 2
    width = ny * y_local
    a_block, b_block = rank // nx, rank // ny
    half = (nx // 2, ny, pairs, a_block, 2 * b_block)
    field = (2, x_local, y_local)
    specs = [pl.BlockSpec(field, lambda i, s: ((s[1] * own + offset) // 2 + i, 0, 0))]
    specs += [pl.BlockSpec(field, lambda i, s: (i, 0, 0))] * (ny - 1)
    specs += [whole_spec(fy[0].shape)] * 2 + [whole_spec(fxt.shape)]
    args = [flat, *parts, *fy, fxt]
    first = gram is None
    if not first:
        specs.append(whole_spec((width, width)))
        args.append(gram)
    half_spec = pl.BlockSpec(
        (nx // 2, ny, 1, a_block, 2 * b_block), lambda i, s: (0, 0, i, 0, 0)
    )
    out_specs = [half_spec] * 2
    out_shape = [jax.ShapeDtypeStruct(half, F32)] * 2
    scratch = [pltpu.VMEM((2 * x_local, width), F32)]
    if last:
        gshape = (ny, y_local // 2, width)
        out_specs += [whole_spec(gshape)] * 2
        out_shape += [jax.ShapeDtypeStruct(gshape, F32)] * 2
        scratch.append(pltpu.VMEM((width, width), F32))
    else:
        out_specs.append(whole_spec((width, width)))
        out_shape.append(jax.ShapeDtypeStruct((width, width), F32))
    flops = 2 * n * x_local * (width * width + width * rank + rank * rank) * 3
    return pl.pallas_call(
        functools.partial(chunk_kernel, sizes, first, last),
        grid_spec=pltpu.PrefetchScalarGridSpec(
            num_scalar_prefetch=1,
            grid=(pairs,),
            in_specs=specs,
            out_specs=out_specs,
            scratch_shapes=scratch,
        ),
        out_shape=out_shape,
        cost_estimate=pl.CostEstimate(flops=flops, bytes_accessed=1 << 22, transcendentals=0),
    )(where, *args)


def gram_x_kernel(sizes, s_ref, *refs):
    nx = sizes[0]
    fields, (keep_ref, sent_ref, tall_ref, gram_ref) = refs[:nx], refs[nx:]
    pair, x_local, y_local = fields[0].shape
    me_x = s_ref[0]
    for o in range(nx):
        start = pl.multiple_of((me_x ^ o) * x_local, x_local)
        for p in range(pair):
            tall_ref[pl.ds(start, x_local), p * y_local : (p + 1) * y_local] = fields[o][p]
    tall = split(tall_ref[...])
    gram = dot3(tall, tall, LANES)
    step = pl.program_id(0)

    @pl.when(step == 0)
    def _():
        gram_ref[...] = gram

    @pl.when(step > 0)
    def _():
        gram_ref[...] += gram

    @pl.when(step == pl.num_programs(0) - 1)
    def _():
        bit = me_x & 1
        for j in range(nx // 2):
            mine = pl.multiple_of((2 * j + bit) * x_local, x_local)
            other = pl.multiple_of((2 * j + 1 - bit) * x_local, x_local)
            keep_ref[j] = gram_ref[pl.ds(mine, x_local), :]
            sent_ref[j] = gram_ref[pl.ds(other, x_local), :]


def gram_x_terms(sizes, where, flat, parts):
    nx = sizes[0]
    own, x_local, y_local = parts[0].shape
    width = nx * x_local
    field = (2, x_local, y_local)
    specs = [pl.BlockSpec(field, lambda i, s: (s[0] * own // 2 + i, 0, 0))]
    specs += [pl.BlockSpec(field, lambda i, s: (i, 0, 0))] * (nx - 1)
    half = (nx // 2, x_local, width)
    flops = 2 * own * y_local * width * width * 3
    return pl.pallas_call(
        functools.partial(gram_x_kernel, sizes),
        grid_spec=pltpu.PrefetchScalarGridSpec(
            num_scalar_prefetch=1,
            grid=(own // 2,),
            in_specs=specs,
            out_specs=[whole_spec(half)] * 2,
            scratch_shapes=[pltpu.VMEM((width, 2 * y_local), F32), pltpu.VMEM((width, width), F32)],
        ),
        out_shape=[jax.ShapeDtypeStruct(half, F32)] * 2,
        cost_estimate=pl.CostEstimate(flops=flops, bytes_accessed=1 << 23, transcendentals=0),
    )(where, flat, *parts)


def unpack_kernel(ny, n, own, s_ref, *refs):
    parts, out_ref = refs[:-1], refs[-1]
    chunks = len(parts) // ny
    b_block = out_ref.shape[2]
    for k in range(ny):
        for c in range(chunks):
            part = parts[c * ny + k]
            for j in range(n // 2):
                base = (s_ref[1] ^ k) * own + c * n + 2 * j
                out_ref[base] = part[j, :, :b_block]
                out_ref[base + 1] = part[j, :, b_block:]


def unpack(sizes, where, parts, rows):
    ny = sizes[1]
    half, a_block, lanes = parts[0].shape
    shape = (rows, a_block, lanes // 2)
    return pl.pallas_call(
        functools.partial(unpack_kernel, ny, 2 * half, rows // ny),
        grid_spec=pltpu.PrefetchScalarGridSpec(
            num_scalar_prefetch=1,
            grid=(1,),
            in_specs=[whole_spec(p.shape) for p in parts],
            out_specs=whole_spec(shape),
        ),
        out_shape=jax.ShapeDtypeStruct(shape, F32),
        cost_estimate=pl.CostEstimate(flops=1000, bytes_accessed=3 << 20, transcendentals=0),
    )(where, *parts)


def local_step(slab, factor_x, factor_y):
    z_cells, s_local, x_local, y_local = slab.shape
    sizes = nx, ny, ns = tuple(lax.axis_size(a) for a in ("gx", "gy", "sa"))
    me_x, me_y, me_s = (lax.axis_index(a) for a in ("gx", "gy", "sa"))
    where = jnp.stack([me_x, me_y, me_s]).astype(jnp.int32)
    rank = factor_x.shape[1]
    a_block, b_block = rank // nx, rank // ny
    rows = z_cells * s_local
    flat = slab.reshape((rows, x_local, y_local))
    own_y, own_x = rows // ny, rows // nx
    n = own_y // CHUNKS
    x_total, y_total, s_total = x_local * nx, y_local * ny, s_local * ns

    source = flat
    along_y = []
    for c in range(CHUNKS):
        cut = {
            k: lax.dynamic_slice_in_dim(source, (me_y ^ k) * own_y + c * n, n, 0)
            for k in far_first(ny)
        }
        source, cut = lax.optimization_barrier((source, cut))
        along_y.append({k: swap(cut[k], "gy", k) for k in far_first(ny)})
        if c == 0:
            mine = pick(factor_y.reshape((nx, y_local // nx, rank)), me_x, 0)
            crossed = jnp.stack([swap(mine, "gy", k) for k in range(1, ny)])
            pieces = [crossed] + [swap(crossed, "gx", o) for o in range(1, nx)]
            cut = {
                k: lax.dynamic_slice_in_dim(source, (me_x ^ k) * own_x, own_x, 0)
                for k in far_first(nx)
            }
            source, cut = lax.optimization_barrier((source, cut))
            along_x = {k: swap(cut[k], "gx", k) for k in far_first(nx)}
    fy = gather_fy(sizes, where, factor_y, pieces)
    fxt = factor_x.T

    gram = None
    core_parts = []
    for c in range(CHUNKS):
        parts = [along_y[c][k] for k in range(1, ny)]
        last = c == CHUNKS - 1
        out = chunk_terms(sizes, where, flat, c * n, parts, fy, fxt, gram, last)
        keep, sent, gram = out[0], out[1], out[2:]
        if last:
            gkeep, gsent = gram
            ggot = swap(gsent, "gx", 1)
        else:
            gram = gram[0]
        bit = 1
        while bit < nx:
            got = swap(sent, "gx", bit)
            keep = keep + got
            if 2 * bit < nx:
                sent = keep[1::2]
                keep = keep[0::2]
            bit *= 2
        keep = keep[0]
        z_parts = [pick(keep, me_y ^ k, 0) for k in range(ny)]
        core_parts += [swap(z_parts[k], "gy", k) if k else z_parts[0] for k in range(ny)]
    core = unpack(sizes, where, core_parts, rows)
    core = core.reshape((z_cells, s_local, a_block, b_block))

    keep, sent = gram_x_terms(sizes, where, flat, [along_x[k] for k in range(1, nx)])
    got = swap(sent, "gx", 1)
    bit = 2
    while bit < nx:
        keep = keep.reshape((-1, 2, x_local, x_total))
        got = got.reshape((-1, 2, x_local, x_total))
        mybit = (me_x // bit) & 1
        sent = pick(keep, 1 - mybit, 1) + pick(got, 1 - mybit, 1)
        keep = pick(keep, mybit, 1) + pick(got, mybit, 1)
        got = swap(sent, "gx", bit)
        bit *= 2
    total = (keep[0] + got[0]).reshape((ny, ns, -1, x_total))
    keep = pick(total, me_s, 1)
    for k in range(1, ns):
        keep = keep + swap(pick(total, me_s ^ k, 1), "sa", k)
    gram_x = pick(keep, me_y, 0)
    for k in range(1, ny):
        gram_x = gram_x + swap(pick(keep, me_y ^ k, 0), "gy", k)
    gram_x = gram_x / (y_total * z_cells * s_total)

    keep, got = gkeep, ggot
    bit = 2
    while bit < nx:
        shape = (ny, 2, keep.shape[1] // 2, y_total)
        keep, got = keep.reshape(shape), got.reshape(shape)
        mybit = (me_x // bit) & 1
        sent = pick(keep, 1 - mybit, 1) + pick(got, 1 - mybit, 1)
        keep = pick(keep, mybit, 1) + pick(got, mybit, 1)
        got = swap(sent, "gx", bit)
        bit *= 2
    total = (keep + got).reshape((ny, ns, -1, y_total))
    keep = pick(total, me_s, 1)
    for k in range(1, ns):
        keep = keep + swap(pick(total, me_s ^ k, 1), "sa", k)
    row = pick(keep, me_y, 0)
    for k in range(1, ny):
        row = row + swap(pick(keep, me_y ^ k, 0), "gy", k)
    row = row / (x_total * z_cells * s_total)
    both = jnp.stack([row] + [swap(row, "sa", k) for k in range(1, ns)])
    cur = jnp.concatenate([pick(both, me_s ^ k, 0) for k in range(ns)], axis=0)
    bit = nx // 2
    while bit:
        got = swap(cur, "gx", bit)
        high = (me_x // bit) % 2 == 1
        cur = jnp.concatenate([jnp.where(high, got, cur), jnp.where(high, cur, got)], axis=0)
        bit //= 2
    return (gram_x, cur, core)


def solution(mesh):
    in_specs = (P(None, "sa", "gx", "gy"), P("gx", None), P("gy", None))
    out_specs = (P(("gx", "gy", "sa"), None), P("gy", None), P(None, "sa", "gx", "gy"))
    return jax.shard_map(
        local_step, mesh=mesh, in_specs=in_specs, out_specs=out_specs, check_vma=False
    )
```

time: 426 us -> 259 us (0.61)
  blocking collectives: 197 us -> 0 us
  starting transfers between devices: 3.96 us -> 94.7 us
  waiting for transfers between devices: 160 us -> 82.2 us
  Pallas kernels: 0 us -> 45.9 us
  matrix products: 27.1 us -> 0 us
  between operations: 13.8 us -> 1.18 us
  other arithmetic: 6.73 us -> 13.2 us
    all_to_all x3 -> x0, blocking collectives: 168 us -> none  [the longest x1 98.4 us: shards(): lax.all_to_all(lax.all_to_all(flat, 'gx', split_axis=0, concat_axis=1, ti...]
    reduce_scatter x2 -> x0, waiting for transfers between devices: 108 us -> none  [the longest x1 108 us: shards(): lax.psum_scatter(local_gx, ('gx', 'gy', 'sa'), scatter_dimension=0, tiled...]
    ppermute x0 -> x56, starting transfers between devices: none -> 94.7 us  [swap(): return lax.ppermute(value, axis, [(i, i ^ offset) for i in range(size)])]
    ppermute x0 -> x56, waiting for transfers between devices: none -> 82.2 us  [swap(): return lax.ppermute(value, axis, [(i, i ^ offset) for i in range(size)])]
    psum x1 -> x0, waiting for transfers between devices: 51.8 us -> none  [shards(): gram_y = lax.psum(part_gy, ('gx', 'sa')) / (x_total * z_cells * s_total)]
    pallas_call x0 -> x7, Pallas kernels: none -> 45.9 us  [the longest x4 29.7 us: chunk_terms(): pl.pallas_call(functools.partial(chunk_kernel, sizes, first, last), grid_...]
    all_gather x2 -> x0, blocking collectives: 28.8 us -> none  [the longest x1 22.1 us: shards(): whole_fy = lax.all_gather(factor_y, 'gy', axis=0, tiled=True)]
    dot_general x4 -> x0, matrix products: 27.1 us -> none  [the longest x1 10.4 us: shards(): jnp.einsum('rxy,rxw->yw', slices, slices, precision=highest, preferred_el...]
  transfers between devices with their start and end apart: 4 -> 56, of which waited for: 2 -> 18; matrix products, arithmetic and copies ran while one was open for 6% -> 11% of each run, Pallas kernels for 0% -> 15%
where the time goes in v1:
time: 259 us; the launch traced here: 258 us
  starting transfers between devices  94.7 us (37%)
  waiting for transfers between devices  82.2 us (32%)
  Pallas kernels  45.9 us (18%)
  local copies, waits for them, and re-layouts  21 us (8%)
  other arithmetic  13.2 us (5%)
    ppermute x56, starting transfers between devices, swap(): return lax.ppermute(value, axis, [(i, i ^ offset) for i in range(size)])  94.7 us
    ppermute x56, waiting for transfers between devices, swap(): return lax.ppermute(value, axis, [(i, i ^ offset) for i in range(size)])  82.2 us
    pallas_call x4, Pallas kernels, chunk_terms(): pl.pallas_call(functools.partial(chunk_kernel, sizes, first, last), grid_...  29.7 us
    pallas_call x1, Pallas kernels, gram_x_terms(): pl.pallas_call(functools.partial(gram_x_kernel, sizes), grid_spec=pltpu.P...  9.89 us
    add x8, other arithmetic, local_step(): keep = keep + got  6.51 us
    dynamic_slice x4, local copies, waits for them, and re-layouts, local_step(): lax.dynamic_slice_in_dim(source, (me_y ^ k) * own_y + c * n, n, 0)  6.13 us
    unnamed x65, local copies, waits for them, and re-layouts  5.71 us
  transfers between devices with their start and end apart: 56, of which 18 were waited for; matrix products, arithmetic and copies ran while one was open for 11% of the time, Pallas kernels for 15%

profile of v1, /device:TPU:0, one launch (start us, length us, event | category | flops | bytes accessed | tf_op | source)
XLA Modules:
  0.0 258.1 jit_solution(9119288608024447556)
XLA Ops:
  1.4 5.1 %collective-permute-start.14 = (f32[32,256]{1,0:T(8,128)S(1)}, f32[32,256]{1,0:T(8,128)S(1)}, u32[]{:S(2)}, u32[]{:S(2)}) collective-permute-start(f32[32,256]{1,0:T(8,128)S(1)} %dynamic-slice_bitcast_fusion.21), channel_id=1, source_target_pairs={{0,6},{2,4},{4,2},{6,0},{1,7},{3,5},{5,3},{7,1},{8,14},{10,12},{12... | collective-permute-start | bytes 98312 | tf_op jit(solution)/shard_map/ppermute | solution.py:21
  8.2 3.5 %constant_dynamic-slice_fusion.9 = (f32[16,128,128]{2,1,0:T(8,128)S(1)}, f32[16,128,128]{2,1,0:T(8,128)}, f32[16,128,128]{2,1,0:T(8,128)}) fusion(f32[64,128,128]{2,1,0:T(8,128)} %bitcast.105, s32[]{:T(128)S(6)} %select_n.156, s32[]{:T(128)S(6)} %select_n.155, s32[]{:T(128)S(6)} %select_n.154), kind=kLoop, calls=%fused_computation.70 | loop fusion | bytes 6291468 | tf_op jit(solution)/shard_map/dynamic_slice | solution.py:301
  12.9 1.9 constant_dynamic-slice_fusion.3
  20.1 2.4 collective-permute-start.25
  24.6 3.9 %collective-permute-start.26 = (f32[4,128,128]{2,1,0:T(8,128)S(1)}, f32[4,128,128]{2,1,0:T(8,128)}, u32[]{:S(2)}, u32[]{:S(2)}) collective-permute-start(f32[4,128,128]{2,1,0:T(8,128)S(1)} %get-tuple-element.61), channel_id=1, source_target_pairs={{0,6},{2,4},{4,2},{6,0},{1,7},{3,5},{5,3},{7,1},{8,14},{10,12},{12... | collective-permute-start | bytes 786440 | tf_op jit(solution)/shard_map/ppermute | solution.py:21
  29.6 7.0 %collective-permute-done.24.refs_1_ = f32[4,128,128]{2,1,0:T(8,128)S(1)} collective-permute-done((f32[4,128,128]{2,1,0:T(8,128)S(1)}, f32[4,128,128]{2,1,0:T(8,128)S(1)}, u32[]{:S(2)}, u32[]{:S(2)}) %collective-permute-start.24) | collective-permute-done | bytes 262176 | tf_op jit(solution)/shard_map/ppermute | solution.py:21
  36.6 7.6 %collective-permute-start.23 = (f32[4,128,128]{2,1,0:T(8,128)S(1)}, f32[4,128,128]{2,1,0:T(8,128)}, u32[]{:S(2)}, u32[]{:S(2)}) collective-permute-start(f32[4,128,128]{2,1,0:T(8,128)S(1)} %get-tuple-element.58), channel_id=1, source_target_pairs={{0,6},{2,4},{4,2},{6,0},{1,7},{3,5},{5,3},{7,1},{8,14},{10,12},{12... | collective-permute-start | bytes 786440 | tf_op jit(solution)/shard_map/ppermute | solution.py:21
  44.2 1.9 constant_dynamic-slice_fusion
  48.5 2.7 %shard_map.59 = (bf16[512,256]{1,0:T(8,128)(2,1)}, bf16[512,256]{1,0:T(8,128)(2,1)}) custom-call(s32[3]{0:T(128)} %pad_add_fusion.s_ref, f32[128,256]{1,0:T(8,128)} %own_ref.1, f32[3,32,256]{2,1,0:T(8,128)} %copy-done.7, f32[3,32,256]{2,1,0:T(8,128)} %copy-done.14, f32[3,32,256]{2,1,0:T(8,128)} %copy-done.15, f32[3,32,256]{2,1,0:T(8,128)} %collective-permute-done.17.refs_3_), custom_call_target="tpu_custom_call" | custom-call | flops 1000 | bytes 1048576 | tf_op jit(solution)/shard_map/pallas_call | solution.py:62
  51.4 7.1 %shard_map.60 = (f32[2,4,2,64,128]{4,3,2,1,0:T(8,128)}, f32[2,4,2,64,128]{4,3,2,1,0:T(8,128)}, f32[512,512]{1,0:T(8,128)}) custom-call(s32[3]{0:T(128)} %pad_add_fusion.s_ref, f32[64,128,128]{2,1,0:T(8,128)} %bitcast.109, f32[4,128,128]{2,1,0:T(8,128)} %copy-done.8, f32[4,128,128]{2,1,0:T(8,128)} %collective-permute-done.25.refs_2_, ...), custom_call_target="tpu_custom_call" | custom-call | flops 1409286144 | bytes 4194304 | tf_op jit(solution)/shard_map/pallas_call | solution.py:176
  58.4 21.9 %collective-permute-start.9 = (f32[4,128,128]{2,1,0:T(8,128)}, f32[4,128,128]{2,1,0:T(8,128)S(1)}, u32[]{:S(2)}, u32[]{:S(2)}) collective-permute-start(f32[4,128,128]{2,1,0:T(8,128)} %get-tuple-element.48), channel_id=1, source_target_pairs={{0,2},{2,0},{4,6},{6,4},{1,3},{3,1},{5,7},{7,5},{8,10},{10,8},{12,... | collective-permute-start | bytes 786440 | tf_op jit(solution)/shard_map/ppermute | solution.py:21
  80.4 2.4 collective-permute-start.11
  82.8 7.5 %shard_map.61 = (f32[2,4,2,64,128]{4,3,2,1,0:T(8,128)}, f32[2,4,2,64,128]{4,3,2,1,0:T(8,128)}, f32[512,512]{1,0:T(8,128)}) custom-call(s32[3]{0:T(128)} %pad_add_fusion.s_ref, f32[64,128,128]{2,1,0:T(8,128)} %bitcast.110, f32[4,128,128]{2,1,0:T(8,128)} %collective-permute-done.21.refs_1_, f32[4,128,128]{2,1,0:T(8,128)} %collective-permute-done.22.refs_2_, ...), custom_call_target="tpu_custom_call" | custom-call | flops 1409286144 | bytes 4194304 | tf_op jit(solution)/shard_map/pallas_call | solution.py:176
  91.2 7.5 %shard_map.62 = (f32[2,4,2,64,128]{4,3,2,1,0:T(8,128)}, f32[2,4,2,64,128]{4,3,2,1,0:T(8,128)}, f32[512,512]{1,0:T(8,128)}) custom-call(s32[3]{0:T(128)} %pad_add_fusion.s_ref, f32[64,128,128]{2,1,0:T(8,128)} %bitcast.111, f32[4,128,128]{2,1,0:T(8,128)} %collective-permute-done.18.refs_1_, f32[4,128,128]{2,1,0:T(8,128)} %copy-done.9, ...), custom_call_target="tpu_custom_call" | custom-call | flops 1409286144 | bytes 4194304 | tf_op jit(solution)/shard_map/pallas_call | solution.py:176
  98.8 10.2 %collective-permute-done.10.refs_2_ = f32[4,128,128]{2,1,0:T(8,128)S(1)} collective-permute-done((f32[4,128,128]{2,1,0:T(8,128)}, f32[4,128,128]{2,1,0:T(8,128)S(1)}, u32[]{:S(2)}, u32[]{:S(2)}) %collective-permute-start.10) | collective-permute-done | bytes 262176 | tf_op jit(solution)/shard_map/ppermute | solution.py:21
  109.8 7.6 %shard_map.63 = (f32[2,4,2,64,128]{4,3,2,1,0:T(8,128)}, f32[2,4,2,64,128]{4,3,2,1,0:T(8,128)}, f32[4,64,512]{2,1,0:T(8,128)}, f32[4,64,512]{2,1,0:T(8,128)}) custom-call(s32[3]{0:T(128)} %pad_add_fusion.s_ref, f32[64,128,128]{2,1,0:T(8,128)} %bitcast.112, f32[4,128,128]{2,1,0:T(8,128)} %copy-done.10, f32[4,128,128]{2,1,0:T(8,128)} %copy-done.12, ...), custom_call_target="tpu_custom_call" | custom-call | flops 1409286144 | bytes 4194304 | tf_op jit(solution)/shard_map/pallas_call | solution.py:176
  133.3 41.6 %collective-permute-done.28 = f32[4,32,512]{2,1,0:T(8,128)S(1)} collective-permute-done((f32[4,32,512]{2,1,0:T(8,128)}, f32[4,32,512]{2,1,0:T(8,128)S(1)}, u32[]{:S(2)}, u32[]{:S(2)}) %collective-permute-start.28) | collective-permute-done | bytes 262176 | tf_op jit(solution)/shard_map/ppermute | solution.py:21
  177.6 2.9 %collective-permute-done.37 = f32[1,4,2,64,128]{4,3,2,1,0:T(8,128)S(1)} collective-permute-done((f32[1,4,2,64,128]{4,3,2,1,0:T(8,128)S(1)}, f32[1,4,2,64,128]{4,3,2,1,0:T(8,128)S(1)}, u32[]{:S(2)}, u32[]{:S(2)}) %collective-permute-start.37) | collective-permute-done | bytes 262176 | tf_op jit(solution)/shard_map/ppermute | solution.py:21
  185.0 5.7 %collective-permute-start.38 = (f32[2,64,128]{2,1,0:T(8,128)}, f32[2,64,128]{2,1,0:T(8,128)S(1)}, u32[]{:S(2)}, u32[]{:S(2)}) collective-permute-start(f32[2,64,128]{2,1,0:T(8,128)} %get-tuple-element.104), channel_id=1, source_target_pairs={{0,2},{2,0},{4,6},{6,4},{1,3},{3,1},{5,7},{7,5},{8,10},{10,8},{12,... | collective-permute-start | bytes 196616 | tf_op jit(solution)/shard_map/ppermute | solution.py:21
  190.7 9.9 %shard_map.58 = (f32[2,128,512]{2,1,0:T(8,128)}, f32[2,128,512]{2,1,0:T(8,128)}) custom-call(s32[3]{0:T(128)} %pad_add_fusion.s_ref, f32[64,128,128]{2,1,0:T(8,128)} %bitcast.113, f32[16,128,128]{2,1,0:T(8,128)} %collective-permute-done.refs_1_, f32[16,128,128]{2,1,0:T(8,128)} %collective-permute-done.1.refs_2_, f32[16,128,128]{2,1,0:T(8,128)} %collective-permute-done.2.refs_3_), custom_call_target="tpu_custom_call" | custom-call | flops 3221225472 | bytes 8388608 | tf_op jit(solution)/shard_map/pallas_call | solution.py:230
  200.6 2.1 collective-permute-start.39
  208.0 2.5 collective-permute-start.44
  213.6 2.6 collective-permute-start.49
  222.1 2.6 %collective-permute-start.50 = (f32[2,64,128]{2,1,0:T(8,128)S(1)}, f32[2,64,128]{2,1,0:T(8,128)S(1)}, u32[]{:S(2)}, u32[]{:S(2)}) collective-permute-start(f32[2,64,128]{2,1,0:T(8,128)S(1)} %get-tuple-element.94), channel_id=1, source_target_pairs={{0,6},{2,4},{4,2},{6,0},{1,7},{3,5},{5,3},{7,1},{8,14},{10,12},{12... | collective-permute-start | bytes 196616 | tf_op jit(solution)/shard_map/ppermute | solution.py:21
  224.7 1.8 collective-permute-start.54
  226.5 2.6 %collective-permute-start.55 = (f32[2,64,128]{2,1,0:T(8,128)S(1)}, f32[2,64,128]{2,1,0:T(8,128)S(1)}, u32[]{:S(2)}, u32[]{:S(2)}) collective-permute-start(f32[2,64,128]{2,1,0:T(8,128)S(1)} %get-tuple-element.90), channel_id=1, source_target_pairs={{0,6},{2,4},{4,2},{6,0},{1,7},{3,5},{5,3},{7,1},{8,14},{10,12},{12... | collective-permute-start | bytes 196616 | tf_op jit(solution)/shard_map/ppermute | solution.py:21
  230.5 2.1 collective-permute-done.55.refs_15_
  233.2 3.6 %shard_map.64 = f32[64,64,64]{2,1,0:T(8,128)} custom-call(s32[3]{0:T(128)} %pad_add_fusion.s_ref, f32[2,64,128]{2,1,0:T(8,128)} %get-tuple-element.105.refs_0_, f32[2,64,128]{2,1,0:T(8,128)} %copy-done.18, f32[2,64,128]{2,1,0:T(8,128)} %copy-done.19, f32[2,64,128]{2,1,0:T(8,128)} %copy-done.20, f32[2,64,128]{2,1,0:T(8,128)} %get-tuple-element.101.refs_4_, ...), custom_call_target="tpu_custom_call" | custom-call | flops 1000 | bytes 3145728 | tf_op jit(solution)/shard_map/pallas_call | solution.py:261
  239.0 2.1 collective-permute-done.34
  241.3 3.6 %collective-permute-done.4 = f32[1,128,512]{2,1,0:T(8,128)S(1)} collective-permute-done((f32[1,128,512]{2,1,0:T(8,128)S(1)}, f32[1,128,512]{2,1,0:T(8,128)S(1)}, u32[]{:S(2)}, u32[]{:S(2)}) %collective-permute-start.4) | collective-permute-done | bytes 262176 | tf_op jit(solution)/shard_map/ppermute | solution.py:21
  245.6 4.4 %collective-permute-done.5 = f32[4,16,512]{2,1,0:T(8,128)S(1)} collective-permute-done((f32[4,16,512]{2,1,0:T(8,128)S(1)}, f32[4,16,512]{2,1,0:T(8,128)S(1)}, u32[]{:S(2)}, u32[]{:S(2)}) %collective-permute-start.5) | collective-permute-done | bytes 131104 | tf_op jit(solution)/shard_map/ppermute | solution.py:21
  250.0 2.7 %collective-permute-start.8 = (f32[16,512]{1,0:T(8,128)S(1)}, f32[16,512]{1,0:T(8,128)S(1)}, u32[]{:S(2)}, u32[]{:S(2)}) collective-permute-start(f32[16,512]{1,0:T(8,128)S(1)} %get-tuple-element.114), channel_id=1, source_target_pairs={{0,6},{2,4},{4,2},{6,0},{1,7},{3,5},{5,3},{7,1},{8,14},{10,12},{12... | collective-permute-start | bytes 98312 | tf_op jit(solution)/shard_map/ppermute | solution.py:21
  (194 shorter events, 63.9 us)
Async XLA Ops:
  1.4 15.4 %collective-permute-start.14 = (f32[32,256]{1,0:T(8,128)S(1)}, f32[32,256]{1,0:T(8,128)S(1)}, u32[]{:S(2)}, u32[]{:S(2)}) collective-permute-start(f32[32,256]{1,0:T(8,128)S(1)} %dynamic-slice_bitcast_fusion.21), channel_id=1, source_target_pairs={{0,6},{2,4},{4,2},{6,0},{1,7},{3,5},{5,3},{7,1},{8,14},{10,12},{12... | collective-permute-start | bytes 98312 | tf_op jit(solution)/shard_map/ppermute | solution.py:21
  6.5 10.3 %collective-permute-start.13 = (f32[32,256]{1,0:T(8,128)S(1)}, f32[32,256]{1,0:T(8,128)S(1)}, u32[]{:S(2)}, u32[]{:S(2)}) collective-permute-start(f32[32,256]{1,0:T(8,128)S(1)} %dynamic-slice_bitcast_fusion.21), channel_id=1, source_target_pairs={{0,4},{2,6},{4,0},{6,2},{1,5},{3,7},{5,1},{7,3},{8,12},{10,14},{12... | collective-permute-start | bytes 98312 | tf_op jit(solution)/shard_map/ppermute | solution.py:21
  6.5 10.3 %collective-permute-start.12 = (f32[32,256]{1,0:T(8,128)S(1)}, f32[32,256]{1,0:T(8,128)S(1)}, u32[]{:S(2)}, u32[]{:S(2)}) collective-permute-start(f32[32,256]{1,0:T(8,128)S(1)} %dynamic-slice_bitcast_fusion.21), channel_id=1, source_target_pairs={{0,2},{2,0},{4,6},{6,4},{1,3},{3,1},{5,7},{7,5},{8,10},{10,8},{12,... | collective-permute-start | bytes 98312 | tf_op jit(solution)/shard_map/ppermute | solution.py:21
  14.8 13.7 %collective-permute-start.18 = (f32[4,128,128]{2,1,0:T(8,128)}, f32[4,128,128]{2,1,0:T(8,128)}, u32[]{:S(2)}, u32[]{:S(2)}) collective-permute-start(f32[4,128,128]{2,1,0:T(8,128)} %get-tuple-element.53), channel_id=1, source_target_pairs={{0,2},{2,0},{4,6},{6,4},{1,3},{3,1},{5,7},{7,5},{8,10},{10,8},{12,... | collective-permute-start | bytes 786440 | tf_op jit(solution)/shard_map/ppermute | solution.py:21
  16.2 20.4 %collective-permute-start.24 = (f32[4,128,128]{2,1,0:T(8,128)S(1)}, f32[4,128,128]{2,1,0:T(8,128)S(1)}, u32[]{:S(2)}, u32[]{:S(2)}) collective-permute-start(f32[4,128,128]{2,1,0:T(8,128)S(1)} %get-tuple-element.59), channel_id=1, source_target_pairs={{0,2},{2,0},{4,6},{6,4},{1,3},{3,1},{5,7},{7,5},{8,10},{10,8},{12,... | collective-permute-start | bytes 786440 | tf_op jit(solution)/shard_map/ppermute | solution.py:21
  20.1 8.4 %collective-permute-start.17 = (f32[3,32,256]{2,1,0:T(8,128)S(1)}, f32[3,32,256]{2,1,0:T(8,128)}, u32[]{:S(2)}, u32[]{:S(2)}) collective-permute-start(f32[3,32,256]{2,1,0:T(8,128)S(1)} %pad_maximum_fusion.2.refs_0_), channel_id=1, source_target_pairs={{0,24},{8,16},{16,8},{24,0},{1,25},{9,17},{17,9},{25,1},{2,26},{10... | collective-permute-start | bytes 294920 | tf_op jit(solution)/shard_map/ppermute | solution.py:21
  20.1 31.0 %collective-permute-start.25 = (f32[4,128,128]{2,1,0:T(8,128)S(1)}, f32[4,128,128]{2,1,0:T(8,128)}, u32[]{:S(2)}, u32[]{:S(2)}) collective-permute-start(f32[4,128,128]{2,1,0:T(8,128)S(1)} %get-tuple-element.60), channel_id=1, source_target_pairs={{0,4},{2,6},{4,0},{6,2},{1,5},{3,7},{5,1},{7,3},{8,12},{10,14},{12... | collective-permute-start | bytes 786440 | tf_op jit(solution)/shard_map/ppermute | solution.py:21
  24.6 26.6 %collective-permute-start.26 = (f32[4,128,128]{2,1,0:T(8,128)S(1)}, f32[4,128,128]{2,1,0:T(8,128)}, u32[]{:S(2)}, u32[]{:S(2)}) collective-permute-start(f32[4,128,128]{2,1,0:T(8,128)S(1)} %get-tuple-element.61), channel_id=1, source_target_pairs={{0,6},{2,4},{4,2},{6,0},{1,7},{3,5},{5,3},{7,1},{8,14},{10,12},{12... | collective-permute-start | bytes 786440 | tf_op jit(solution)/shard_map/ppermute | solution.py:21
  28.5 29.9 %collective-permute-start.21 = (f32[4,128,128]{2,1,0:T(8,128)S(1)}, f32[4,128,128]{2,1,0:T(8,128)}, u32[]{:S(2)}, u32[]{:S(2)}) collective-permute-start(f32[4,128,128]{2,1,0:T(8,128)S(1)} %get-tuple-element.56), channel_id=1, source_target_pairs={{0,2},{2,0},{4,6},{6,4},{1,3},{3,1},{5,7},{7,5},{8,10},{10,8},{12,... | collective-permute-start | bytes 786440 | tf_op jit(solution)/shard_map/ppermute | solution.py:21
  28.5 51.9 %collective-permute-start.22 = (f32[4,128,128]{2,1,0:T(8,128)S(1)}, f32[4,128,128]{2,1,0:T(8,128)}, u32[]{:S(2)}, u32[]{:S(2)}) collective-permute-start(f32[4,128,128]{2,1,0:T(8,128)S(1)} %get-tuple-element.57), channel_id=1, source_target_pairs={{0,4},{2,6},{4,0},{6,2},{1,5},{3,7},{5,1},{7,3},{8,12},{10,14},{12... | collective-permute-start | bytes 786440 | tf_op jit(solution)/shard_map/ppermute | solution.py:21
  36.6 43.8 %collective-permute-start.23 = (f32[4,128,128]{2,1,0:T(8,128)S(1)}, f32[4,128,128]{2,1,0:T(8,128)}, u32[]{:S(2)}, u32[]{:S(2)}) collective-permute-start(f32[4,128,128]{2,1,0:T(8,128)S(1)} %get-tuple-element.58), channel_id=1, source_target_pairs={{0,6},{2,4},{4,2},{6,0},{1,7},{3,5},{5,3},{7,1},{8,14},{10,12},{12... | collective-permute-start | bytes 786440 | tf_op jit(solution)/shard_map/ppermute | solution.py:21
  51.2 39.2 %collective-permute-start.19 = (f32[4,128,128]{2,1,0:T(8,128)S(1)}, f32[4,128,128]{2,1,0:T(8,128)S(1)}, u32[]{:S(2)}, u32[]{:S(2)}) collective-permute-start(f32[4,128,128]{2,1,0:T(8,128)S(1)} %get-tuple-element.54), channel_id=1, source_target_pairs={{0,4},{2,6},{4,0},{6,2},{1,5},{3,7},{5,1},{7,3},{8,12},{10,14},{12... | collective-permute-start | bytes 786440 | tf_op jit(solution)/shard_map/ppermute | solution.py:21
  51.2 39.2 %collective-permute-start.20 = (f32[4,128,128]{2,1,0:T(8,128)S(1)}, f32[4,128,128]{2,1,0:T(8,128)S(1)}, u32[]{:S(2)}, u32[]{:S(2)}) collective-permute-start(f32[4,128,128]{2,1,0:T(8,128)S(1)} %get-tuple-element.55), channel_id=1, source_target_pairs={{0,6},{2,4},{4,2},{6,0},{1,7},{3,5},{5,3},{7,1},{8,14},{10,12},{12... | collective-permute-start | bytes 786440 | tf_op jit(solution)/shard_map/ppermute | solution.py:21
  58.4 40.3 %collective-permute-start.9 = (f32[4,128,128]{2,1,0:T(8,128)}, f32[4,128,128]{2,1,0:T(8,128)S(1)}, u32[]{:S(2)}, u32[]{:S(2)}) collective-permute-start(f32[4,128,128]{2,1,0:T(8,128)} %get-tuple-element.48), channel_id=1, source_target_pairs={{0,2},{2,0},{4,6},{6,4},{1,3},{3,1},{5,7},{7,5},{8,10},{10,8},{12,... | collective-permute-start | bytes 786440 | tf_op jit(solution)/shard_map/ppermute | solution.py:21
  80.4 28.6 %collective-permute-start.10 = (f32[4,128,128]{2,1,0:T(8,128)}, f32[4,128,128]{2,1,0:T(8,128)S(1)}, u32[]{:S(2)}, u32[]{:S(2)}) collective-permute-start(f32[4,128,128]{2,1,0:T(8,128)} %get-tuple-element.49), channel_id=1, source_target_pairs={{0,4},{2,6},{4,0},{6,2},{1,5},{3,7},{5,1},{7,3},{8,12},{10,14},{12... | collective-permute-start | bytes 786440 | tf_op jit(solution)/shard_map/ppermute | solution.py:21
  80.4 28.6 %collective-permute-start.11 = (f32[4,128,128]{2,1,0:T(8,128)S(1)}, f32[4,128,128]{2,1,0:T(8,128)S(1)}, u32[]{:S(2)}, u32[]{:S(2)}) collective-permute-start(f32[4,128,128]{2,1,0:T(8,128)S(1)} %get-tuple-element.50), channel_id=1, source_target_pairs={{0,6},{2,4},{4,2},{6,0},{1,7},{3,5},{5,3},{7,1},{8,14},{10,12},{12... | collective-permute-start | bytes 786440 | tf_op jit(solution)/shard_map/ppermute | solution.py:21
  118.5 11.9 %collective-permute-start.51 = (f32[2,4,2,64,128]{4,3,2,1,0:T(8,128)}, f32[2,4,2,64,128]{4,3,2,1,0:T(8,128)}, u32[]{:S(2)}, u32[]{:S(2)}) collective-permute-start(f32[2,4,2,64,128]{4,3,2,1,0:T(8,128)} %get-tuple-element.74), channel_id=1, source_target_pairs={{0,8},{8,0},{16,24},{24,16},{1,9},{9,1},{17,25},{25,17},{2,10},{10... | collective-permute-start | bytes 1572872 | tf_op jit(solution)/shard_map/ppermute | solution.py:21
  119.8 63.1 %collective-permute-start = (f32[16,128,128]{2,1,0:T(8,128)}, f32[16,128,128]{2,1,0:T(8,128)}, u32[]{:S(2)}, u32[]{:S(2)}) collective-permute-start(f32[16,128,128]{2,1,0:T(8,128)} %get-tuple-element.40), channel_id=1, source_target_pairs={{0,8},{8,0},{16,24},{24,16},{1,9},{9,1},{17,25},{25,17},{2,10},{10... | collective-permute-start | bytes 3145736 | tf_op jit(solution)/shard_map/ppermute | solution.py:21
  120.5 62.7 %collective-permute-start.1 = (f32[16,128,128]{2,1,0:T(8,128)}, f32[16,128,128]{2,1,0:T(8,128)}, u32[]{:S(2)}, u32[]{:S(2)}) collective-permute-start(f32[16,128,128]{2,1,0:T(8,128)} %get-tuple-element.41), channel_id=1, source_target_pairs={{0,16},{8,24},{16,0},{24,8},{1,17},{9,25},{17,1},{25,9},{2,18},{10... | collective-permute-start | bytes 3145736 | tf_op jit(solution)/shard_map/ppermute | solution.py:21
  122.2 62.7 %collective-permute-start.2 = (f32[16,128,128]{2,1,0:T(8,128)S(1)}, f32[16,128,128]{2,1,0:T(8,128)}, u32[]{:S(2)}, u32[]{:S(2)}) collective-permute-start(f32[16,128,128]{2,1,0:T(8,128)S(1)} %get-tuple-element.42), channel_id=1, source_target_pairs={{0,24},{8,16},{16,8},{24,0},{1,25},{9,17},{17,9},{25,1},{2,26},{10... | collective-permute-start | bytes 3145736 | tf_op jit(solution)/shard_map/ppermute | solution.py:21
  124.5 50.4 %collective-permute-start.28 = (f32[4,32,512]{2,1,0:T(8,128)}, f32[4,32,512]{2,1,0:T(8,128)S(1)}, u32[]{:S(2)}, u32[]{:S(2)}) collective-permute-start(f32[4,32,512]{2,1,0:T(8,128)} %add_bitcast_fusion), channel_id=1, source_target_pairs={{0,16},{8,24},{16,0},{24,8},{1,17},{9,25},{17,1},{25,9},{2,18},{10... | collective-permute-start | bytes 786440 | tf_op jit(solution)/shard_map/ppermute | solution.py:21
  130.4 50.1 %collective-permute-start.37 = (f32[1,4,2,64,128]{4,3,2,1,0:T(8,128)S(1)}, f32[1,4,2,64,128]{4,3,2,1,0:T(8,128)S(1)}, u32[]{:S(2)}, u32[]{:S(2)}) collective-permute-start(f32[1,4,2,64,128]{4,3,2,1,0:T(8,128)S(1)} %slice.41), channel_id=1, source_target_pairs={{0,16},{8,24},{16,0},{24,8},{1,17},{9,25},{17,1},{25,9},{2,18},{10... | collective-permute-start | bytes 786440 | tf_op jit(solution)/shard_map/ppermute | solution.py:21
  174.8 25.8 %collective-permute-start.42 = (f32[1,4,2,64,128]{4,3,2,1,0:T(8,128)}, f32[1,4,2,64,128]{4,3,2,1,0:T(8,128)}, u32[]{:S(2)}, u32[]{:S(2)}) collective-permute-start(f32[1,4,2,64,128]{4,3,2,1,0:T(8,128)} %slice.43), channel_id=1, source_target_pairs={{0,16},{8,24},{16,0},{24,8},{1,17},{9,25},{17,1},{25,9},{2,18},{10... | collective-permute-start | bytes 786440 | tf_op jit(solution)/shard_map/ppermute | solution.py:21
  180.4 23.9 %collective-permute-start.47 = (f32[1,4,2,64,128]{4,3,2,1,0:T(8,128)}, f32[1,4,2,64,128]{4,3,2,1,0:T(8,128)S(1)}, u32[]{:S(2)}, u32[]{:S(2)}) collective-permute-start(f32[1,4,2,64,128]{4,3,2,1,0:T(8,128)} %slice.45), channel_id=1, source_target_pairs={{0,16},{8,24},{16,0},{24,8},{1,17},{9,25},{17,1},{25,9},{2,18},{10... | collective-permute-start | bytes 786440 | tf_op jit(solution)/shard_map/ppermute | solution.py:21
  182.9 22.9 %collective-permute-start.52 = (f32[1,4,2,64,128]{4,3,2,1,0:T(8,128)}, f32[1,4,2,64,128]{4,3,2,1,0:T(8,128)}, u32[]{:S(2)}, u32[]{:S(2)}) collective-permute-start(f32[1,4,2,64,128]{4,3,2,1,0:T(8,128)} %slice.47), channel_id=1, source_target_pairs={{0,16},{8,24},{16,0},{24,8},{1,17},{9,25},{17,1},{25,9},{2,18},{10... | collective-permute-start | bytes 786440 | tf_op jit(solution)/shard_map/ppermute | solution.py:21
  183.2 24.8 %collective-permute-start.29 = (f32[4,16,512]{2,1,0:T(8,128)S(1)}, f32[4,16,512]{2,1,0:T(8,128)}, u32[]{:S(2)}, u32[]{:S(2)}) collective-permute-start(f32[4,16,512]{2,1,0:T(8,128)S(1)} %dynamic-slice_bitcast_fusion), channel_id=1, source_target_pairs={{0,1},{1,0},{2,3},{3,2},{4,5},{5,4},{6,7},{7,6},{8,9},{9,8},{10,11... | collective-permute-start | bytes 393224 | tf_op jit(solution)/shard_map/ppermute | solution.py:21
  185.0 26.5 %collective-permute-start.38 = (f32[2,64,128]{2,1,0:T(8,128)}, f32[2,64,128]{2,1,0:T(8,128)S(1)}, u32[]{:S(2)}, u32[]{:S(2)}) collective-permute-start(f32[2,64,128]{2,1,0:T(8,128)} %get-tuple-element.104), channel_id=1, source_target_pairs={{0,2},{2,0},{4,6},{6,4},{1,3},{3,1},{5,7},{7,5},{8,10},{10,8},{12,... | collective-permute-start | bytes 196616 | tf_op jit(solution)/shard_map/ppermute | solution.py:21
  200.6 12.3 %collective-permute-start.39 = (f32[2,64,128]{2,1,0:T(8,128)S(1)}, f32[2,64,128]{2,1,0:T(8,128)S(1)}, u32[]{:S(2)}, u32[]{:S(2)}) collective-permute-start(f32[2,64,128]{2,1,0:T(8,128)S(1)} %copy-done.17), channel_id=1, source_target_pairs={{0,4},{2,6},{4,0},{6,2},{1,5},{3,7},{5,1},{7,3},{8,12},{10,14},{12... | collective-permute-start | bytes 196616 | tf_op jit(solution)/shard_map/ppermute | solution.py:21
  204.4 8.6 %collective-permute-start.40 = (f32[2,64,128]{2,1,0:T(8,128)S(1)}, f32[2,64,128]{2,1,0:T(8,128)S(1)}, u32[]{:S(2)}, u32[]{:S(2)}) collective-permute-start(f32[2,64,128]{2,1,0:T(8,128)S(1)} %copy-done.16), channel_id=1, source_target_pairs={{0,6},{2,4},{4,2},{6,0},{1,7},{3,5},{5,3},{7,1},{8,14},{10,12},{12... | collective-permute-start | bytes 196616 | tf_op jit(solution)/shard_map/ppermute | solution.py:21
  213.5 24.8 %collective-permute-start.3 = (f32[2,128,512]{2,1,0:T(8,128)}, f32[2,128,512]{2,1,0:T(8,128)S(1)}, u32[]{:S(2)}, u32[]{:S(2)}) collective-permute-start(f32[2,128,512]{2,1,0:T(8,128)} %get-tuple-element.44), channel_id=1, source_target_pairs={{0,8},{8,0},{16,24},{24,16},{1,9},{9,1},{17,25},{25,17},{2,10},{10... | collective-permute-start | bytes 1572872 | tf_op jit(solution)/shard_map/ppermute | solution.py:21
  213.6 8.6 %collective-permute-start.49 = (f32[2,64,128]{2,1,0:T(8,128)S(1)}, f32[2,64,128]{2,1,0:T(8,128)S(1)}, u32[]{:S(2)}, u32[]{:S(2)}) collective-permute-start(f32[2,64,128]{2,1,0:T(8,128)S(1)} %get-tuple-element.95), channel_id=1, source_target_pairs={{0,4},{2,6},{4,0},{6,2},{1,5},{3,7},{5,1},{7,3},{8,12},{10,14},{12... | collective-permute-start | bytes 196616 | tf_op jit(solution)/shard_map/ppermute | solution.py:21
  216.1 8.6 %collective-permute-start.32 = (f32[16,512]{1,0:T(8,128)S(1)}, f32[16,512]{1,0:T(8,128)S(1)}, u32[]{:S(2)}, u32[]{:S(2)}) collective-permute-start(f32[16,512]{1,0:T(8,128)S(1)} %get-tuple-element.111), channel_id=1, source_target_pairs={{0,6},{2,4},{4,2},{6,0},{1,7},{3,5},{5,3},{7,1},{8,14},{10,12},{12... | collective-permute-start | bytes 98312 | tf_op jit(solution)/shard_map/ppermute | solution.py:21
  (56 other events, 489.9 us)

commit v2 on v1

--- a/solution.py
+++ b/solution.py
@@ -8,7 +8,6 @@
 from jax.sharding import PartitionSpec as P
 
 
-CHUNKS = 4
 F32 = jnp.float32
 BF16 = jnp.bfloat16
 ROWS = (((0,), (0,)), ((), ()))
@@ -21,10 +20,6 @@
     return lax.ppermute(value, axis, [(i, i ^ offset) for i in range(size)])
 
 
-def far_first(size):
-    return [k for k in range(1, size) if k >= size // 2] + [k for k in range(1, size // 2)]
-
-
 def pick(value, index, axis):
     return lax.dynamic_index_in_dim(value, index, axis, keepdims=False)
 
@@ -35,12 +30,88 @@
 
 
 def dot3(left, right, dims):
-    dot = functools.partial(lax.dot_general, dimension_numbers=dims, preferred_element_type=F32)
-    return dot(left[0], right[0]) + (dot(left[0], right[1]) + dot(left[1], right[0]))
+    (lc,), (rc,) = dims[0]
+    lhs = jnp.concatenate([left[0], left[0], left[1]], axis=lc)
+    rhs = jnp.concatenate([right[0], right[1], right[0]], axis=rc)
+    return lax.dot_general(lhs, rhs, dims, preferred_element_type=F32)
+
+
+def params():
+    return pltpu.CompilerParams(vmem_limit_bytes=24 << 20)
+
+
+def chunk_sizes(own):
+    edge = max(2, own // 8)
+    middle = (own - 2 * edge) // 2
+    sizes = (edge, middle, own - 2 * edge - middle, edge)
+    assert all(n > 0 and n % 2 == 0 for n in sizes)
+    return sizes
 
 
 def whole_spec(shape):
     return pl.BlockSpec(shape, lambda i, s: (0,) * len(shape))
+
+
+def cut_kernel(s_ref, *refs):
+    half = len(refs) // 2
+    for source, target in zip(refs[:half], refs[half:]):
+        target[...] = source[...]
+
+
+def cut(where, flat, pieces):
+    block = (2,) + flat.shape[1:]
+    steps = max(size for *_, size in pieces) // 2
+    in_specs, out_specs, out_shape = [], [], []
+    for axis, k, own, start, size in pieces:
+
+        def source(i, s, axis=axis, k=k, own=own, start=start, size=size):
+            return (((s[axis] ^ k) * own + start) // 2 + jnp.minimum(i, size // 2 - 1), 0, 0)
+
+        def target(i, s, size=size):
+            return (jnp.minimum(i, size // 2 - 1), 0, 0)
+
+        in_specs.append(pl.BlockSpec(block, source))
+        out_specs.append(pl.BlockSpec(block, target))
+        out_shape.append(jax.ShapeDtypeStruct((size,) + flat.shape[1:], F32))
+    return pl.pallas_call(
+        cut_kernel,
+        grid_spec=pltpu.PrefetchScalarGridSpec(
+            num_scalar_prefetch=1, grid=(steps,), in_specs=in_specs, out_specs=out_specs
+        ),
+        out_shape=out_shape,
+        compiler_params=params(),
+        cost_estimate=pl.CostEstimate(flops=1000, bytes_accessed=1 << 22, transcendentals=0),
+    )(where, *[flat] * len(pieces))
+
+
+def reverse_bits(value, count):
+    bits = count.bit_length() - 1
+    return sum(((value >> i) & 1) << (bits - 1 - i) for i in range(bits))
+
+
+def rows_kernel(terms, s_ref, *refs):
+    parts, out_ref = refs[:-1], refs[-1]
+    size = parts[0].shape[0]
+    for o, part in enumerate(parts):
+        place = reverse_bits(s_ref[0] ^ o, len(parts))
+        out_ref[pl.ds(pl.multiple_of(place * size, size), size), :] = part[...] / terms
+
+
+def place_rows(where, parts, terms):
+    size, width = parts[0].shape
+    shape = (len(parts) * size, width)
+    return pl.pallas_call(
+        functools.partial(rows_kernel, terms),
+        grid_spec=pltpu.PrefetchScalarGridSpec(
+            num_scalar_prefetch=1,
+            grid=(1,),
+            in_specs=[whole_spec((size, width))] * len(parts),
+            out_specs=whole_spec(shape),
+        ),
+        out_shape=jax.ShapeDtypeStruct(shape, F32),
+        compiler_params=params(),
+        cost_estimate=pl.CostEstimate(flops=1000, bytes_accessed=1 << 19, transcendentals=0),
+    )(where, *parts)
 
 
 def fy_kernel(ny, nx, s_ref, own_ref, *refs):
@@ -69,6 +140,7 @@
             scratch_shapes=[pltpu.VMEM(shape, F32)],
         ),
         out_shape=[jax.ShapeDtypeStruct(shape, BF16)] * 2,
+        compiler_params=params(),
         cost_estimate=pl.CostEstimate(flops=1000, bytes_accessed=1 << 20, transcendentals=0),
     )(where, factor_y, *pieces)
 
@@ -84,30 +156,23 @@
         gkeep_ref, gsent_ref, wide_ref, gram_ref = refs
     else:
         gram_ref, wide_ref = refs
-    step = pl.program_id(0)
-    pair, x_local, y_local = fields[0].shape
+    n, x_local, y_local = fields[0].shape
     me_x, me_y = s_ref[0], s_ref[1]
     for k in range(ny):
         start = pl.multiple_of((me_y ^ k) * y_local, y_local)
-        wide_ref[:, pl.ds(start, y_local)] = fields[k][...].reshape(pair * x_local, y_local)
+        wide_ref[:, pl.ds(start, y_local)] = fields[k][...].reshape(n * x_local, y_local)
     wide = split(wide_ref[...])
     gram = dot3(wide, wide, ROWS)
-
-    @pl.when(step == 0)
-    def _():
-        gram_ref[...] = gram if first else gin_ref[...] + gram
-
-    @pl.when(step > 0)
-    def _():
-        gram_ref[...] += gram
+    gram_ref[...] = gram if first else gin_ref[...] + gram
 
     half = dot3(wide, (fyh_ref[...], fyl_ref[...]), PLAIN)
     b_block = half.shape[1] // ny
     paired = jnp.concatenate(
         [
             half[p * x_local : (p + 1) * x_local, q * b_block : (q + 1) * b_block]
+            for j in range(n // 2)
             for q in range(ny)
-            for p in range(pair)
+            for p in (2 * j, 2 * j + 1)
         ],
         axis=1,
     )
@@ -120,50 +185,42 @@
         axis=0,
     )
     full = dot3(split(fx), split(paired), PLAIN)
-    lanes = pair * b_block
+    lanes = 2 * b_block
     for o in range(nx):
         target = sent_ref if o % 2 else keep_ref
-        for q in range(ny):
-            target[o // 2, q, 0] = full[
-                o * a_block : (o + 1) * a_block, q * lanes : (q + 1) * lanes
-            ]
+        for j in range(n // 2):
+            for q in range(ny):
+                at = (j * ny + q) * lanes
+                target[o // 2, q, j] = full[o * a_block : (o + 1) * a_block, at : at + lanes]
     if last:
-
-        @pl.when(step == pl.num_programs(0) - 1)
-        def _():
-            part = y_local // 2
-            bit = me_x & 1
-            for k in range(ny):
-                mine = pl.multiple_of(k * y_local + bit * part, part)
-                other = pl.multiple_of(k * y_local + (1 - bit) * part, part)
-                gkeep_ref[k] = gram_ref[pl.ds(mine, part), :]
-                gsent_ref[k] = gram_ref[pl.ds(other, part), :]
-
-
-def chunk_terms(sizes, where, flat, offset, parts, fy, fxt, gram, last):
+        part = y_local // 2
+        bit = me_x & 1
+        for k in range(ny):
+            mine = pl.multiple_of(k * y_local + bit * part, part)
+            other = pl.multiple_of(k * y_local + (1 - bit) * part, part)
+            gkeep_ref[k] = gram_ref[pl.ds(mine, part), :]
+            gsent_ref[k] = gram_ref[pl.ds(other, part), :]
+
+
+def chunk_terms(sizes, where, parts, fy, fxt, gram, last):
     nx, ny, _ = sizes
     n, x_local, y_local = parts[0].shape
-    own = flat.shape[0] // ny
     rank = fxt.shape[0]
     pairs = n // 2
     width = ny * y_local
     a_block, b_block = rank // nx, rank // ny
     half = (nx // 2, ny, pairs, a_block, 2 * b_block)
-    field = (2, x_local, y_local)
-    specs = [pl.BlockSpec(field, lambda i, s: ((s[1] * own + offset) // 2 + i, 0, 0))]
-    specs += [pl.BlockSpec(field, lambda i, s: (i, 0, 0))] * (ny - 1)
+    field = (n, x_local, y_local)
+    specs = [whole_spec(field)] * ny
     specs += [whole_spec(fy[0].shape)] * 2 + [whole_spec(fxt.shape)]
-    args = [flat, *parts, *fy, fxt]
+    args = [*parts, *fy, fxt]
     first = gram is None
     if not first:
         specs.append(whole_spec((width, width)))
         args.append(gram)
-    half_spec = pl.BlockSpec(
-        (nx // 2, ny, 1, a_block, 2 * b_block), lambda i, s: (0, 0, i, 0, 0)
-    )
-    out_specs = [half_spec] * 2
+    out_specs = [whole_spec(half)] * 2
     out_shape = [jax.ShapeDtypeStruct(half, F32)] * 2
-    scratch = [pltpu.VMEM((2 * x_local, width), F32)]
+    scratch = [pltpu.VMEM((n * x_local, width), F32)]
     if last:
         gshape = (ny, y_local // 2, width)
         out_specs += [whole_spec(gshape)] * 2
@@ -177,12 +234,13 @@
         functools.partial(chunk_kernel, sizes, first, last),
         grid_spec=pltpu.PrefetchScalarGridSpec(
             num_scalar_prefetch=1,
-            grid=(pairs,),
+            grid=(1,),
             in_specs=specs,
             out_specs=out_specs,
             scratch_shapes=scratch,
         ),
         out_shape=out_shape,
+        compiler_params=params(),
         cost_estimate=pl.CostEstimate(flops=flops, bytes_accessed=1 << 22, transcendentals=0),
     )(where, *args)
 
@@ -222,8 +280,9 @@
     nx = sizes[0]
     own, x_local, y_local = parts[0].shape
     width = nx * x_local
-    field = (2, x_local, y_local)
-    specs = [pl.BlockSpec(field, lambda i, s: (s[0] * own // 2 + i, 0, 0))]
+    batch = 4
+    field = (batch, x_local, y_local)
+    specs = [pl.BlockSpec(field, lambda i, s: (s[0] * own // batch + i, 0, 0))]
     specs += [pl.BlockSpec(field, lambda i, s: (i, 0, 0))] * (nx - 1)
     half = (nx // 2, x_local, width)
     flops = 2 * own * y_local * width * width * 3
@@ -231,35 +290,35 @@
         functools.partial(gram_x_kernel, sizes),
         grid_spec=pltpu.PrefetchScalarGridSpec(
             num_scalar_prefetch=1,
-            grid=(own // 2,),
+            grid=(own // batch,),
             in_specs=specs,
             out_specs=[whole_spec(half)] * 2,
-            scratch_shapes=[pltpu.VMEM((width, 2 * y_local), F32), pltpu.VMEM((width, width), F32)],
+            scratch_shapes=[pltpu.VMEM((width, batch * y_local), F32), pltpu.VMEM((width, width), F32)],
         ),
         out_shape=[jax.ShapeDtypeStruct(half, F32)] * 2,
+        compiler_params=params(),
         cost_estimate=pl.CostEstimate(flops=flops, bytes_accessed=1 << 23, transcendentals=0),
     )(where, flat, *parts)
 
 
-def unpack_kernel(ny, n, own, s_ref, *refs):
+def unpack_kernel(ny, own, starts, s_ref, *refs):
     parts, out_ref = refs[:-1], refs[-1]
-    chunks = len(parts) // ny
     b_block = out_ref.shape[2]
-    for k in range(ny):
-        for c in range(chunks):
+    for c, start in enumerate(starts):
+        for k in range(ny):
             part = parts[c * ny + k]
-            for j in range(n // 2):
-                base = (s_ref[1] ^ k) * own + c * n + 2 * j
+            for j in range(part.shape[0]):
+                base = (s_ref[1] ^ k) * own + start + 2 * j
                 out_ref[base] = part[j, :, :b_block]
                 out_ref[base + 1] = part[j, :, b_block:]
 
 
-def unpack(sizes, where, parts, rows):
+def unpack(sizes, where, parts, starts, rows):
     ny = sizes[1]
-    half, a_block, lanes = parts[0].shape
+    _, a_block, lanes = parts[0].shape
     shape = (rows, a_block, lanes // 2)
     return pl.pallas_call(
-        functools.partial(unpack_kernel, ny, 2 * half, rows // ny),
+        functools.partial(unpack_kernel, ny, rows // ny, starts),
         grid_spec=pltpu.PrefetchScalarGridSpec(
             num_scalar_prefetch=1,
             grid=(1,),
@@ -267,6 +326,7 @@
             out_specs=whole_spec(shape),
         ),
         out_shape=jax.ShapeDtypeStruct(shape, F32),
+        compiler_params=params(),
         cost_estimate=pl.CostEstimate(flops=1000, bytes_accessed=3 << 20, transcendentals=0),
     )(where, *parts)
 
@@ -281,37 +341,33 @@
     rows = z_cells * s_local
     flat = slab.reshape((rows, x_local, y_local))
     own_y, own_x = rows // ny, rows // nx
-    n = own_y // CHUNKS
+    counts = chunk_sizes(own_y)
+    starts = [sum(counts[:c]) for c in range(len(counts))]
     x_total, y_total, s_total = x_local * nx, y_local * ny, s_local * ns
 
-    source = flat
+    keys = [[(1, k, own_y, starts[c], counts[c]) for k in range(ny)] for c in range(len(counts))]
+    x_keys = [(0, k, own_x, 0, own_x) for k in range(1, nx)]
+    groups = [keys[0][1:], x_keys, [keys[0][0]] + sum(keys[1:], [])]
+    pieces = {}
+    for group in groups:
+        pieces.update(zip(group, cut(where, flat, group)))
     along_y = []
-    for c in range(CHUNKS):
-        cut = {
-            k: lax.dynamic_slice_in_dim(source, (me_y ^ k) * own_y + c * n, n, 0)
-            for k in far_first(ny)
-        }
-        source, cut = lax.optimization_barrier((source, cut))
-        along_y.append({k: swap(cut[k], "gy", k) for k in far_first(ny)})
-        if c == 0:
-            mine = pick(factor_y.reshape((nx, y_local // nx, rank)), me_x, 0)
-            crossed = jnp.stack([swap(mine, "gy", k) for k in range(1, ny)])
-            pieces = [crossed] + [swap(crossed, "gx", o) for o in range(1, nx)]
-            cut = {
-                k: lax.dynamic_slice_in_dim(source, (me_x ^ k) * own_x, own_x, 0)
-                for k in far_first(nx)
-            }
-            source, cut = lax.optimization_barrier((source, cut))
-            along_x = {k: swap(cut[k], "gx", k) for k in far_first(nx)}
-    fy = gather_fy(sizes, where, factor_y, pieces)
+    for c in range(len(counts)):
+        here = [pieces[keys[c][0]]]
+        here += [swap(pieces[keys[c][k]], "gy", k) for k in range(1, ny)]
+        along_y.append(here)
+    along_x = [swap(pieces[x_keys[k - 1]], "gx", k) for k in range(1, nx)]
+    mine = pick(factor_y.reshape((nx, y_local // nx, rank)), me_x, 0)
+    crossed = jnp.stack([swap(mine, "gy", k) for k in range(1, ny)])
+    fy_parts = [crossed] + [swap(crossed, "gx", o) for o in range(1, nx)]
+    fy = gather_fy(sizes, where, factor_y, fy_parts)
     fxt = factor_x.T
 
     gram = None
     core_parts = []
-    for c in range(CHUNKS):
-        parts = [along_y[c][k] for k in range(1, ny)]
-        last = c == CHUNKS - 1
-        out = chunk_terms(sizes, where, flat, c * n, parts, fy, fxt, gram, last)
+    for c in range(len(counts)):
+        last = c == len(counts) - 1
+        out = chunk_terms(sizes, where, along_y[c], fy, fxt, gram, last)
         keep, sent, gram = out[0], out[1], out[2:]
         if last:
             gkeep, gsent = gram
@@ -329,10 +385,10 @@
         keep = keep[0]
         z_parts = [pick(keep, me_y ^ k, 0) for k in range(ny)]
         core_parts += [swap(z_parts[k], "gy", k) if k else z_parts[0] for k in range(ny)]
-    core = unpack(sizes, where, core_parts, rows)
+    core = unpack(sizes, where, core_parts, starts, rows)
     core = core.reshape((z_cells, s_local, a_block, b_block))
 
-    keep, sent = gram_x_terms(sizes, where, flat, [along_x[k] for k in range(1, nx)])
+    keep, sent = gram_x_terms(sizes, where, flat, along_x)
     got = swap(sent, "gx", 1)
     bit = 2
     while bit < nx:
@@ -362,23 +418,16 @@
         keep = pick(keep, mybit, 1) + pick(got, mybit, 1)
         got = swap(sent, "gx", bit)
         bit *= 2
-    total = (keep + got).reshape((ny, ns, -1, y_total))
-    keep = pick(total, me_s, 1)
+    total = keep + got
+    row = pick(total, me_y, 0)
+    for k in range(1, ny):
+        row = row + swap(pick(total, me_y ^ k, 0), "gy", k)
+    summed = row
     for k in range(1, ns):
-        keep = keep + swap(pick(total, me_s ^ k, 1), "sa", k)
-    row = pick(keep, me_y, 0)
-    for k in range(1, ny):
-        row = row + swap(pick(keep, me_y ^ k, 0), "gy", k)
-    row = row / (x_total * z_cells * s_total)
-    both = jnp.stack([row] + [swap(row, "sa", k) for k in range(1, ns)])
-    cur = jnp.concatenate([pick(both, me_s ^ k, 0) for k in range(ns)], axis=0)
-    bit = nx // 2
-    while bit:
-        got = swap(cur, "gx", bit)
-        high = (me_x // bit) % 2 == 1
-        cur = jnp.concatenate([jnp.where(high, got, cur), jnp.where(high, cur, got)], axis=0)
-        bit //= 2
-    return (gram_x, cur, core)
+        summed = summed + swap(row, "sa", k)
+    parts = [summed] + [swap(summed, "gx", o) for o in range(1, nx)]
+    gram_y = place_rows(where, parts, x_total * z_cells * s_total)
+    return (gram_x, gram_y, core)
 
 
 def solution(mesh):

time: 259 us -> 225 us (0.87)
  starting transfers between devices: 94.7 us -> 75.6 us
  waiting for transfers between devices: 82.2 us -> 97.3 us
  Pallas kernels: 45.9 us -> 33.1 us
  local copies, waits for them, and re-layouts: 21 us -> 12.8 us
  other arithmetic: 13.2 us -> 5.16 us
    ppermute x56, starting transfers between devices: 94.7 us -> 75.6 us  [swap(): return lax.ppermute(value, axis, [(i, i ^ offset) for i in range(size)])]
    ppermute x56, waiting for transfers between devices: 82.2 us -> 97.3 us  [swap(): return lax.ppermute(value, axis, [(i, i ^ offset) for i in range(size)])]
    pallas_call x4, Pallas kernels: 29.7 us -> 15.4 us  [chunk_terms(): pl.pallas_call(functools.partial(chunk_kernel, sizes, first, last), grid_...]
    dynamic_slice x5 -> x0, local copies, waits for them, and re-layouts: 9.62 us -> none  [the longest x4 6.13 us: local_step(): lax.dynamic_slice_in_dim(source, (me_y ^ k) * own_y + c * n, n, 0)]
    pallas_call x1 -> x5, Pallas kernels: 3.56 us -> 10.1 us  [the longest x3 6.64 us: cut(): pl.pallas_call(cut_kernel, grid_spec=pltpu.PrefetchScalarGridSpec(num_sca...]
    unnamed x65 -> x39, local copies, waits for them, and re-layouts: 5.71 us -> 11.8 us
    add x8, other arithmetic: 6.51 us -> 2.28 us  [local_step(): keep = keep + got]
    pallas_call x1, Pallas kernels: 9.89 us -> 6.89 us  [gram_x_terms(): pl.pallas_call(functools.partial(gram_x_kernel, sizes), grid_spec=pltpu.P...]
  transfers between devices with their start and end apart: 56 -> 56, of which waited for: 18 -> 17; matrix products, arithmetic and copies ran while one was open for 11% -> 2% of each run, Pallas kernels for 15% -> 15%
where the time goes in v2:
time: 225 us
  waiting for transfers between devices  97.3 us (43%)
  starting transfers between devices  75.6 us (34%)
  Pallas kernels  33.1 us (15%)
  local copies, waits for them, and re-layouts  12.8 us (6%)
  other arithmetic  5.16 us (2%)
    ppermute x56, waiting for transfers between devices, swap(): return lax.ppermute(value, axis, [(i, i ^ offset) for i in range(size)])  97.3 us
    ppermute x56, starting transfers between devices, swap(): return lax.ppermute(value, axis, [(i, i ^ offset) for i in range(size)])  75.6 us
    pallas_call x4, Pallas kernels, chunk_terms(): pl.pallas_call(functools.partial(chunk_kernel, sizes, first, last), grid_...  15.4 us
    unnamed x39, local copies, waits for them, and re-layouts  11.8 us
    pallas_call x1, Pallas kernels, gram_x_terms(): pl.pallas_call(functools.partial(gram_x_kernel, sizes), grid_spec=pltpu.P...  6.89 us
    pallas_call x3, Pallas kernels, cut(): pl.pallas_call(cut_kernel, grid_spec=pltpu.PrefetchScalarGridSpec(num_sca...  6.64 us
  transfers between devices with their start and end apart: 56, of which 17 were waited for; matrix products, arithmetic and copies ran while one was open for 2% of the time, Pallas kernels for 15%

profile of v2, /device:TPU:0, one launch (start us, length us, event | category | flops | bytes accessed | tf_op | source)
XLA Modules:
  0.0 225.0 jit_solution(14784108816863503902)
XLA Ops:
  1.4 3.1 %collective-permute-start.12 = (f32[32,256]{1,0:T(8,128)S(1)}, f32[32,256]{1,0:T(8,128)S(1)}, u32[]{:S(2)}, u32[]{:S(2)}) collective-permute-start(f32[32,256]{1,0:T(8,128)S(1)} %dynamic-slice_bitcast_fusion.20), channel_id=1, source_target_pairs={{0,2},{2,0},{4,6},{6,4},{1,3},{3,1},{5,7},{7,5},{8,10},{10,8},{12,... | collective-permute-start | bytes 98312 | tf_op jit(solution)/shard_map/ppermute | solution.py:20
  4.5 2.6 %collective-permute-start.13 = (f32[32,256]{1,0:T(8,128)S(1)}, f32[32,256]{1,0:T(8,128)S(1)}, u32[]{:S(2)}, u32[]{:S(2)}) collective-permute-start(f32[32,256]{1,0:T(8,128)S(1)} %dynamic-slice_bitcast_fusion.20), channel_id=1, source_target_pairs={{0,4},{2,6},{4,0},{6,2},{1,5},{3,7},{5,1},{7,3},{8,12},{10,14},{12... | collective-permute-start | bytes 98312 | tf_op jit(solution)/shard_map/ppermute | solution.py:20
  7.0 2.8 %collective-permute-done.13 = f32[32,256]{1,0:T(8,128)S(1)} collective-permute-done((f32[32,256]{1,0:T(8,128)S(1)}, f32[32,256]{1,0:T(8,128)S(1)}, u32[]{:S(2)}, u32[]{:S(2)}) %collective-permute-start.13) | collective-permute-done | bytes 32800 | tf_op jit(solution)/shard_map/ppermute | solution.py:20
  9.8 2.9 %collective-permute-done.14 = f32[32,256]{1,0:T(8,128)S(1)} collective-permute-done((f32[32,256]{1,0:T(8,128)S(1)}, f32[32,256]{1,0:T(8,128)S(1)}, u32[]{:S(2)}, u32[]{:S(2)}) %collective-permute-start.14) | collective-permute-done | bytes 32800 | tf_op jit(solution)/shard_map/ppermute | solution.py:20
  14.5 2.2 copy-done
  16.7 2.5 %shard_map.60 = (f32[2,128,128]{2,1,0:T(8,128)S(1)}, f32[6,128,128]{2,1,0:T(8,128)S(1)}, f32[6,128,128]{2,1,0:T(8,128)S(1)}, f32[6,128,128]{2,1,0:T(8,128)}, f32...) custom-call(s32[3]{0:T(128)S(1)} %pad_add_fusion.s_ref, ...), custom_call_target="tpu_custom_call" | custom-call | flops 1000 | bytes 4194304 | tf_op jit(solution)/shard_map/pallas_call | solution.py:76
  22.7 2.6 %collective-permute-start.26 = (f32[2,128,128]{2,1,0:T(8,128)S(1)}, f32[2,128,128]{2,1,0:T(8,128)S(1)}, u32[]{:S(2)}, u32[]{:S(2)}) collective-permute-start(f32[2,128,128]{2,1,0:T(8,128)S(1)} %get-tuple-element.61), channel_id=1, source_target_pairs={{0,6},{2,4},{4,2},{6,0},{1,7},{3,5},{5,3},{7,1},{8,14},{10,12},{12... | collective-permute-start | bytes 393224 | tf_op jit(solution)/shard_map/ppermute | solution.py:20
  25.9 14.2 %collective-permute-done.24.refs_1_ = f32[2,128,128]{2,1,0:T(8,128)S(1)} collective-permute-done((f32[2,128,128]{2,1,0:T(8,128)S(1)}, f32[2,128,128]{2,1,0:T(8,128)S(1)}, u32[]{:S(2)}, u32[]{:S(2)}) %collective-permute-start.24) | collective-permute-done | bytes 131104 | tf_op jit(solution)/shard_map/ppermute | solution.py:20
  43.6 17.0 %collective-permute-done.10.refs_2_ = f32[2,128,128]{2,1,0:T(8,128)S(1)} collective-permute-done((f32[2,128,128]{2,1,0:T(8,128)S(1)}, f32[2,128,128]{2,1,0:T(8,128)S(1)}, u32[]{:S(2)}, u32[]{:S(2)}) %collective-permute-start.10) | collective-permute-done | bytes 131104 | tf_op jit(solution)/shard_map/ppermute | solution.py:20
  61.3 9.8 %collective-permute-done.11.refs_3_ = f32[2,128,128]{2,1,0:T(8,128)S(1)} collective-permute-done((f32[2,128,128]{2,1,0:T(8,128)S(1)}, f32[2,128,128]{2,1,0:T(8,128)S(1)}, u32[]{:S(2)}, u32[]{:S(2)}) %collective-permute-start.11) | collective-permute-done | bytes 131104 | tf_op jit(solution)/shard_map/ppermute | solution.py:20
  71.7 11.9 %collective-permute-start.19 = (f32[6,128,128]{2,1,0:T(8,128)}, f32[6,128,128]{2,1,0:T(8,128)}, u32[]{:S(2)}, u32[]{:S(2)}) collective-permute-start(f32[6,128,128]{2,1,0:T(8,128)} %get-tuple-element.52), channel_id=1, source_target_pairs={{0,4},{2,6},{4,0},{6,2},{1,5},{3,7},{5,1},{7,3},{8,12},{10,14},{12... | collective-permute-start | bytes 1179656 | tf_op jit(solution)/shard_map/ppermute | solution.py:20
  84.4 2.8 %collective-permute-start.20 = (f32[6,128,128]{2,1,0:T(8,128)}, f32[6,128,128]{2,1,0:T(8,128)}, u32[]{:S(2)}, u32[]{:S(2)}) collective-permute-start(f32[6,128,128]{2,1,0:T(8,128)} %get-tuple-element.53), channel_id=1, source_target_pairs={{0,6},{2,4},{4,2},{6,0},{1,7},{3,5},{5,3},{7,1},{8,14},{10,12},{12... | collective-permute-start | bytes 1179656 | tf_op jit(solution)/shard_map/ppermute | solution.py:20
  87.2 3.5 %shard_map.58 = (f32[16,128,128]{2,1,0:T(8,128)}, f32[16,128,128]{2,1,0:T(8,128)}, f32[16,128,128]{2,1,0:T(8,128)S(1)}) custom-call(s32[3]{0:T(128)S(1)} %pad_add_fusion.s_ref, f32[64,128,128]{2,1,0:T(8,128)S(1)} %bitcast.113, f32[64,128,128]{2,1,0:T(8,128)S(1)} %bitcast.114, f32[64,128,128]{2,1,0:T(8,128)S(1)} %bitcast.115), custom_call_target="tpu_custom_call" | custom-call | flops 1000 | bytes 4194304 | tf_op jit(solution)/shard_map/pallas_call | solution.py:76
  91.5 2.0 shard_map.63
  97.5 5.2 %shard_map.64 = (f32[2,4,3,64,128]{4,3,2,1,0:T(8,128)S(1)}, f32[2,4,3,64,128]{4,3,2,1,0:T(8,128)S(1)}, f32[512,512]{1,0:T(8,128)S(1)}) custom-call(s32[3]{0:T(128)S(1)} %pad_add_fusion.s_ref, f32[6,128,128]{2,1,0:T(8,128)S(1)} %copy-done.8, f32[6,128,128]{2,1,0:T(8,128)S(1)} %copy-done.10, f32[6,128,128]{2,1,0:T(8,128)} %collective-permute-done.22.refs_2_, ...), custom_call_target="tpu_custom_call" | custom-call | flops 2113929216 | bytes 4194304 | tf_op jit(solution)/shard_map/pallas_call | solution.py:233
  103.6 7.2 %collective-permute-done.19.refs_2_ = f32[6,128,128]{2,1,0:T(8,128)} collective-permute-done((f32[6,128,128]{2,1,0:T(8,128)}, f32[6,128,128]{2,1,0:T(8,128)}, u32[]{:S(2)}, u32[]{:S(2)}) %collective-permute-start.19) | collective-permute-done | bytes 393248 | tf_op jit(solution)/shard_map/ppermute | solution.py:20
  110.8 5.3 %shard_map.65 = (f32[2,4,3,64,128]{4,3,2,1,0:T(8,128)S(1)}, f32[2,4,3,64,128]{4,3,2,1,0:T(8,128)S(1)}, f32[512,512]{1,0:T(8,128)S(1)}) custom-call(s32[3]{0:T(128)S(1)} %pad_add_fusion.s_ref, f32[6,128,128]{2,1,0:T(8,128)S(1)} %copy-done.6, f32[6,128,128]{2,1,0:T(8,128)} %collective-permute-done.18.refs_1_, f32[6,128,128]{2,1,0:T(8,128)} %collective-permute-done.19.refs_2_, ...), custom_call_target="tpu_custom_call" | custom-call | flops 2113929216 | bytes 4194304 | tf_op jit(solution)/shard_map/pallas_call | solution.py:233
  117.0 2.9 %shard_map.66 = (f32[2,4,1,64,128]{4,3,2,1,0:T(8,128)S(1)}, f32[2,4,1,64,128]{4,3,2,1,0:T(8,128)}, f32[4,64,512]{2,1,0:T(8,128)S(1)}, f32[4,64,512]{2,1,0:T(8,128)}) custom-call(s32[3]{0:T(128)S(1)} %pad_add_fusion.s_ref, f32[2,128,128]{2,1,0:T(8,128)S(1)} %copy-done.12, f32[2,128,128]{2,1,0:T(8,128)S(1)} %collective-permute-done.9.refs_1_, ...), custom_call_target="tpu_custom_call" | custom-call | flops 704643072 | bytes 4194304 | tf_op jit(solution)/shard_map/pallas_call | solution.py:233
  122.2 22.5 %collective-permute-done.37 = f32[1,4,1,64,128]{4,3,2,1,0:T(8,128)S(1)} collective-permute-done((f32[1,4,1,64,128]{4,3,2,1,0:T(8,128)S(1)}, f32[1,4,1,64,128]{4,3,2,1,0:T(8,128)S(1)}, u32[]{:S(2)}, u32[]{:S(2)}) %collective-permute-start.37) | collective-permute-done | bytes 131104 | tf_op jit(solution)/shard_map/ppermute | solution.py:20
  151.3 2.2 copy-done.1
  153.5 6.9 %shard_map.59 = (f32[2,128,512]{2,1,0:T(8,128)S(1)}, f32[2,128,512]{2,1,0:T(8,128)S(1)}) custom-call(s32[3]{0:T(128)S(1)} %pad_add_fusion.s_ref, f32[64,128,128]{2,1,0:T(8,128)S(1)} %bitcast.116, f32[16,128,128]{2,1,0:T(8,128)} %collective-permute-done.refs_1_, f32[16,128,128]{2,1,0:T(8,128)} %collective-permute-done.1.refs_2_, ...), custom_call_target="tpu_custom_call" | custom-call | flops 3221225472 | bytes 8388608 | tf_op jit(solution)/shard_map/pallas_call | solution.py:289
  163.2 2.8 %collective-permute-start.31 = (f32[32,512]{1,0:T(8,128)S(1)}, f32[32,512]{1,0:T(8,128)S(1)}, u32[]{:S(2)}, u32[]{:S(2)}) collective-permute-start(f32[32,512]{1,0:T(8,128)S(1)} %get-tuple-element.84), channel_id=1, source_target_pairs={{0,6},{2,4},{4,2},{6,0},{1,7},{3,5},{5,3},{7,1},{8,14},{10,12},{12... | collective-permute-start | bytes 196616 | tf_op jit(solution)/shard_map/ppermute | solution.py:20
  173.5 2.7 %collective-permute-done.32 = f32[32,512]{1,0:T(8,128)S(1)} collective-permute-done((f32[32,512]{1,0:T(8,128)S(1)}, f32[32,512]{1,0:T(8,128)S(1)}, u32[]{:S(2)}, u32[]{:S(2)}) %collective-permute-start.32) | collective-permute-done | bytes 65568 | tf_op jit(solution)/shard_map/ppermute | solution.py:20
  176.3 2.4 %collective-permute-start.40 = (f32[1,64,128]{2,1,0:T(8,128)S(1)}, f32[1,64,128]{2,1,0:T(8,128)S(1)}, u32[]{:S(2)}, u32[]{:S(2)}) collective-permute-start(f32[1,64,128]{2,1,0:T(8,128)S(1)} %get-tuple-element.90), channel_id=1, source_target_pairs={{0,6},{2,4},{4,2},{6,0},{1,7},{3,5},{5,3},{7,1},{8,14},{10,12},{12... | collective-permute-start | bytes 98312 | tf_op jit(solution)/shard_map/ppermute | solution.py:20
  180.7 6.9 %collective-permute-done.42 = f32[1,4,3,64,128]{4,3,2,1,0:T(8,128)S(1)} collective-permute-done((f32[1,4,3,64,128]{4,3,2,1,0:T(8,128)S(1)}, f32[1,4,3,64,128]{4,3,2,1,0:T(8,128)S(1)}, u32[]{:S(2)}, u32[]{:S(2)}) %collective-permute-start.42) | collective-permute-done | bytes 393248 | tf_op jit(solution)/shard_map/ppermute | solution.py:20
  189.0 2.2 collective-permute-done.4
  194.3 2.8 %collective-permute-start.55 = (f32[1,64,128]{2,1,0:T(8,128)S(1)}, f32[1,64,128]{2,1,0:T(8,128)S(1)}, u32[]{:S(2)}, u32[]{:S(2)}) collective-permute-start(f32[1,64,128]{2,1,0:T(8,128)S(1)} %get-tuple-element.86), channel_id=1, source_target_pairs={{0,6},{2,4},{4,2},{6,0},{1,7},{3,5},{5,3},{7,1},{8,14},{10,12},{12... | collective-permute-start | bytes 98312 | tf_op jit(solution)/shard_map/ppermute | solution.py:20
  200.8 2.8 %collective-permute-start.50 = (f32[3,64,128]{2,1,0:T(8,128)S(1)}, f32[3,64,128]{2,1,0:T(8,128)S(1)}, u32[]{:S(2)}, u32[]{:S(2)}) collective-permute-start(f32[3,64,128]{2,1,0:T(8,128)S(1)} %get-tuple-element.75), channel_id=1, source_target_pairs={{0,6},{2,4},{4,2},{6,0},{1,7},{3,5},{5,3},{7,1},{8,14},{10,12},{12... | collective-permute-start | bytes 294920 | tf_op jit(solution)/shard_map/ppermute | solution.py:20
  205.2 2.8 %collective-permute-start.45 = (f32[3,64,128]{2,1,0:T(8,128)S(1)}, f32[3,64,128]{2,1,0:T(8,128)S(1)}, u32[]{:S(2)}, u32[]{:S(2)}) collective-permute-start(f32[3,64,128]{2,1,0:T(8,128)S(1)} %get-tuple-element.79), channel_id=1, source_target_pairs={{0,6},{2,4},{4,2},{6,0},{1,7},{3,5},{5,3},{7,1},{8,14},{10,12},{12... | collective-permute-start | bytes 294920 | tf_op jit(solution)/shard_map/ppermute | solution.py:20
  207.9 3.5 %collective-permute-done.49.refs_10_ = f32[3,64,128]{2,1,0:T(8,128)S(1)} collective-permute-done((f32[3,64,128]{2,1,0:T(8,128)S(1)}, f32[3,64,128]{2,1,0:T(8,128)S(1)}, u32[]{:S(2)}, u32[]{:S(2)}) %collective-permute-start.49) | collective-permute-done | bytes 98336 | tf_op jit(solution)/shard_map/ppermute | solution.py:20
  211.5 7.2 %collective-permute-start.7 = (f32[16,512]{1,0:T(8,128)S(1)}, f32[16,512]{1,0:T(8,128)S(1)}, u32[]{:S(2)}, u32[]{:S(2)}) collective-permute-start(f32[16,512]{1,0:T(8,128)S(1)} %get-tuple-element.96), channel_id=1, source_target_pairs={{0,4},{2,6},{4,0},{6,2},{1,5},{3,7},{5,1},{7,3},{8,12},{10,14},{12... | collective-permute-start | bytes 98312 | tf_op jit(solution)/shard_map/ppermute | solution.py:20
  221.1 2.2 shard_map.68
  (160 shorter events, 53.5 us)
Async XLA Ops:
  20.0 63.7 %collective-permute-start.21 = (f32[6,128,128]{2,1,0:T(8,128)S(1)}, f32[6,128,128]{2,1,0:T(8,128)S(1)}, u32[]{:S(2)}, u32[]{:S(2)}) collective-permute-start(f32[6,128,128]{2,1,0:T(8,128)S(1)} %get-tuple-element.55), channel_id=1, source_target_pairs={{0,2},{2,0},{4,6},{6,4},{1,3},{3,1},{5,7},{7,5},{8,10},{10,8},{12,... | collective-permute-start | bytes 1179656 | tf_op jit(solution)/shard_map/ppermute | solution.py:20
  20.9 19.2 %collective-permute-start.24 = (f32[2,128,128]{2,1,0:T(8,128)S(1)}, f32[2,128,128]{2,1,0:T(8,128)S(1)}, u32[]{:S(2)}, u32[]{:S(2)}) collective-permute-start(f32[2,128,128]{2,1,0:T(8,128)S(1)} %get-tuple-element.59), channel_id=1, source_target_pairs={{0,2},{2,0},{4,6},{6,4},{1,3},{3,1},{5,7},{7,5},{8,10},{10,8},{12,... | collective-permute-start | bytes 393224 | tf_op jit(solution)/shard_map/ppermute | solution.py:20
  22.7 18.2 %collective-permute-start.25 = (f32[2,128,128]{2,1,0:T(8,128)S(1)}, f32[2,128,128]{2,1,0:T(8,128)S(1)}, u32[]{:S(2)}, u32[]{:S(2)}) collective-permute-start(f32[2,128,128]{2,1,0:T(8,128)S(1)} %get-tuple-element.60), channel_id=1, source_target_pairs={{0,4},{2,6},{4,0},{6,2},{1,5},{3,7},{5,1},{7,3},{8,12},{10,14},{12... | collective-permute-start | bytes 393224 | tf_op jit(solution)/shard_map/ppermute | solution.py:20
  22.7 20.0 %collective-permute-start.26 = (f32[2,128,128]{2,1,0:T(8,128)S(1)}, f32[2,128,128]{2,1,0:T(8,128)S(1)}, u32[]{:S(2)}, u32[]{:S(2)}) collective-permute-start(f32[2,128,128]{2,1,0:T(8,128)S(1)} %get-tuple-element.61), channel_id=1, source_target_pairs={{0,6},{2,4},{4,2},{6,0},{1,7},{3,5},{5,3},{7,1},{8,14},{10,12},{12... | collective-permute-start | bytes 393224 | tf_op jit(solution)/shard_map/ppermute | solution.py:20
  25.3 35.3 %collective-permute-start.10 = (f32[2,128,128]{2,1,0:T(8,128)S(1)}, f32[2,128,128]{2,1,0:T(8,128)S(1)}, u32[]{:S(2)}, u32[]{:S(2)}) collective-permute-start(f32[2,128,128]{2,1,0:T(8,128)S(1)} %get-tuple-element.46), channel_id=1, source_target_pairs={{0,4},{2,6},{4,0},{6,2},{1,5},{3,7},{5,1},{7,3},{8,12},{10,14},{12... | collective-permute-start | bytes 393224 | tf_op jit(solution)/shard_map/ppermute | solution.py:20
  40.1 53.5 %collective-permute-start.22 = (f32[6,128,128]{2,1,0:T(8,128)}, f32[6,128,128]{2,1,0:T(8,128)}, u32[]{:S(2)}, u32[]{:S(2)}) collective-permute-start(f32[6,128,128]{2,1,0:T(8,128)} %get-tuple-element.56), channel_id=1, source_target_pairs={{0,4},{2,6},{4,0},{6,2},{1,5},{3,7},{5,1},{7,3},{8,12},{10,14},{12... | collective-permute-start | bytes 1179656 | tf_op jit(solution)/shard_map/ppermute | solution.py:20
  40.9 52.8 %collective-permute-start.23 = (f32[6,128,128]{2,1,0:T(8,128)}, f32[6,128,128]{2,1,0:T(8,128)}, u32[]{:S(2)}, u32[]{:S(2)}) collective-permute-start(f32[6,128,128]{2,1,0:T(8,128)} %get-tuple-element.57), channel_id=1, source_target_pairs={{0,6},{2,4},{4,2},{6,0},{1,7},{3,5},{5,3},{7,1},{8,14},{10,12},{12... | collective-permute-start | bytes 1179656 | tf_op jit(solution)/shard_map/ppermute | solution.py:20
  42.8 52.5 %collective-permute-start.18 = (f32[6,128,128]{2,1,0:T(8,128)}, f32[6,128,128]{2,1,0:T(8,128)}, u32[]{:S(2)}, u32[]{:S(2)}) collective-permute-start(f32[6,128,128]{2,1,0:T(8,128)} %get-tuple-element.51), channel_id=1, source_target_pairs={{0,2},{2,0},{4,6},{6,4},{1,3},{3,1},{5,7},{7,5},{8,10},{10,8},{12,... | collective-permute-start | bytes 1179656 | tf_op jit(solution)/shard_map/ppermute | solution.py:20
  71.7 39.0 %collective-permute-start.19 = (f32[6,128,128]{2,1,0:T(8,128)}, f32[6,128,128]{2,1,0:T(8,128)}, u32[]{:S(2)}, u32[]{:S(2)}) collective-permute-start(f32[6,128,128]{2,1,0:T(8,128)} %get-tuple-element.52), channel_id=1, source_target_pairs={{0,4},{2,6},{4,0},{6,2},{1,5},{3,7},{5,1},{7,3},{8,12},{10,14},{12... | collective-permute-start | bytes 1179656 | tf_op jit(solution)/shard_map/ppermute | solution.py:20
  84.4 26.4 %collective-permute-start.20 = (f32[6,128,128]{2,1,0:T(8,128)}, f32[6,128,128]{2,1,0:T(8,128)}, u32[]{:S(2)}, u32[]{:S(2)}) collective-permute-start(f32[6,128,128]{2,1,0:T(8,128)} %get-tuple-element.53), channel_id=1, source_target_pairs={{0,6},{2,4},{4,2},{6,0},{1,7},{3,5},{5,3},{7,1},{8,14},{10,12},{12... | collective-permute-start | bytes 1179656 | tf_op jit(solution)/shard_map/ppermute | solution.py:20
  93.6 55.6 %collective-permute-start = (f32[16,128,128]{2,1,0:T(8,128)}, f32[16,128,128]{2,1,0:T(8,128)}, u32[]{:S(2)}, u32[]{:S(2)}) collective-permute-start(f32[16,128,128]{2,1,0:T(8,128)} %get-tuple-element.39), channel_id=1, source_target_pairs={{0,8},{8,0},{16,24},{24,16},{1,9},{9,1},{17,25},{25,17},{2,10},{10... | collective-permute-start | bytes 3145736 | tf_op jit(solution)/shard_map/ppermute | solution.py:20
  93.7 57.1 %collective-permute-start.1 = (f32[16,128,128]{2,1,0:T(8,128)}, f32[16,128,128]{2,1,0:T(8,128)}, u32[]{:S(2)}, u32[]{:S(2)}) collective-permute-start(f32[16,128,128]{2,1,0:T(8,128)} %get-tuple-element.40), channel_id=1, source_target_pairs={{0,16},{8,24},{16,0},{24,8},{1,17},{9,25},{17,1},{25,9},{2,18},{10... | collective-permute-start | bytes 3145736 | tf_op jit(solution)/shard_map/ppermute | solution.py:20
  95.2 56.1 %collective-permute-start.2 = (f32[16,128,128]{2,1,0:T(8,128)S(1)}, f32[16,128,128]{2,1,0:T(8,128)}, u32[]{:S(2)}, u32[]{:S(2)}) collective-permute-start(f32[16,128,128]{2,1,0:T(8,128)S(1)} %get-tuple-element.41), channel_id=1, source_target_pairs={{0,24},{8,16},{16,8},{24,0},{1,25},{9,17},{17,9},{25,1},{2,26},{10... | collective-permute-start | bytes 3145736 | tf_op jit(solution)/shard_map/ppermute | solution.py:20
  119.9 27.8 %collective-permute-start.27 = (f32[4,64,512]{2,1,0:T(8,128)}, f32[4,64,512]{2,1,0:T(8,128)}, u32[]{:S(2)}, u32[]{:S(2)}) collective-permute-start(f32[4,64,512]{2,1,0:T(8,128)} %get-tuple-element.66), channel_id=1, source_target_pairs={{0,8},{8,0},{16,24},{24,16},{1,9},{9,1},{17,25},{25,17},{2,10},{10... | collective-permute-start | bytes 1572872 | tf_op jit(solution)/shard_map/ppermute | solution.py:20
  121.2 23.5 %collective-permute-start.37 = (f32[1,4,1,64,128]{4,3,2,1,0:T(8,128)S(1)}, f32[1,4,1,64,128]{4,3,2,1,0:T(8,128)S(1)}, u32[]{:S(2)}, u32[]{:S(2)}) collective-permute-start(f32[1,4,1,64,128]{4,3,2,1,0:T(8,128)S(1)} %slice.41), channel_id=1, source_target_pairs={{0,16},{8,24},{16,0},{24,8},{1,17},{9,25},{17,1},{25,9},{2,18},{10... | collective-permute-start | bytes 393224 | tf_op jit(solution)/shard_map/ppermute | solution.py:20
  146.6 16.6 %collective-permute-start.46 = (f32[2,4,3,64,128]{4,3,2,1,0:T(8,128)}, f32[2,4,3,64,128]{4,3,2,1,0:T(8,128)S(1)}, u32[]{:S(2)}, u32[]{:S(2)}) collective-permute-start(f32[2,4,3,64,128]{4,3,2,1,0:T(8,128)} %copy-done.4), channel_id=1, source_target_pairs={{0,8},{8,0},{16,24},{24,16},{1,9},{9,1},{17,25},{25,17},{2,10},{10... | collective-permute-start | bytes 2359304 | tf_op jit(solution)/shard_map/ppermute | solution.py:20
  147.8 18.4 %collective-permute-start.41 = (f32[2,4,3,64,128]{4,3,2,1,0:T(8,128)}, f32[2,4,3,64,128]{4,3,2,1,0:T(8,128)S(1)}, u32[]{:S(2)}, u32[]{:S(2)}) collective-permute-start(f32[2,4,3,64,128]{4,3,2,1,0:T(8,128)} %copy-done.3), channel_id=1, source_target_pairs={{0,8},{8,0},{16,24},{24,16},{1,9},{9,1},{17,25},{25,17},{2,10},{10... | collective-permute-start | bytes 2359304 | tf_op jit(solution)/shard_map/ppermute | solution.py:20
  149.2 12.4 %collective-permute-start.52 = (f32[1,4,1,64,128]{4,3,2,1,0:T(8,128)S(1)}, f32[1,4,1,64,128]{4,3,2,1,0:T(8,128)S(1)}, u32[]{:S(2)}, u32[]{:S(2)}) collective-permute-start(f32[1,4,1,64,128]{4,3,2,1,0:T(8,128)S(1)} %slice.47), channel_id=1, source_target_pairs={{0,16},{8,24},{16,0},{24,8},{1,17},{9,25},{17,1},{25,9},{2,18},{10... | collective-permute-start | bytes 393224 | tf_op jit(solution)/shard_map/ppermute | solution.py:20
  160.4 15.8 %collective-permute-start.3 = (f32[2,128,512]{2,1,0:T(8,128)S(1)}, f32[2,128,512]{2,1,0:T(8,128)S(1)}, u32[]{:S(2)}, u32[]{:S(2)}) collective-permute-start(f32[2,128,512]{2,1,0:T(8,128)S(1)} %get-tuple-element.43), channel_id=1, source_target_pairs={{0,8},{8,0},{16,24},{24,16},{1,9},{9,1},{17,25},{25,17},{2,10},{10... | collective-permute-start | bytes 1572872 | tf_op jit(solution)/shard_map/ppermute | solution.py:20
  166.2 26.7 %collective-permute-start.38 = (f32[1,64,128]{2,1,0:T(8,128)S(1)}, f32[1,64,128]{2,1,0:T(8,128)S(1)}, u32[]{:S(2)}, u32[]{:S(2)}) collective-permute-start(f32[1,64,128]{2,1,0:T(8,128)S(1)} %get-tuple-element.92), channel_id=1, source_target_pairs={{0,2},{2,0},{4,6},{6,4},{1,3},{3,1},{5,7},{7,5},{8,10},{10,8},{12,... | collective-permute-start | bytes 98312 | tf_op jit(solution)/shard_map/ppermute | solution.py:20
  167.2 12.0 %collective-permute-start.47 = (f32[1,4,3,64,128]{4,3,2,1,0:T(8,128)S(1)}, f32[1,4,3,64,128]{4,3,2,1,0:T(8,128)S(1)}, u32[]{:S(2)}, u32[]{:S(2)}) collective-permute-start(f32[1,4,3,64,128]{4,3,2,1,0:T(8,128)S(1)} %slice.45), channel_id=1, source_target_pairs={{0,16},{8,24},{16,0},{24,8},{1,17},{9,25},{17,1},{25,9},{2,18},{10... | collective-permute-start | bytes 1179656 | tf_op jit(solution)/shard_map/ppermute | solution.py:20
  170.4 17.2 %collective-permute-start.42 = (f32[1,4,3,64,128]{4,3,2,1,0:T(8,128)S(1)}, f32[1,4,3,64,128]{4,3,2,1,0:T(8,128)S(1)}, u32[]{:S(2)}, u32[]{:S(2)}) collective-permute-start(f32[1,4,3,64,128]{4,3,2,1,0:T(8,128)S(1)} %slice.43), channel_id=1, source_target_pairs={{0,16},{8,24},{16,0},{24,8},{1,17},{9,25},{17,1},{25,9},{2,18},{10... | collective-permute-start | bytes 1179656 | tf_op jit(solution)/shard_map/ppermute | solution.py:20
  176.2 18.1 %collective-permute-start.39 = (f32[1,64,128]{2,1,0:T(8,128)S(1)}, f32[1,64,128]{2,1,0:T(8,128)S(1)}, u32[]{:S(2)}, u32[]{:S(2)}) collective-permute-start(f32[1,64,128]{2,1,0:T(8,128)S(1)} %get-tuple-element.91), channel_id=1, source_target_pairs={{0,4},{2,6},{4,0},{6,2},{1,5},{3,7},{5,1},{7,3},{8,12},{10,14},{12... | collective-permute-start | bytes 98312 | tf_op jit(solution)/shard_map/ppermute | solution.py:20
  176.3 20.9 %collective-permute-start.40 = (f32[1,64,128]{2,1,0:T(8,128)S(1)}, f32[1,64,128]{2,1,0:T(8,128)S(1)}, u32[]{:S(2)}, u32[]{:S(2)}) collective-permute-start(f32[1,64,128]{2,1,0:T(8,128)S(1)} %get-tuple-element.90), channel_id=1, source_target_pairs={{0,6},{2,4},{4,2},{6,0},{1,7},{3,5},{5,3},{7,1},{8,14},{10,12},{12... | collective-permute-start | bytes 98312 | tf_op jit(solution)/shard_map/ppermute | solution.py:20
  179.2 12.0 %collective-permute-start.4 = (f32[1,128,512]{2,1,0:T(8,128)S(1)}, f32[1,128,512]{2,1,0:T(8,128)S(1)}, u32[]{:S(2)}, u32[]{:S(2)}) collective-permute-start(f32[1,128,512]{2,1,0:T(8,128)S(1)} %dynamic-slice_add_fusion), channel_id=1, source_target_pairs={{0,16},{8,24},{16,0},{24,8},{1,17},{9,25},{17,1},{25,9},{2,18},{10... | collective-permute-start | bytes 786440 | tf_op jit(solution)/shard_map/ppermute | solution.py:20
  200.1 11.3 %collective-permute-start.49 = (f32[3,64,128]{2,1,0:T(8,128)S(1)}, f32[3,64,128]{2,1,0:T(8,128)S(1)}, u32[]{:S(2)}, u32[]{:S(2)}) collective-permute-start(f32[3,64,128]{2,1,0:T(8,128)S(1)} %get-tuple-element.76), channel_id=1, source_target_pairs={{0,4},{2,6},{4,0},{6,2},{1,5},{3,7},{5,1},{7,3},{8,12},{10,14},{12... | collective-permute-start | bytes 294920 | tf_op jit(solution)/shard_map/ppermute | solution.py:20
  200.8 10.7 %collective-permute-start.50 = (f32[3,64,128]{2,1,0:T(8,128)S(1)}, f32[3,64,128]{2,1,0:T(8,128)S(1)}, u32[]{:S(2)}, u32[]{:S(2)}) collective-permute-start(f32[3,64,128]{2,1,0:T(8,128)S(1)} %get-tuple-element.75), channel_id=1, source_target_pairs={{0,6},{2,4},{4,2},{6,0},{1,7},{3,5},{5,3},{7,1},{8,14},{10,12},{12... | collective-permute-start | bytes 294920 | tf_op jit(solution)/shard_map/ppermute | solution.py:20
  203.5 15.1 %collective-permute-start.43 = (f32[3,64,128]{2,1,0:T(8,128)S(1)}, f32[3,64,128]{2,1,0:T(8,128)S(1)}, u32[]{:S(2)}, u32[]{:S(2)}) collective-permute-start(f32[3,64,128]{2,1,0:T(8,128)S(1)} %get-tuple-element.81), channel_id=1, source_target_pairs={{0,2},{2,0},{4,6},{6,4},{1,3},{3,1},{5,7},{7,5},{8,10},{10,8},{12,... | collective-permute-start | bytes 294920 | tf_op jit(solution)/shard_map/ppermute | solution.py:20
  203.6 17.5 %collective-permute-start.44 = (f32[3,64,128]{2,1,0:T(8,128)S(1)}, f32[3,64,128]{2,1,0:T(8,128)S(1)}, u32[]{:S(2)}, u32[]{:S(2)}) collective-permute-start(f32[3,64,128]{2,1,0:T(8,128)S(1)} %get-tuple-element.80), channel_id=1, source_target_pairs={{0,4},{2,6},{4,0},{6,2},{1,5},{3,7},{5,1},{7,3},{8,12},{10,14},{12... | collective-permute-start | bytes 294920 | tf_op jit(solution)/shard_map/ppermute | solution.py:20
  205.2 16.0 %collective-permute-start.45 = (f32[3,64,128]{2,1,0:T(8,128)S(1)}, f32[3,64,128]{2,1,0:T(8,128)S(1)}, u32[]{:S(2)}, u32[]{:S(2)}) collective-permute-start(f32[3,64,128]{2,1,0:T(8,128)S(1)} %get-tuple-element.79), channel_id=1, source_target_pairs={{0,6},{2,4},{4,2},{6,0},{1,7},{3,5},{5,3},{7,1},{8,14},{10,12},{12... | collective-permute-start | bytes 294920 | tf_op jit(solution)/shard_map/ppermute | solution.py:20
  211.4 11.9 %collective-permute-start.6 = (f32[16,512]{1,0:T(8,128)S(1)}, f32[16,512]{1,0:T(8,128)S(1)}, u32[]{:S(2)}, u32[]{:S(2)}) collective-permute-start(f32[16,512]{1,0:T(8,128)S(1)} %get-tuple-element.94), channel_id=1, source_target_pairs={{0,2},{2,0},{4,6},{6,4},{1,3},{3,1},{5,7},{7,5},{8,10},{10,8},{12,... | collective-permute-start | bytes 98312 | tf_op jit(solution)/shard_map/ppermute | solution.py:20
  211.5 11.9 %collective-permute-start.7 = (f32[16,512]{1,0:T(8,128)S(1)}, f32[16,512]{1,0:T(8,128)S(1)}, u32[]{:S(2)}, u32[]{:S(2)}) collective-permute-start(f32[16,512]{1,0:T(8,128)S(1)} %get-tuple-element.96), channel_id=1, source_target_pairs={{0,4},{2,6},{4,0},{6,2},{1,5},{3,7},{5,1},{7,3},{8,12},{10,14},{12... | collective-permute-start | bytes 98312 | tf_op jit(solution)/shard_map/ppermute | solution.py:20
  (43 other events, 245.8 us)

commit v3 on v2

--- a/solution.py
+++ b/solution.py
@@ -41,9 +41,7 @@
 
 
 def chunk_sizes(own):
-    edge = max(2, own // 8)
-    middle = (own - 2 * edge) // 2
-    sizes = (edge, middle, own - 2 * edge - middle, edge)
+    sizes = (own // 2, own // 2 - max(2, own // 8), max(2, own // 8))
     assert all(n > 0 and n % 2 == 0 for n in sizes)
     return sizes
 
@@ -79,7 +77,6 @@
             num_scalar_prefetch=1, grid=(steps,), in_specs=in_specs, out_specs=out_specs
         ),
         out_shape=out_shape,
-        compiler_params=params(),
         cost_estimate=pl.CostEstimate(flops=1000, bytes_accessed=1 << 22, transcendentals=0),
     )(where, *[flat] * len(pieces))
 
@@ -377,10 +374,10 @@
         bit = 1
         while bit < nx:
             got = swap(sent, "gx", bit)
+            if 2 * bit < nx:
+                sent = keep[1::2] + got[1::2]
+                keep, got = keep[0::2], got[0::2]
             keep = keep + got
-            if 2 * bit < nx:
-                sent = keep[1::2]
-                keep = keep[0::2]
             bit *= 2
         keep = keep[0]
         z_parts = [pick(keep, me_y ^ k, 0) for k in range(ny)]

time: 225 us -> 268 us (1.19)
  waiting for transfers between devices: 97.3 us -> 155 us
  starting transfers between devices: 75.6 us -> 55.4 us
  Pallas kernels: 33.1 us -> 41 us
  local copies, waits for them, and re-layouts: 12.8 us -> 8.22 us
    ppermute x56 -> x48, waiting for transfers between devices: 97.3 us -> 155 us  [swap(): return lax.ppermute(value, axis, [(i, i ^ offset) for i in range(size)])]
    ppermute x56 -> x48, starting transfers between devices: 75.6 us -> 55.4 us  [swap(): return lax.ppermute(value, axis, [(i, i ^ offset) for i in range(size)])]
    pallas_call x3, Pallas kernels: 6.64 us -> 16.6 us  [cut(): pl.pallas_call(cut_kernel, grid_spec=pltpu.PrefetchScalarGridSpec(num_sca...]
    unnamed x39 -> x29, local copies, waits for them, and re-layouts: 11.8 us -> 8.07 us
    pallas_call x4 -> x3, Pallas kernels: 15.4 us -> 13.3 us  [chunk_terms(): pl.pallas_call(functools.partial(chunk_kernel, sizes, first, last), grid_...]
  transfers between devices with their start and end apart: 56 -> 48, of which waited for: 17 -> 14; matrix products, arithmetic and copies ran while one was open for 2% -> 2% of each run, Pallas kernels for 15% -> 12%
where the time goes in v3:
time: 268 us; the launch traced here: 267 us
  waiting for transfers between devices  155 us (58%)
  starting transfers between devices  55.4 us (21%)
  Pallas kernels  41 us (15%)
  local copies, waits for them, and re-layouts  8.22 us (3%)
  other arithmetic  6.42 us (2%)
    ppermute x48, waiting for transfers between devices, swap(): return lax.ppermute(value, axis, [(i, i ^ offset) for i in range(size)])  155 us
    ppermute x48, starting transfers between devices, swap(): return lax.ppermute(value, axis, [(i, i ^ offset) for i in range(size)])  55.4 us
    pallas_call x3, Pallas kernels, cut(): pl.pallas_call(cut_kernel, grid_spec=pltpu.PrefetchScalarGridSpec(num_sca...  16.6 us
    pallas_call x3, Pallas kernels, chunk_terms(): pl.pallas_call(functools.partial(chunk_kernel, sizes, first, last), grid_...  13.3 us
    unnamed x29, local copies, waits for them, and re-layouts  8.07 us
    pallas_call x1, Pallas kernels, gram_x_terms(): pl.pallas_call(functools.partial(gram_x_kernel, sizes), grid_spec=pltpu.P...  6.89 us
  transfers between devices with their start and end apart: 48, of which 14 were waited for; matrix products, arithmetic and copies ran while one was open for 2% of the time, Pallas kernels for 12%

profile of v3, /device:TPU:0, one launch (start us, length us, event | category | flops | bytes accessed | tf_op | source)
XLA Modules:
  0.0 267.4 jit_solution(4735515412468252734)
XLA Ops:
  1.3 4.5 %shard_map.62 = (f32[8,128,128]{2,1,0:T(8,128)}, f32[8,128,128]{2,1,0:T(8,128)}, f32[8,128,128]{2,1,0:T(8,128)}) custom-call(s32[3]{0:T(128)} %pad_add_fusion.s_ref, f32[64,128,128]{2,1,0:T(8,128)} %bitcast.89, f32[64,128,128]{2,1,0:T(8,128)} %bitcast.90, f32[64,128,128]{2,1,0:T(8,128)} %bitcast.91), custom_call_target="tpu_custom_call" | custom-call | flops 1000 | bytes 4194304 | tf_op jit(solution)/shard_map/pallas_call | solution.py:74
  5.7 3.1 %collective-permute-start.21 = (f32[8,128,128]{2,1,0:T(8,128)}, f32[8,128,128]{2,1,0:T(8,128)S(1)}, u32[]{:S(2)}, u32[]{:S(2)}) collective-permute-start(f32[8,128,128]{2,1,0:T(8,128)} %get-tuple-element.48), channel_id=1, source_target_pairs={{0,2},{2,0},{4,6},{6,4},{1,3},{3,1},{5,7},{7,5},{8,10},{10,8},{12,... | collective-permute-start | bytes 1572872 | tf_op jit(solution)/shard_map/ppermute | solution.py:20
  8.8 2.6 collective-permute-start.22
  12.3 3.5 %collective-permute-start.13 = (f32[32,256]{1,0:T(8,128)S(1)}, f32[32,256]{1,0:T(8,128)S(1)}, u32[]{:S(2)}, u32[]{:S(2)}) collective-permute-start(f32[32,256]{1,0:T(8,128)S(1)} %dynamic-slice_bitcast_fusion.16), channel_id=1, source_target_pairs={{0,4},{2,6},{4,0},{6,2},{1,5},{3,7},{5,1},{7,3},{8,12},{10,14},{12... | collective-permute-start | bytes 98312 | tf_op jit(solution)/shard_map/ppermute | solution.py:20
  15.8 28.0 %collective-permute-done.12 = f32[32,256]{1,0:T(8,128)S(1)} collective-permute-done((f32[32,256]{1,0:T(8,128)S(1)}, f32[32,256]{1,0:T(8,128)S(1)}, u32[]{:S(2)}, u32[]{:S(2)}) %collective-permute-start.12) | collective-permute-done | bytes 32800 | tf_op jit(solution)/shard_map/ppermute | solution.py:20
  43.8 2.5 collective-permute-start.14
  46.2 13.3 %collective-permute-done.13 = f32[32,256]{1,0:T(8,128)S(1)} collective-permute-done((f32[32,256]{1,0:T(8,128)S(1)}, f32[32,256]{1,0:T(8,128)S(1)}, u32[]{:S(2)}, u32[]{:S(2)}) %collective-permute-start.13) | collective-permute-done | bytes 32800 | tf_op jit(solution)/shard_map/ppermute | solution.py:20
  62.1 5.3 %shard_map.60 = (f32[8,128,128]{2,1,0:T(8,128)}, f32[6,128,128]{2,1,0:T(8,128)}, f32[6,128,128]{2,1,0:T(8,128)}, f32[6,128,128]{2,1,0:T(8,128)}, f32[6,128,128]{...) custom-call(s32[3]{0:T(128)} %pad_add_fusion.s_ref, ...), custom_call_target="tpu_custom_call" | custom-call | flops 1000 | bytes 4194304 | tf_op jit(solution)/shard_map/pallas_call | solution.py:74
  68.4 2.1 collective-permute-start.19
  80.0 5.1 %shard_map.63 = (f32[2,4,4,64,128]{4,3,2,1,0:T(8,128)S(1)}, f32[2,4,4,64,128]{4,3,2,1,0:T(8,128)S(1)}, f32[512,512]{1,0:T(8,128)S(1)}) custom-call(s32[3]{0:T(128)S(1)} %copy-done.2, f32[8,128,128]{2,1,0:T(8,128)S(1)} %copy-done.9, f32[8,128,128]{2,1,0:T(8,128)S(1)} %collective-permute-done.21.refs_1_, f32[8,128,128]{2,1,0:T(8,128)S(1)} %copy-done.6, ...), custom_call_target="tpu_custom_call" | custom-call | flops 2818572288 | bytes 4194304 | tf_op jit(solution)/shard_map/pallas_call | solution.py:230
  87.2 17.0 %collective-permute-done.19.refs_2_ = f32[6,128,128]{2,1,0:T(8,128)} collective-permute-done((f32[6,128,128]{2,1,0:T(8,128)}, f32[6,128,128]{2,1,0:T(8,128)}, u32[]{:S(2)}, u32[]{:S(2)}) %collective-permute-start.19) | collective-permute-done | bytes 393248 | tf_op jit(solution)/shard_map/ppermute | solution.py:20
  104.2 5.3 %shard_map.64 = (f32[2,4,3,64,128]{4,3,2,1,0:T(8,128)S(1)}, f32[2,4,3,64,128]{4,3,2,1,0:T(8,128)S(1)}, f32[512,512]{1,0:T(8,128)S(1)}) custom-call(s32[3]{0:T(128)S(1)} %copy-done.2, f32[6,128,128]{2,1,0:T(8,128)S(1)} %copy-done.10, f32[6,128,128]{2,1,0:T(8,128)} %collective-permute-done.18.refs_1_, f32[6,128,128]{2,1,0:T(8,128)} %collective-permute-done.19.refs_2_, ...), custom_call_target="tpu_custom_call" | custom-call | flops 2113929216 | bytes 4194304 | tf_op jit(solution)/shard_map/pallas_call | solution.py:230
  109.5 5.8 %collective-permute-done.10.refs_2_ = f32[2,128,128]{2,1,0:T(8,128)S(1)} collective-permute-done((f32[2,128,128]{2,1,0:T(8,128)}, f32[2,128,128]{2,1,0:T(8,128)S(1)}, u32[]{:S(2)}, u32[]{:S(2)}) %collective-permute-start.10) | collective-permute-done | bytes 131104 | tf_op jit(solution)/shard_map/ppermute | solution.py:20
  115.3 2.9 %shard_map.65 = (f32[2,4,1,64,128]{4,3,2,1,0:T(8,128)S(1)}, f32[2,4,1,64,128]{4,3,2,1,0:T(8,128)}, f32[4,64,512]{2,1,0:T(8,128)S(1)}, f32[4,64,512]{2,1,0:T(8,128)}) custom-call(s32[3]{0:T(128)S(1)} %copy-done.2, f32[2,128,128]{2,1,0:T(8,128)S(1)} %copy-done.11, f32[2,128,128]{2,1,0:T(8,128)S(1)} %collective-permute-done.9.refs_1_, ...), custom_call_target="tpu_custom_call" | custom-call | flops 704643072 | bytes 4194304 | tf_op jit(solution)/shard_map/pallas_call | solution.py:230
  118.7 6.9 %shard_map.58 = (f32[16,128,128]{2,1,0:T(8,128)}, f32[16,128,128]{2,1,0:T(8,128)}, f32[16,128,128]{2,1,0:T(8,128)}) custom-call(s32[3]{0:T(128)} %pad_add_fusion.s_ref, f32[64,128,128]{2,1,0:T(8,128)} %bitcast.101, f32[64,128,128]{2,1,0:T(8,128)} %bitcast.102, f32[64,128,128]{2,1,0:T(8,128)} %bitcast.103), custom_call_target="tpu_custom_call" | custom-call | flops 1000 | bytes 4194304 | tf_op jit(solution)/shard_map/pallas_call | solution.py:74
  129.3 1.7 fusion.2
  132.2 45.1 %collective-permute-done.44 = f32[1,4,1,64,128]{4,3,2,1,0:T(8,128)} collective-permute-done((f32[1,4,1,64,128]{4,3,2,1,0:T(8,128)S(1)}, f32[1,4,1,64,128]{4,3,2,1,0:T(8,128)}, u32[]{:S(2)}, u32[]{:S(2)}) %collective-permute-start.44) | collective-permute-done | bytes 131104 | tf_op jit(solution)/shard_map/ppermute | solution.py:20
  178.3 4.1 %collective-permute-done.25 = f32[4,32,512]{2,1,0:T(8,128)} collective-permute-done((f32[4,32,512]{2,1,0:T(8,128)}, f32[4,32,512]{2,1,0:T(8,128)}, u32[]{:S(2)}, u32[]{:S(2)}) %collective-permute-start.25) | collective-permute-done | bytes 262176 | tf_op jit(solution)/shard_map/ppermute | solution.py:20
  183.5 3.3 %collective-permute-start.26 = (f32[32,512]{1,0:T(8,128)S(1)}, f32[32,512]{1,0:T(8,128)S(1)}, u32[]{:S(2)}, u32[]{:S(2)}) collective-permute-start(f32[32,512]{1,0:T(8,128)S(1)} %get-tuple-element.69), channel_id=1, source_target_pairs={{0,2},{2,0},{4,6},{6,4},{1,3},{3,1},{5,7},{7,5},{8,10},{10,8},{12,... | collective-permute-start | bytes 196616 | tf_op jit(solution)/shard_map/ppermute | solution.py:20
  189.4 2.2 copy-done
  191.6 6.9 %shard_map.59 = (f32[2,128,512]{2,1,0:T(8,128)S(1)}, f32[2,128,512]{2,1,0:T(8,128)S(1)}) custom-call(s32[3]{0:T(128)S(1)} %copy-done.3, f32[64,128,128]{2,1,0:T(8,128)S(1)} %bitcast.104, f32[16,128,128]{2,1,0:T(8,128)} %collective-permute-done.refs_1_, f32[16,128,128]{2,1,0:T(8,128)} %collective-permute-done.1.refs_2_, ...), custom_call_target="tpu_custom_call" | custom-call | flops 3221225472 | bytes 8388608 | tf_op jit(solution)/shard_map/pallas_call | solution.py:286
  200.2 2.9 %collective-permute-done.29 = f32[32,512]{1,0:T(8,128)S(1)} collective-permute-done((f32[32,512]{1,0:T(8,128)S(1)}, f32[32,512]{1,0:T(8,128)S(1)}, u32[]{:S(2)}, u32[]{:S(2)}) %collective-permute-start.29) | collective-permute-done | bytes 65568 | tf_op jit(solution)/shard_map/ppermute | solution.py:20
  206.2 2.1 collective-permute-done.31.refs_2_
  208.3 2.0 collective-permute-start.46
  215.1 14.2 %collective-permute-done.4 = f32[1,128,512]{2,1,0:T(8,128)S(1)} collective-permute-done((f32[1,128,512]{2,1,0:T(8,128)S(1)}, f32[1,128,512]{2,1,0:T(8,128)S(1)}, u32[]{:S(2)}, u32[]{:S(2)}) %collective-permute-start.4) | collective-permute-done | bytes 262176 | tf_op jit(solution)/shard_map/ppermute | solution.py:20
  231.9 3.3 %collective-permute-done.5 = f32[4,16,512]{2,1,0:T(8,128)S(1)} collective-permute-done((f32[4,16,512]{2,1,0:T(8,128)S(1)}, f32[4,16,512]{2,1,0:T(8,128)S(1)}, u32[]{:S(2)}, u32[]{:S(2)}) %collective-permute-start.5) | collective-permute-done | bytes 131104 | tf_op jit(solution)/shard_map/ppermute | solution.py:20
  235.4 6.6 %collective-permute-done.34 = f32[1,4,4,64,128]{4,3,2,1,0:T(8,128)S(1)} collective-permute-done((f32[1,4,4,64,128]{4,3,2,1,0:T(8,128)S(1)}, f32[1,4,4,64,128]{4,3,2,1,0:T(8,128)S(1)}, u32[]{:S(2)}, u32[]{:S(2)}) %collective-permute-start.34) | collective-permute-done | bytes 524320 | tf_op jit(solution)/shard_map/ppermute | solution.py:20
  243.1 3.4 %collective-permute-start.8 = (f32[16,512]{1,0:T(8,128)S(1)}, f32[16,512]{1,0:T(8,128)S(1)}, u32[]{:S(2)}, u32[]{:S(2)}) collective-permute-start(f32[16,512]{1,0:T(8,128)S(1)} %get-tuple-element.77), channel_id=1, source_target_pairs={{0,6},{2,4},{4,2},{6,0},{1,7},{3,5},{5,3},{7,1},{8,14},{10,12},{12... | collective-permute-start | bytes 98312 | tf_op jit(solution)/shard_map/ppermute | solution.py:20
  248.2 1.9 collective-permute-start.35
  253.3 3.5 %collective-permute-done.41.refs_6_ = f32[3,64,128]{2,1,0:T(8,128)S(1)} collective-permute-done((f32[3,64,128]{2,1,0:T(8,128)S(1)}, f32[3,64,128]{2,1,0:T(8,128)S(1)}, u32[]{:S(2)}, u32[]{:S(2)}) %collective-permute-start.41) | collective-permute-done | bytes 98336 | tf_op jit(solution)/shard_map/ppermute | solution.py:20
  256.8 8.4 %collective-permute-done.36.refs_2_ = f32[4,64,128]{2,1,0:T(8,128)S(1)} collective-permute-done((f32[4,64,128]{2,1,0:T(8,128)S(1)}, f32[4,64,128]{2,1,0:T(8,128)S(1)}, u32[]{:S(2)}, u32[]{:S(2)}) %collective-permute-start.36) | collective-permute-done | bytes 131104 | tf_op jit(solution)/shard_map/ppermute | solution.py:20
  265.2 2.2 shard_map.67
  (126 shorter events, 44.9 us)
Async XLA Ops:
  5.7 64.8 %collective-permute-start.21 = (f32[8,128,128]{2,1,0:T(8,128)}, f32[8,128,128]{2,1,0:T(8,128)S(1)}, u32[]{:S(2)}, u32[]{:S(2)}) collective-permute-start(f32[8,128,128]{2,1,0:T(8,128)} %get-tuple-element.48), channel_id=1, source_target_pairs={{0,2},{2,0},{4,6},{6,4},{1,3},{3,1},{5,7},{7,5},{8,10},{10,8},{12,... | collective-permute-start | bytes 1572872 | tf_op jit(solution)/shard_map/ppermute | solution.py:20
  8.8 63.9 %collective-permute-start.22 = (f32[8,128,128]{2,1,0:T(8,128)}, f32[8,128,128]{2,1,0:T(8,128)S(1)}, u32[]{:S(2)}, u32[]{:S(2)}) collective-permute-start(f32[8,128,128]{2,1,0:T(8,128)} %get-tuple-element.49), channel_id=1, source_target_pairs={{0,4},{2,6},{4,0},{6,2},{1,5},{3,7},{5,1},{7,3},{8,12},{10,14},{12... | collective-permute-start | bytes 1572872 | tf_op jit(solution)/shard_map/ppermute | solution.py:20
  11.4 63.2 %collective-permute-start.23 = (f32[8,128,128]{2,1,0:T(8,128)}, f32[8,128,128]{2,1,0:T(8,128)S(1)}, u32[]{:S(2)}, u32[]{:S(2)}) collective-permute-start(f32[8,128,128]{2,1,0:T(8,128)} %get-tuple-element.50), channel_id=1, source_target_pairs={{0,6},{2,4},{4,2},{6,0},{1,7},{3,5},{5,3},{7,1},{8,14},{10,12},{12... | collective-permute-start | bytes 1572872 | tf_op jit(solution)/shard_map/ppermute | solution.py:20
  11.4 32.4 %collective-permute-start.12 = (f32[32,256]{1,0:T(8,128)S(1)}, f32[32,256]{1,0:T(8,128)S(1)}, u32[]{:S(2)}, u32[]{:S(2)}) collective-permute-start(f32[32,256]{1,0:T(8,128)S(1)} %dynamic-slice_bitcast_fusion.16), channel_id=1, source_target_pairs={{0,2},{2,0},{4,6},{6,4},{1,3},{3,1},{5,7},{7,5},{8,10},{10,8},{12,... | collective-permute-start | bytes 98312 | tf_op jit(solution)/shard_map/ppermute | solution.py:20
  12.3 47.2 %collective-permute-start.13 = (f32[32,256]{1,0:T(8,128)S(1)}, f32[32,256]{1,0:T(8,128)S(1)}, u32[]{:S(2)}, u32[]{:S(2)}) collective-permute-start(f32[32,256]{1,0:T(8,128)S(1)} %dynamic-slice_bitcast_fusion.16), channel_id=1, source_target_pairs={{0,4},{2,6},{4,0},{6,2},{1,5},{3,7},{5,1},{7,3},{8,12},{10,14},{12... | collective-permute-start | bytes 98312 | tf_op jit(solution)/shard_map/ppermute | solution.py:20
  43.8 15.7 %collective-permute-start.14 = (f32[32,256]{1,0:T(8,128)S(1)}, f32[32,256]{1,0:T(8,128)S(1)}, u32[]{:S(2)}, u32[]{:S(2)}) collective-permute-start(f32[32,256]{1,0:T(8,128)S(1)} %dynamic-slice_bitcast_fusion.16), channel_id=1, source_target_pairs={{0,6},{2,4},{4,2},{6,0},{1,7},{3,5},{5,3},{7,1},{8,14},{10,12},{12... | collective-permute-start | bytes 98312 | tf_op jit(solution)/shard_map/ppermute | solution.py:20
  67.4 19.7 %collective-permute-start.18 = (f32[6,128,128]{2,1,0:T(8,128)}, f32[6,128,128]{2,1,0:T(8,128)}, u32[]{:S(2)}, u32[]{:S(2)}) collective-permute-start(f32[6,128,128]{2,1,0:T(8,128)} %get-tuple-element.44), channel_id=1, source_target_pairs={{0,2},{2,0},{4,6},{6,4},{1,3},{3,1},{5,7},{7,5},{8,10},{10,8},{12,... | collective-permute-start | bytes 1179656 | tf_op jit(solution)/shard_map/ppermute | solution.py:20
  68.4 35.8 %collective-permute-start.19 = (f32[6,128,128]{2,1,0:T(8,128)}, f32[6,128,128]{2,1,0:T(8,128)}, u32[]{:S(2)}, u32[]{:S(2)}) collective-permute-start(f32[6,128,128]{2,1,0:T(8,128)} %get-tuple-element.45), channel_id=1, source_target_pairs={{0,4},{2,6},{4,0},{6,2},{1,5},{3,7},{5,1},{7,3},{8,12},{10,14},{12... | collective-permute-start | bytes 1179656 | tf_op jit(solution)/shard_map/ppermute | solution.py:20
  70.5 33.6 %collective-permute-start.20 = (f32[6,128,128]{2,1,0:T(8,128)}, f32[6,128,128]{2,1,0:T(8,128)}, u32[]{:S(2)}, u32[]{:S(2)}) collective-permute-start(f32[6,128,128]{2,1,0:T(8,128)} %get-tuple-element.46), channel_id=1, source_target_pairs={{0,6},{2,4},{4,2},{6,0},{1,7},{3,5},{5,3},{7,1},{8,14},{10,12},{12... | collective-permute-start | bytes 1179656 | tf_op jit(solution)/shard_map/ppermute | solution.py:20
  73.5 41.8 %collective-permute-start.10 = (f32[2,128,128]{2,1,0:T(8,128)}, f32[2,128,128]{2,1,0:T(8,128)S(1)}, u32[]{:S(2)}, u32[]{:S(2)}) collective-permute-start(f32[2,128,128]{2,1,0:T(8,128)} %get-tuple-element.39), channel_id=1, source_target_pairs={{0,4},{2,6},{4,0},{6,2},{1,5},{3,7},{5,1},{7,3},{8,12},{10,14},{12... | collective-permute-start | bytes 393224 | tf_op jit(solution)/shard_map/ppermute | solution.py:20
  75.4 39.9 %collective-permute-start.11 = (f32[2,128,128]{2,1,0:T(8,128)}, f32[2,128,128]{2,1,0:T(8,128)S(1)}, u32[]{:S(2)}, u32[]{:S(2)}) collective-permute-start(f32[2,128,128]{2,1,0:T(8,128)} %get-tuple-element.40), channel_id=1, source_target_pairs={{0,6},{2,4},{4,2},{6,0},{1,7},{3,5},{5,3},{7,1},{8,14},{10,12},{12... | collective-permute-start | bytes 393224 | tf_op jit(solution)/shard_map/ppermute | solution.py:20
  87.1 28.2 %collective-permute-start.9 = (f32[2,128,128]{2,1,0:T(8,128)S(1)}, f32[2,128,128]{2,1,0:T(8,128)S(1)}, u32[]{:S(2)}, u32[]{:S(2)}) collective-permute-start(f32[2,128,128]{2,1,0:T(8,128)S(1)} %copy-done.13), channel_id=1, source_target_pairs={{0,2},{2,0},{4,6},{6,4},{1,3},{3,1},{5,7},{7,5},{8,10},{10,8},{12,... | collective-permute-start | bytes 393224 | tf_op jit(solution)/shard_map/ppermute | solution.py:20
  118.2 11.1 %collective-permute-start.24 = (f32[4,64,512]{2,1,0:T(8,128)}, f32[4,64,512]{2,1,0:T(8,128)}, u32[]{:S(2)}, u32[]{:S(2)}) collective-permute-start(f32[4,64,512]{2,1,0:T(8,128)} %get-tuple-element.54), channel_id=1, source_target_pairs={{0,8},{8,0},{16,24},{24,16},{1,9},{9,1},{17,25},{25,17},{2,10},{10... | collective-permute-start | bytes 1572872 | tf_op jit(solution)/shard_map/ppermute | solution.py:20
  125.6 57.9 %collective-permute-start = (f32[16,128,128]{2,1,0:T(8,128)}, f32[16,128,128]{2,1,0:T(8,128)}, u32[]{:S(2)}, u32[]{:S(2)}) collective-permute-start(f32[16,128,128]{2,1,0:T(8,128)} %get-tuple-element.32), channel_id=1, source_target_pairs={{0,8},{8,0},{16,24},{24,16},{1,9},{9,1},{17,25},{25,17},{2,10},{10... | collective-permute-start | bytes 3145736 | tf_op jit(solution)/shard_map/ppermute | solution.py:20
  125.7 61.2 %collective-permute-start.1 = (f32[16,128,128]{2,1,0:T(8,128)}, f32[16,128,128]{2,1,0:T(8,128)}, u32[]{:S(2)}, u32[]{:S(2)}) collective-permute-start(f32[16,128,128]{2,1,0:T(8,128)} %get-tuple-element.33), channel_id=1, source_target_pairs={{0,16},{8,24},{16,0},{24,8},{1,17},{9,25},{17,1},{25,9},{2,18},{10... | collective-permute-start | bytes 3145736 | tf_op jit(solution)/shard_map/ppermute | solution.py:20
  126.5 61.4 %collective-permute-start.2 = (f32[16,128,128]{2,1,0:T(8,128)}, f32[16,128,128]{2,1,0:T(8,128)}, u32[]{:S(2)}, u32[]{:S(2)}) collective-permute-start(f32[16,128,128]{2,1,0:T(8,128)} %get-tuple-element.34), channel_id=1, source_target_pairs={{0,24},{8,16},{16,8},{24,0},{1,25},{9,17},{17,9},{25,1},{2,26},{10... | collective-permute-start | bytes 3145736 | tf_op jit(solution)/shard_map/ppermute | solution.py:20
  128.4 48.9 %collective-permute-start.44 = (f32[1,4,1,64,128]{4,3,2,1,0:T(8,128)S(1)}, f32[1,4,1,64,128]{4,3,2,1,0:T(8,128)}, u32[]{:S(2)}, u32[]{:S(2)}) collective-permute-start(f32[1,4,1,64,128]{4,3,2,1,0:T(8,128)S(1)} %slice_add_fusion.4), channel_id=1, source_target_pairs={{0,16},{8,24},{16,0},{24,8},{1,17},{9,25},{17,1},{25,9},{2,18},{10... | collective-permute-start | bytes 393224 | tf_op jit(solution)/shard_map/ppermute | solution.py:20
  131.0 51.4 %collective-permute-start.25 = (f32[4,32,512]{2,1,0:T(8,128)}, f32[4,32,512]{2,1,0:T(8,128)}, u32[]{:S(2)}, u32[]{:S(2)}) collective-permute-start(f32[4,32,512]{2,1,0:T(8,128)} %fusion.2), channel_id=1, source_target_pairs={{0,16},{8,24},{16,0},{24,8},{1,17},{9,25},{17,1},{25,9},{2,18},{10... | collective-permute-start | bytes 786440 | tf_op jit(solution)/shard_map/ppermute | solution.py:20
  177.3 26.8 %collective-permute-start.38 = (f32[2,4,3,64,128]{4,3,2,1,0:T(8,128)S(1)}, f32[2,4,3,64,128]{4,3,2,1,0:T(8,128)S(1)}, u32[]{:S(2)}, u32[]{:S(2)}) collective-permute-start(f32[2,4,3,64,128]{4,3,2,1,0:T(8,128)S(1)} %get-tuple-element.58), channel_id=1, source_target_pairs={{0,8},{8,0},{16,24},{24,16},{1,9},{9,1},{17,25},{25,17},{2,10},{10... | collective-permute-start | bytes 2359304 | tf_op jit(solution)/shard_map/ppermute | solution.py:20
  182.4 31.0 %collective-permute-start.33 = (f32[2,4,4,64,128]{4,3,2,1,0:T(8,128)}, f32[2,4,4,64,128]{4,3,2,1,0:T(8,128)S(1)}, u32[]{:S(2)}, u32[]{:S(2)}) collective-permute-start(f32[2,4,4,64,128]{4,3,2,1,0:T(8,128)} %copy-done.4), channel_id=1, source_target_pairs={{0,8},{8,0},{16,24},{24,16},{1,9},{9,1},{17,25},{25,17},{2,10},{10... | collective-permute-start | bytes 3145736 | tf_op jit(solution)/shard_map/ppermute | solution.py:20
  183.5 14.9 %collective-permute-start.26 = (f32[32,512]{1,0:T(8,128)S(1)}, f32[32,512]{1,0:T(8,128)S(1)}, u32[]{:S(2)}, u32[]{:S(2)}) collective-permute-start(f32[32,512]{1,0:T(8,128)S(1)} %get-tuple-element.69), channel_id=1, source_target_pairs={{0,2},{2,0},{4,6},{6,4},{1,3},{3,1},{5,7},{7,5},{8,10},{10,8},{12,... | collective-permute-start | bytes 196616 | tf_op jit(solution)/shard_map/ppermute | solution.py:20
  186.8 11.7 %collective-permute-start.27 = (f32[32,512]{1,0:T(8,128)S(1)}, f32[32,512]{1,0:T(8,128)S(1)}, u32[]{:S(2)}, u32[]{:S(2)}) collective-permute-start(f32[32,512]{1,0:T(8,128)S(1)} %get-tuple-element.71), channel_id=1, source_target_pairs={{0,4},{2,6},{4,0},{6,2},{1,5},{3,7},{5,1},{7,3},{8,12},{10,14},{12... | collective-permute-start | bytes 196616 | tf_op jit(solution)/shard_map/ppermute | solution.py:20
  198.5 14.4 %collective-permute-start.3 = (f32[2,128,512]{2,1,0:T(8,128)S(1)}, f32[2,128,512]{2,1,0:T(8,128)S(1)}, u32[]{:S(2)}, u32[]{:S(2)}) collective-permute-start(f32[2,128,512]{2,1,0:T(8,128)S(1)} %get-tuple-element.36), channel_id=1, source_target_pairs={{0,8},{8,0},{16,24},{24,16},{1,9},{9,1},{17,25},{25,17},{2,10},{10... | collective-permute-start | bytes 1572872 | tf_op jit(solution)/shard_map/ppermute | solution.py:20
  205.1 37.0 %collective-permute-start.45 = (f32[1,64,128]{2,1,0:T(8,128)S(1)}, f32[1,64,128]{2,1,0:T(8,128)S(1)}, u32[]{:S(2)}, u32[]{:S(2)}) collective-permute-start(f32[1,64,128]{2,1,0:T(8,128)S(1)} %get-tuple-element.74), channel_id=1, source_target_pairs={{0,2},{2,0},{4,6},{6,4},{1,3},{3,1},{5,7},{7,5},{8,10},{10,8},{12,... | collective-permute-start | bytes 98312 | tf_op jit(solution)/shard_map/ppermute | solution.py:20
  208.3 34.9 %collective-permute-start.46 = (f32[1,64,128]{2,1,0:T(8,128)S(1)}, f32[1,64,128]{2,1,0:T(8,128)S(1)}, u32[]{:S(2)}, u32[]{:S(2)}) collective-permute-start(f32[1,64,128]{2,1,0:T(8,128)S(1)} %get-tuple-element.73), channel_id=1, source_target_pairs={{0,4},{2,6},{4,0},{6,2},{1,5},{3,7},{5,1},{7,3},{8,12},{10,14},{12... | collective-permute-start | bytes 98312 | tf_op jit(solution)/shard_map/ppermute | solution.py:20
  210.2 36.4 %collective-permute-start.47 = (f32[1,64,128]{2,1,0:T(8,128)S(1)}, f32[1,64,128]{2,1,0:T(8,128)S(1)}, u32[]{:S(2)}, u32[]{:S(2)}) collective-permute-start(f32[1,64,128]{2,1,0:T(8,128)S(1)} %get-tuple-element.72), channel_id=1, source_target_pairs={{0,6},{2,4},{4,2},{6,0},{1,7},{3,5},{5,3},{7,1},{8,14},{10,12},{12... | collective-permute-start | bytes 98312 | tf_op jit(solution)/shard_map/ppermute | solution.py:20
  212.9 17.3 %collective-permute-start.39 = (f32[1,4,3,64,128]{4,3,2,1,0:T(8,128)S(1)}, f32[1,4,3,64,128]{4,3,2,1,0:T(8,128)S(1)}, u32[]{:S(2)}, u32[]{:S(2)}) collective-permute-start(f32[1,4,3,64,128]{4,3,2,1,0:T(8,128)S(1)} %slice_add_fusion.2), channel_id=1, source_target_pairs={{0,16},{8,24},{16,0},{24,8},{1,17},{9,25},{17,1},{25,9},{2,18},{10... | collective-permute-start | bytes 1179656 | tf_op jit(solution)/shard_map/ppermute | solution.py:20
  213.4 15.8 %collective-permute-start.4 = (f32[1,128,512]{2,1,0:T(8,128)S(1)}, f32[1,128,512]{2,1,0:T(8,128)S(1)}, u32[]{:S(2)}, u32[]{:S(2)}) collective-permute-start(f32[1,128,512]{2,1,0:T(8,128)S(1)} %dynamic-slice_add_fusion), channel_id=1, source_target_pairs={{0,16},{8,24},{16,0},{24,8},{1,17},{9,25},{17,1},{25,9},{2,18},{10... | collective-permute-start | bytes 786440 | tf_op jit(solution)/shard_map/ppermute | solution.py:20
  229.2 12.7 %collective-permute-start.34 = (f32[1,4,4,64,128]{4,3,2,1,0:T(8,128)S(1)}, f32[1,4,4,64,128]{4,3,2,1,0:T(8,128)S(1)}, u32[]{:S(2)}, u32[]{:S(2)}) collective-permute-start(f32[1,4,4,64,128]{4,3,2,1,0:T(8,128)S(1)} %slice_add_fusion), channel_id=1, source_target_pairs={{0,16},{8,24},{16,0},{24,8},{1,17},{9,25},{17,1},{25,9},{2,18},{10... | collective-permute-start | bytes 1572872 | tf_op jit(solution)/shard_map/ppermute | solution.py:20
  235.2 11.5 %collective-permute-start.40 = (f32[3,64,128]{2,1,0:T(8,128)S(1)}, f32[3,64,128]{2,1,0:T(8,128)S(1)}, u32[]{:S(2)}, u32[]{:S(2)}) collective-permute-start(f32[3,64,128]{2,1,0:T(8,128)S(1)} %get-tuple-element.67), channel_id=1, source_target_pairs={{0,2},{2,0},{4,6},{6,4},{1,3},{3,1},{5,7},{7,5},{8,10},{10,8},{12,... | collective-permute-start | bytes 294920 | tf_op jit(solution)/shard_map/ppermute | solution.py:20
  250.2 15.0 %collective-permute-start.36 = (f32[4,64,128]{2,1,0:T(8,128)S(1)}, f32[4,64,128]{2,1,0:T(8,128)S(1)}, u32[]{:S(2)}, u32[]{:S(2)}) collective-permute-start(f32[4,64,128]{2,1,0:T(8,128)S(1)} %get-tuple-element.62), channel_id=1, source_target_pairs={{0,4},{2,6},{4,0},{6,2},{1,5},{3,7},{5,1},{7,3},{8,12},{10,14},{12... | collective-permute-start | bytes 393224 | tf_op jit(solution)/shard_map/ppermute | solution.py:20
  251.2 14.0 %collective-permute-start.37 = (f32[4,64,128]{2,1,0:T(8,128)S(1)}, f32[4,64,128]{2,1,0:T(8,128)S(1)}, u32[]{:S(2)}, u32[]{:S(2)}) collective-permute-start(f32[4,64,128]{2,1,0:T(8,128)S(1)} %get-tuple-element.61), channel_id=1, source_target_pairs={{0,6},{2,4},{4,2},{6,0},{1,7},{3,5},{5,3},{7,1},{8,14},{10,12},{12... | collective-permute-start | bytes 393224 | tf_op jit(solution)/shard_map/ppermute | solution.py:20
  (30 other events, 284.9 us)

commit v4 on v3

--- a/solution.py
+++ b/solution.py
@@ -1,4 +1,5 @@
 import functools
+import math
 
 import jax
 import jax.numpy as jnp
@@ -20,6 +21,10 @@
     return lax.ppermute(value, axis, [(i, i ^ offset) for i in range(size)])
 
 
+def early_shift(size):
+    return size // 2
+
+
 def pick(value, index, axis):
     return lax.dynamic_index_in_dim(value, index, axis, keepdims=False)
 
@@ -40,10 +45,10 @@
     return pltpu.CompilerParams(vmem_limit_bytes=24 << 20)
 
 
-def chunk_sizes(own):
-    sizes = (own // 2, own // 2 - max(2, own // 8), max(2, own // 8))
+def piece_sizes(own):
+    sizes = (own // 4,) * 4
     assert all(n > 0 and n % 2 == 0 for n in sizes)
-    return sizes
+    return sizes, ((0, 1), (2,), (3,))
 
 
 def whole_spec(shape):
@@ -57,16 +62,18 @@
 
 
 def cut(where, flat, pieces):
-    block = (2,) + flat.shape[1:]
-    steps = max(size for *_, size in pieces) // 2
+    unit = math.gcd(4, *[n for _, _, *counts in pieces for n in counts])
+    block = (unit,) + flat.shape[1:]
+    steps = max(size for *_, size in pieces) // unit
     in_specs, out_specs, out_shape = [], [], []
     for axis, k, own, start, size in pieces:
 
         def source(i, s, axis=axis, k=k, own=own, start=start, size=size):
-            return (((s[axis] ^ k) * own + start) // 2 + jnp.minimum(i, size // 2 - 1), 0, 0)
+            first = ((s[axis] ^ k) * own + start) // unit
+            return (first + jnp.minimum(i, size // unit - 1), 0, 0)
 
         def target(i, s, size=size):
-            return (jnp.minimum(i, size // 2 - 1), 0, 0)
+            return (jnp.minimum(i, size // unit - 1), 0, 0)
 
         in_specs.append(pl.BlockSpec(block, source))
         out_specs.append(pl.BlockSpec(block, target))
@@ -142,9 +149,9 @@
     )(where, factor_y, *pieces)
 
 
-def chunk_kernel(sizes, first, last, s_ref, *refs):
+def chunk_kernel(sizes, count, first, last, s_ref, *refs):
     nx, ny, _ = sizes
-    fields, refs = refs[:ny], refs[ny:]
+    fields, refs = refs[: count * ny], refs[count * ny :]
     (fyh_ref, fyl_ref, fxt_ref), refs = refs[:3], refs[3:]
     if not first:
         gin_ref, refs = refs[0], refs[1:]
@@ -153,11 +160,17 @@
         gkeep_ref, gsent_ref, wide_ref, gram_ref = refs
     else:
         gram_ref, wide_ref = refs
-    n, x_local, y_local = fields[0].shape
+    _, x_local, y_local = fields[0].shape
     me_x, me_y = s_ref[0], s_ref[1]
+    n = wide_ref.shape[0] // x_local
     for k in range(ny):
         start = pl.multiple_of((me_y ^ k) * y_local, y_local)
-        wide_ref[:, pl.ds(start, y_local)] = fields[k][...].reshape(n * x_local, y_local)
+        row = 0
+        for p in range(count):
+            part = fields[p * ny + k]
+            rows = part.shape[0] * x_local
+            wide_ref[row : row + rows, pl.ds(start, y_local)] = part[...].reshape(rows, y_local)
+            row += rows
     wide = split(wide_ref[...])
     gram = dot3(wide, wide, ROWS)
     gram_ref[...] = gram if first else gin_ref[...] + gram
@@ -201,14 +214,15 @@
 
 def chunk_terms(sizes, where, parts, fy, fxt, gram, last):
     nx, ny, _ = sizes
-    n, x_local, y_local = parts[0].shape
+    _, x_local, y_local = parts[0].shape
+    count = len(parts) // ny
+    n = sum(part.shape[0] for part in parts[::ny])
     rank = fxt.shape[0]
     pairs = n // 2
     width = ny * y_local
     a_block, b_block = rank // nx, rank // ny
     half = (nx // 2, ny, pairs, a_block, 2 * b_block)
-    field = (n, x_local, y_local)
-    specs = [whole_spec(field)] * ny
+    specs = [whole_spec(part.shape) for part in parts]
     specs += [whole_spec(fy[0].shape)] * 2 + [whole_spec(fxt.shape)]
     args = [*parts, *fy, fxt]
     first = gram is None
@@ -228,7 +242,7 @@
         out_shape.append(jax.ShapeDtypeStruct((width, width), F32))
     flops = 2 * n * x_local * (width * width + width * rank + rank * rank) * 3
     return pl.pallas_call(
-        functools.partial(chunk_kernel, sizes, first, last),
+        functools.partial(chunk_kernel, sizes, count, first, last),
         grid_spec=pltpu.PrefetchScalarGridSpec(
             num_scalar_prefetch=1,
             grid=(1,),
@@ -338,13 +352,16 @@
     rows = z_cells * s_local
     flat = slab.reshape((rows, x_local, y_local))
     own_y, own_x = rows // ny, rows // nx
-    counts = chunk_sizes(own_y)
+    counts, chunks = piece_sizes(own_y)
     starts = [sum(counts[:c]) for c in range(len(counts))]
     x_total, y_total, s_total = x_local * nx, y_local * ny, s_local * ns
 
     keys = [[(1, k, own_y, starts[c], counts[c]) for k in range(ny)] for c in range(len(counts))]
     x_keys = [(0, k, own_x, 0, own_x) for k in range(1, nx)]
-    groups = [keys[0][1:], x_keys, [keys[0][0]] + sum(keys[1:], [])]
+    own_keys = [key[0] for key in keys]
+    early = early_shift(nx)
+    groups = [keys[0][1:], [x_keys[early - 1]], keys[1][1:] + own_keys[:2]]
+    groups += [keys[2] + keys[3], [key for key in x_keys if key[1] != early]]
     pieces = {}
     for group in groups:
         pieces.update(zip(group, cut(where, flat, group)))
@@ -362,9 +379,10 @@
 
     gram = None
     core_parts = []
-    for c in range(len(counts)):
-        last = c == len(counts) - 1
-        out = chunk_terms(sizes, where, along_y[c], fy, fxt, gram, last)
+    for c, members in enumerate(chunks):
+        last = c == len(chunks) - 1
+        parts = sum((along_y[p] for p in members), [])
+        out = chunk_terms(sizes, where, parts, fy, fxt, gram, last)
         keep, sent, gram = out[0], out[1], out[2:]
         if last:
             gkeep, gsent = gram
@@ -382,7 +400,7 @@
         keep = keep[0]
         z_parts = [pick(keep, me_y ^ k, 0) for k in range(ny)]
         core_parts += [swap(z_parts[k], "gy", k) if k else z_parts[0] for k in range(ny)]
-    core = unpack(sizes, where, core_parts, starts, rows)
+    core = unpack(sizes, where, core_parts, [starts[m[0]] for m in chunks], rows)
     core = core.reshape((z_cells, s_local, a_block, b_block))
 
     keep, sent = gram_x_terms(sizes, where, flat, along_x)

time: 268 us -> 246 us (0.918)
  waiting for transfers between devices: 155 us -> 119 us
  starting transfers between devices: 55.4 us -> 72.2 us
  local copies, waits for them, and re-layouts: 8.22 us -> 3.46 us
    ppermute x48 -> x51, waiting for transfers between devices: 155 us -> 119 us  [swap(): return lax.ppermute(value, axis, [(i, i ^ offset) for i in range(size)])]
    ppermute x48 -> x51, starting transfers between devices: 55.4 us -> 72.2 us  [swap(): return lax.ppermute(value, axis, [(i, i ^ offset) for i in range(size)])]
    unnamed x29 -> x23, local copies, waits for them, and re-layouts: 8.07 us -> 3.3 us
    pallas_call x3 -> x5, Pallas kernels: 16.6 us -> 18.2 us  [cut(): pl.pallas_call(cut_kernel, grid_spec=pltpu.PrefetchScalarGridSpec(num_sca...]
  transfers between devices with their start and end apart: 48 -> 51, of which waited for: 14 -> 13; matrix products, arithmetic and copies ran while one was open for 2% -> 3% of each run, Pallas kernels for 12% -> 14%
where the time goes in v4:
time: 246 us; the launch traced here: 245 us
  waiting for transfers between devices  119 us (48%)
  starting transfers between devices  72.2 us (29%)
  Pallas kernels  41.2 us (17%)
  other arithmetic  7.65 us (3%)
  local copies, waits for them, and re-layouts  3.46 us (1%)
    ppermute x51, waiting for transfers between devices, swap(): return lax.ppermute(value, axis, [(i, i ^ offset) for i in range(size)])  119 us
    ppermute x51, starting transfers between devices, swap(): return lax.ppermute(value, axis, [(i, i ^ offset) for i in range(size)])  72.2 us
    pallas_call x5, Pallas kernels, cut(): pl.pallas_call(cut_kernel, grid_spec=pltpu.PrefetchScalarGridSpec(num_sca...  18.2 us
    pallas_call x3, Pallas kernels, chunk_terms(): pl.pallas_call(functools.partial(chunk_kernel, sizes, count, first, last)...  12.2 us
    pallas_call x1, Pallas kernels, gram_x_terms(): pl.pallas_call(functools.partial(gram_x_kernel, sizes), grid_spec=pltpu.P...  6.71 us
  transfers between devices with their start and end apart: 51, of which 13 were waited for; matrix products, arithmetic and copies ran while one was open for 3% of the time, Pallas kernels for 14%

profile of v4, /device:TPU:0, one launch (start us, length us, event | category | flops | bytes accessed | tf_op | source)
XLA Modules:
  0.0 244.7 jit_solution(9677973957622702431)
XLA Ops:
  1.3 2.8 %shard_map.64 = (f32[4,128,128]{2,1,0:T(8,128)}, f32[4,128,128]{2,1,0:T(8,128)}, f32[4,128,128]{2,1,0:T(8,128)}) custom-call(s32[3]{0:T(128)} %pad_add_fusion.s_ref, f32[64,128,128]{2,1,0:T(8,128)} %bitcast.89, f32[64,128,128]{2,1,0:T(8,128)} %bitcast.90, f32[64,128,128]{2,1,0:T(8,128)} %bitcast.91), custom_call_target="tpu_custom_call" | custom-call | flops 1000 | bytes 4194304 | tf_op jit(solution)/shard_map/pallas_call | solution.py:81
  4.1 3.1 %collective-permute-start.21 = (f32[4,128,128]{2,1,0:T(8,128)}, f32[4,128,128]{2,1,0:T(8,128)S(1)}, u32[]{:S(2)}, u32[]{:S(2)}) collective-permute-start(f32[4,128,128]{2,1,0:T(8,128)} %get-tuple-element.50), channel_id=1, source_target_pairs={{0,2},{2,0},{4,6},{6,4},{1,3},{3,1},{5,7},{7,5},{8,10},{10,8},{12,... | collective-permute-start | bytes 786440 | tf_op jit(solution)/shard_map/ppermute | solution.py:21
  7.2 2.6 %collective-permute-start.22 = (f32[4,128,128]{2,1,0:T(8,128)}, f32[4,128,128]{2,1,0:T(8,128)S(1)}, u32[]{:S(2)}, u32[]{:S(2)}) collective-permute-start(f32[4,128,128]{2,1,0:T(8,128)} %get-tuple-element.51), channel_id=1, source_target_pairs={{0,4},{2,6},{4,0},{6,2},{1,5},{3,7},{5,1},{7,3},{8,12},{10,14},{12... | collective-permute-start | bytes 786440 | tf_op jit(solution)/shard_map/ppermute | solution.py:21
  11.7 2.5 %collective-permute-start.12 = (f32[32,256]{1,0:T(8,128)S(1)}, f32[32,256]{1,0:T(8,128)S(1)}, u32[]{:S(2)}, u32[]{:S(2)}) collective-permute-start(f32[32,256]{1,0:T(8,128)S(1)} %dynamic-slice_bitcast_fusion.16), channel_id=1, source_target_pairs={{0,2},{2,0},{4,6},{6,4},{1,3},{3,1},{5,7},{7,5},{8,10},{10,8},{12,... | collective-permute-start | bytes 98312 | tf_op jit(solution)/shard_map/ppermute | solution.py:21
  14.1 8.8 %collective-permute-done.14 = f32[32,256]{1,0:T(8,128)S(1)} collective-permute-done((f32[32,256]{1,0:T(8,128)S(1)}, f32[32,256]{1,0:T(8,128)S(1)}, u32[]{:S(2)}, u32[]{:S(2)}) %collective-permute-start.14) | collective-permute-done | bytes 32800 | tf_op jit(solution)/shard_map/ppermute | solution.py:21
  26.4 3.0 %shard_map.63 = (f32[4,128,128]{2,1,0:T(8,128)}, f32[4,128,128]{2,1,0:T(8,128)}, f32[4,128,128]{2,1,0:T(8,128)}, f32[4,128,128]{2,1,0:T(8,128)}, f32[4,128,128]{2,1,0:T(8,128)}) custom-call(s32[3]{0:T(128)} %pad_add_fusion.s_ref, f32[64,128,128]{2,1,0:T(8,128)} %bitcast.92, f32[64,128,128]{2,1,0:T(8,128)} %bitcast.93, f32[64,128,128]{2,1,0:T(8,128)} %bitcast.94, ...), custom_call_target="tpu_custom_call" | custom-call | flops 1000 | bytes 4194304 | tf_op jit(solution)/shard_map/pallas_call | solution.py:81
  29.5 3.7 %shard_map.61 = (f32[4,128,128]{2,1,0:T(8,128)}, f32[4,128,128]{2,1,0:T(8,128)}, f32[4,128,128]{2,1,0:T(8,128)}, f32[4,128,128]{2,1,0:T(8,128)}, f32[4,128,128]{...) custom-call(s32[3]{0:T(128)} %pad_add_fusion.s_ref, ...), custom_call_target="tpu_custom_call" | custom-call | flops 1000 | bytes 4194304 | tf_op jit(solution)/shard_map/pallas_call | solution.py:81
  33.2 2.5 %collective-permute-start.23 = (f32[4,128,128]{2,1,0:T(8,128)S(1)}, f32[4,128,128]{2,1,0:T(8,128)S(1)}, u32[]{:S(2)}, u32[]{:S(2)}) collective-permute-start(f32[4,128,128]{2,1,0:T(8,128)S(1)} %copy-done.10), channel_id=1, source_target_pairs={{0,6},{2,4},{4,2},{6,0},{1,7},{3,5},{5,3},{7,1},{8,14},{10,12},{12... | collective-permute-start | bytes 786440 | tf_op jit(solution)/shard_map/ppermute | solution.py:21
  37.7 2.5 %collective-permute-start.26 = (f32[4,128,128]{2,1,0:T(8,128)}, f32[4,128,128]{2,1,0:T(8,128)S(1)}, u32[]{:S(2)}, u32[]{:S(2)}) collective-permute-start(f32[4,128,128]{2,1,0:T(8,128)} %get-tuple-element.56), channel_id=1, source_target_pairs={{0,6},{2,4},{4,2},{6,0},{1,7},{3,5},{5,3},{7,1},{8,14},{10,12},{12... | collective-permute-start | bytes 786440 | tf_op jit(solution)/shard_map/ppermute | solution.py:21
  41.0 3.4 %collective-permute-done.23.refs_3_ = f32[4,128,128]{2,1,0:T(8,128)S(1)} collective-permute-done((f32[4,128,128]{2,1,0:T(8,128)S(1)}, f32[4,128,128]{2,1,0:T(8,128)S(1)}, u32[]{:S(2)}, u32[]{:S(2)}) %collective-permute-start.23) | collective-permute-done | bytes 262176 | tf_op jit(solution)/shard_map/ppermute | solution.py:21
  44.3 3.9 %collective-permute-start.9 = (f32[4,128,128]{2,1,0:T(8,128)}, f32[4,128,128]{2,1,0:T(8,128)S(1)}, u32[]{:S(2)}, u32[]{:S(2)}) collective-permute-start(f32[4,128,128]{2,1,0:T(8,128)} %get-tuple-element.40), channel_id=1, source_target_pairs={{0,2},{2,0},{4,6},{6,4},{1,3},{3,1},{5,7},{7,5},{8,10},{10,8},{12,... | collective-permute-start | bytes 786440 | tf_op jit(solution)/shard_map/ppermute | solution.py:21
  48.3 3.4 %collective-permute-done.24.refs_5_ = f32[4,128,128]{2,1,0:T(8,128)S(1)} collective-permute-done((f32[4,128,128]{2,1,0:T(8,128)}, f32[4,128,128]{2,1,0:T(8,128)S(1)}, u32[]{:S(2)}, u32[]{:S(2)}) %collective-permute-start.24) | collective-permute-done | bytes 262176 | tf_op jit(solution)/shard_map/ppermute | solution.py:21
  52.2 12.5 %collective-permute-done.25.refs_6_ = f32[4,128,128]{2,1,0:T(8,128)S(1)} collective-permute-done((f32[4,128,128]{2,1,0:T(8,128)}, f32[4,128,128]{2,1,0:T(8,128)S(1)}, u32[]{:S(2)}, u32[]{:S(2)}) %collective-permute-start.25) | collective-permute-done | bytes 262176 | tf_op jit(solution)/shard_map/ppermute | solution.py:21
  64.6 2.5 %collective-permute-start.11 = (f32[4,128,128]{2,1,0:T(8,128)}, f32[4,128,128]{2,1,0:T(8,128)S(1)}, u32[]{:S(2)}, u32[]{:S(2)}) collective-permute-start(f32[4,128,128]{2,1,0:T(8,128)} %get-tuple-element.42), channel_id=1, source_target_pairs={{0,6},{2,4},{4,2},{6,0},{1,7},{3,5},{5,3},{7,1},{8,14},{10,12},{12... | collective-permute-start | bytes 786440 | tf_op jit(solution)/shard_map/ppermute | solution.py:21
  67.1 4.7 %collective-permute-start.19 = (f32[4,128,128]{2,1,0:T(8,128)}, f32[4,128,128]{2,1,0:T(8,128)S(1)}, u32[]{:S(2)}, u32[]{:S(2)}) collective-permute-start(f32[4,128,128]{2,1,0:T(8,128)} %get-tuple-element.47), channel_id=1, source_target_pairs={{0,4},{2,6},{4,0},{6,2},{1,5},{3,7},{5,1},{7,3},{8,12},{10,14},{12... | collective-permute-start | bytes 786440 | tf_op jit(solution)/shard_map/ppermute | solution.py:21
  73.2 5.1 %shard_map.65 = (f32[2,4,4,64,128]{4,3,2,1,0:T(8,128)S(1)}, f32[2,4,4,64,128]{4,3,2,1,0:T(8,128)S(1)}, f32[512,512]{1,0:T(8,128)S(1)}) custom-call(s32[3]{0:T(128)S(1)} %copy-done.2, f32[4,128,128]{2,1,0:T(8,128)S(1)} %copy-done.7, f32[4,128,128]{2,1,0:T(8,128)S(1)} %collective-permute-done.21.refs_1_, f32[4,128,128]{2,1,0:T(8,128)S(1)} %collective-permute-done.22.refs_2_, ...), custom_call_target="tpu_custom_call" | custom-call | flops 2818572288 | bytes 4194304 | tf_op jit(solution)/shard_map/pallas_call | solution.py:244
  79.3 30.3 %collective-permute-done.19.refs_2_ = f32[4,128,128]{2,1,0:T(8,128)S(1)} collective-permute-done((f32[4,128,128]{2,1,0:T(8,128)}, f32[4,128,128]{2,1,0:T(8,128)S(1)}, u32[]{:S(2)}, u32[]{:S(2)}) %collective-permute-start.19) | collective-permute-done | bytes 262176 | tf_op jit(solution)/shard_map/ppermute | solution.py:21
  109.6 3.0 %shard_map.66 = (f32[2,4,2,64,128]{4,3,2,1,0:T(8,128)S(1)}, f32[2,4,2,64,128]{4,3,2,1,0:T(8,128)S(1)}, f32[512,512]{1,0:T(8,128)S(1)}) custom-call(s32[3]{0:T(128)S(1)} %copy-done.2, f32[4,128,128]{2,1,0:T(8,128)S(1)} %copy-done.6, f32[4,128,128]{2,1,0:T(8,128)S(1)} %collective-permute-done.18.refs_1_, f32[4,128,128]{2,1,0:T(8,128)S(1)} %collective-permute-done.19.refs_2_, ...), custom_call_target="tpu_custom_call" | custom-call | flops 1409286144 | bytes 4194304 | tf_op jit(solution)/shard_map/pallas_call | solution.py:244
  112.7 4.0 %shard_map.67 = (f32[2,4,2,64,128]{4,3,2,1,0:T(8,128)S(1)}, f32[2,4,2,64,128]{4,3,2,1,0:T(8,128)}, f32[4,64,512]{2,1,0:T(8,128)S(1)}, f32[4,64,512]{2,1,0:T(8,128)}) custom-call(s32[3]{0:T(128)S(1)} %copy-done.2, f32[4,128,128]{2,1,0:T(8,128)S(1)} %copy-done.5, f32[4,128,128]{2,1,0:T(8,128)S(1)} %collective-permute-done.9.refs_1_, ...), custom_call_target="tpu_custom_call" | custom-call | flops 1409286144 | bytes 4194304 | tf_op jit(solution)/shard_map/pallas_call | solution.py:244
  117.2 4.2 %shard_map.59 = f32[16,128,128]{2,1,0:T(8,128)} custom-call(s32[3]{0:T(128)} %pad_add_fusion.s_ref, f32[64,128,128]{2,1,0:T(8,128)} %bitcast.105), custom_call_target="tpu_custom_call" | custom-call | flops 1000 | bytes 4194304 | tf_op jit(solution)/shard_map/pallas_call | solution.py:81
  122.9 4.4 %shard_map.58 = (f32[16,128,128]{2,1,0:T(8,128)}, f32[16,128,128]{2,1,0:T(8,128)}) custom-call(s32[3]{0:T(128)} %pad_add_fusion.s_ref, f32[64,128,128]{2,1,0:T(8,128)} %bitcast.106, f32[64,128,128]{2,1,0:T(8,128)} %bitcast.107), custom_call_target="tpu_custom_call" | custom-call | flops 1000 | bytes 4194304 | tf_op jit(solution)/shard_map/pallas_call | solution.py:81
  132.6 42.6 %collective-permute-done.28 = f32[4,32,512]{2,1,0:T(8,128)S(1)} collective-permute-done((f32[4,32,512]{2,1,0:T(8,128)S(1)}, f32[4,32,512]{2,1,0:T(8,128)S(1)}, u32[]{:S(2)}, u32[]{:S(2)}) %collective-permute-start.28) | collective-permute-done | bytes 262176 | tf_op jit(solution)/shard_map/ppermute | solution.py:21
  178.4 5.4 %collective-permute-start.29 = (f32[32,512]{1,0:T(8,128)S(1)}, f32[32,512]{1,0:T(8,128)S(1)}, u32[]{:S(2)}, u32[]{:S(2)}) collective-permute-start(f32[32,512]{1,0:T(8,128)S(1)} %get-tuple-element.79), channel_id=1, source_target_pairs={{0,2},{2,0},{4,6},{6,4},{1,3},{3,1},{5,7},{7,5},{8,10},{10,8},{12,... | collective-permute-start | bytes 196616 | tf_op jit(solution)/shard_map/ppermute | solution.py:21
  183.9 2.5 %collective-permute-start.31 = (f32[32,512]{1,0:T(8,128)S(1)}, f32[32,512]{1,0:T(8,128)S(1)}, u32[]{:S(2)}, u32[]{:S(2)}) collective-permute-start(f32[32,512]{1,0:T(8,128)S(1)} %get-tuple-element.80), channel_id=1, source_target_pairs={{0,6},{2,4},{4,2},{6,0},{1,7},{3,5},{5,3},{7,1},{8,14},{10,12},{12... | collective-permute-start | bytes 196616 | tf_op jit(solution)/shard_map/ppermute | solution.py:21
  186.4 2.2 copy-done
  188.5 6.7 %shard_map.60 = (f32[2,128,512]{2,1,0:T(8,128)S(1)}, f32[2,128,512]{2,1,0:T(8,128)S(1)}) custom-call(s32[3]{0:T(128)S(1)} %copy-done.3, f32[64,128,128]{2,1,0:T(8,128)S(1)} %bitcast.108, f32[16,128,128]{2,1,0:T(8,128)} %collective-permute-done.refs_1_, f32[16,128,128]{2,1,0:T(8,128)} %collective-permute-done.1.refs_2_, ...), custom_call_target="tpu_custom_call" | custom-call | flops 3221225472 | bytes 8388608 | tf_op jit(solution)/shard_map/pallas_call | solution.py:300
  199.2 1.9 collective-permute-start.49
  204.9 2.7 %collective-permute-done.32 = f32[32,512]{1,0:T(8,128)S(1)} collective-permute-done((f32[32,512]{1,0:T(8,128)S(1)}, f32[32,512]{1,0:T(8,128)S(1)}, u32[]{:S(2)}, u32[]{:S(2)}) %collective-permute-start.32) | collective-permute-done | bytes 65568 | tf_op jit(solution)/shard_map/ppermute | solution.py:21
  208.6 11.7 %collective-permute-done.4 = f32[1,128,512]{2,1,0:T(8,128)S(1)} collective-permute-done((f32[1,128,512]{2,1,0:T(8,128)S(1)}, f32[1,128,512]{2,1,0:T(8,128)S(1)}, u32[]{:S(2)}, u32[]{:S(2)}) %collective-permute-start.4) | collective-permute-done | bytes 262176 | tf_op jit(solution)/shard_map/ppermute | solution.py:21
  220.3 2.5 %collective-permute-start.45 = (f32[2,64,128]{2,1,0:T(8,128)S(1)}, f32[2,64,128]{2,1,0:T(8,128)S(1)}, u32[]{:S(2)}, u32[]{:S(2)}) collective-permute-start(f32[2,64,128]{2,1,0:T(8,128)S(1)} %get-tuple-element.75), channel_id=1, source_target_pairs={{0,6},{2,4},{4,2},{6,0},{1,7},{3,5},{5,3},{7,1},{8,14},{10,12},{12... | collective-permute-start | bytes 196616 | tf_op jit(solution)/shard_map/ppermute | solution.py:21
  236.1 4.1 %collective-permute-start.7 = (f32[16,512]{1,0:T(8,128)S(1)}, f32[16,512]{1,0:T(8,128)S(1)}, u32[]{:S(2)}, u32[]{:S(2)}) collective-permute-start(f32[16,512]{1,0:T(8,128)S(1)} %get-tuple-element.84), channel_id=1, source_target_pairs={{0,4},{2,6},{4,0},{6,2},{1,5},{3,7},{5,1},{7,3},{8,12},{10,14},{12... | collective-permute-start | bytes 98312 | tf_op jit(solution)/shard_map/ppermute | solution.py:21
  241.6 2.2 shard_map.69
  (128 shorter events, 46.3 us)
Async XLA Ops:
  4.1 33.6 %collective-permute-start.21 = (f32[4,128,128]{2,1,0:T(8,128)}, f32[4,128,128]{2,1,0:T(8,128)S(1)}, u32[]{:S(2)}, u32[]{:S(2)}) collective-permute-start(f32[4,128,128]{2,1,0:T(8,128)} %get-tuple-element.50), channel_id=1, source_target_pairs={{0,2},{2,0},{4,6},{6,4},{1,3},{3,1},{5,7},{7,5},{8,10},{10,8},{12,... | collective-permute-start | bytes 786440 | tf_op jit(solution)/shard_map/ppermute | solution.py:21
  7.2 33.0 %collective-permute-start.22 = (f32[4,128,128]{2,1,0:T(8,128)}, f32[4,128,128]{2,1,0:T(8,128)S(1)}, u32[]{:S(2)}, u32[]{:S(2)}) collective-permute-start(f32[4,128,128]{2,1,0:T(8,128)} %get-tuple-element.51), channel_id=1, source_target_pairs={{0,4},{2,6},{4,0},{6,2},{1,5},{3,7},{5,1},{7,3},{8,12},{10,14},{12... | collective-permute-start | bytes 786440 | tf_op jit(solution)/shard_map/ppermute | solution.py:21
  9.7 13.2 %collective-permute-start.14 = (f32[32,256]{1,0:T(8,128)S(1)}, f32[32,256]{1,0:T(8,128)S(1)}, u32[]{:S(2)}, u32[]{:S(2)}) collective-permute-start(f32[32,256]{1,0:T(8,128)S(1)} %dynamic-slice_bitcast_fusion.16), channel_id=1, source_target_pairs={{0,6},{2,4},{4,2},{6,0},{1,7},{3,5},{5,3},{7,1},{8,14},{10,12},{12... | collective-permute-start | bytes 98312 | tf_op jit(solution)/shard_map/ppermute | solution.py:21
  9.8 14.7 %collective-permute-start.13 = (f32[32,256]{1,0:T(8,128)S(1)}, f32[32,256]{1,0:T(8,128)S(1)}, u32[]{:S(2)}, u32[]{:S(2)}) collective-permute-start(f32[32,256]{1,0:T(8,128)S(1)} %dynamic-slice_bitcast_fusion.16), channel_id=1, source_target_pairs={{0,4},{2,6},{4,0},{6,2},{1,5},{3,7},{5,1},{7,3},{8,12},{10,14},{12... | collective-permute-start | bytes 98312 | tf_op jit(solution)/shard_map/ppermute | solution.py:21
  11.7 12.8 %collective-permute-start.12 = (f32[32,256]{1,0:T(8,128)S(1)}, f32[32,256]{1,0:T(8,128)S(1)}, u32[]{:S(2)}, u32[]{:S(2)}) collective-permute-start(f32[32,256]{1,0:T(8,128)S(1)} %dynamic-slice_bitcast_fusion.16), channel_id=1, source_target_pairs={{0,2},{2,0},{4,6},{6,4},{1,3},{3,1},{5,7},{7,5},{8,10},{10,8},{12,... | collective-permute-start | bytes 98312 | tf_op jit(solution)/shard_map/ppermute | solution.py:21
  24.6 11.1 %collective-permute-start.16 = (f32[3,32,256]{2,1,0:T(8,128)S(1)}, f32[3,32,256]{2,1,0:T(8,128)S(1)}, u32[]{:S(2)}, u32[]{:S(2)}) collective-permute-start(f32[3,32,256]{2,1,0:T(8,128)S(1)} %pad_maximum_fusion.refs_0_), channel_id=1, source_target_pairs={{0,16},{8,24},{16,0},{24,8},{1,17},{9,25},{17,1},{25,9},{2,18},{10... | collective-permute-start | bytes 294920 | tf_op jit(solution)/shard_map/ppermute | solution.py:21
  33.2 11.1 %collective-permute-start.23 = (f32[4,128,128]{2,1,0:T(8,128)S(1)}, f32[4,128,128]{2,1,0:T(8,128)S(1)}, u32[]{:S(2)}, u32[]{:S(2)}) collective-permute-start(f32[4,128,128]{2,1,0:T(8,128)S(1)} %copy-done.10), channel_id=1, source_target_pairs={{0,6},{2,4},{4,2},{6,0},{1,7},{3,5},{5,3},{7,1},{8,14},{10,12},{12... | collective-permute-start | bytes 786440 | tf_op jit(solution)/shard_map/ppermute | solution.py:21
  35.7 15.9 %collective-permute-start.24 = (f32[4,128,128]{2,1,0:T(8,128)}, f32[4,128,128]{2,1,0:T(8,128)S(1)}, u32[]{:S(2)}, u32[]{:S(2)}) collective-permute-start(f32[4,128,128]{2,1,0:T(8,128)} %get-tuple-element.54), channel_id=1, source_target_pairs={{0,2},{2,0},{4,6},{6,4},{1,3},{3,1},{5,7},{7,5},{8,10},{10,8},{12,... | collective-permute-start | bytes 786440 | tf_op jit(solution)/shard_map/ppermute | solution.py:21
  35.8 28.9 %collective-permute-start.25 = (f32[4,128,128]{2,1,0:T(8,128)}, f32[4,128,128]{2,1,0:T(8,128)S(1)}, u32[]{:S(2)}, u32[]{:S(2)}) collective-permute-start(f32[4,128,128]{2,1,0:T(8,128)} %get-tuple-element.55), channel_id=1, source_target_pairs={{0,4},{2,6},{4,0},{6,2},{1,5},{3,7},{5,1},{7,3},{8,12},{10,14},{12... | collective-permute-start | bytes 786440 | tf_op jit(solution)/shard_map/ppermute | solution.py:21
  37.7 29.4 %collective-permute-start.26 = (f32[4,128,128]{2,1,0:T(8,128)}, f32[4,128,128]{2,1,0:T(8,128)S(1)}, u32[]{:S(2)}, u32[]{:S(2)}) collective-permute-start(f32[4,128,128]{2,1,0:T(8,128)} %get-tuple-element.56), channel_id=1, source_target_pairs={{0,6},{2,4},{4,2},{6,0},{1,7},{3,5},{5,3},{7,1},{8,14},{10,12},{12... | collective-permute-start | bytes 786440 | tf_op jit(solution)/shard_map/ppermute | solution.py:21
  40.1 31.7 %collective-permute-start.18 = (f32[4,128,128]{2,1,0:T(8,128)}, f32[4,128,128]{2,1,0:T(8,128)S(1)}, u32[]{:S(2)}, u32[]{:S(2)}) collective-permute-start(f32[4,128,128]{2,1,0:T(8,128)} %get-tuple-element.46), channel_id=1, source_target_pairs={{0,2},{2,0},{4,6},{6,4},{1,3},{3,1},{5,7},{7,5},{8,10},{10,8},{12,... | collective-permute-start | bytes 786440 | tf_op jit(solution)/shard_map/ppermute | solution.py:21
  44.3 68.3 %collective-permute-start.9 = (f32[4,128,128]{2,1,0:T(8,128)}, f32[4,128,128]{2,1,0:T(8,128)S(1)}, u32[]{:S(2)}, u32[]{:S(2)}) collective-permute-start(f32[4,128,128]{2,1,0:T(8,128)} %get-tuple-element.40), channel_id=1, source_target_pairs={{0,2},{2,0},{4,6},{6,4},{1,3},{3,1},{5,7},{7,5},{8,10},{10,8},{12,... | collective-permute-start | bytes 786440 | tf_op jit(solution)/shard_map/ppermute | solution.py:21
  51.6 61.0 %collective-permute-start.10 = (f32[4,128,128]{2,1,0:T(8,128)}, f32[4,128,128]{2,1,0:T(8,128)S(1)}, u32[]{:S(2)}, u32[]{:S(2)}) collective-permute-start(f32[4,128,128]{2,1,0:T(8,128)} %get-tuple-element.41), channel_id=1, source_target_pairs={{0,4},{2,6},{4,0},{6,2},{1,5},{3,7},{5,1},{7,3},{8,12},{10,14},{12... | collective-permute-start | bytes 786440 | tf_op jit(solution)/shard_map/ppermute | solution.py:21
  64.6 48.0 %collective-permute-start.11 = (f32[4,128,128]{2,1,0:T(8,128)}, f32[4,128,128]{2,1,0:T(8,128)S(1)}, u32[]{:S(2)}, u32[]{:S(2)}) collective-permute-start(f32[4,128,128]{2,1,0:T(8,128)} %get-tuple-element.42), channel_id=1, source_target_pairs={{0,6},{2,4},{4,2},{6,0},{1,7},{3,5},{5,3},{7,1},{8,14},{10,12},{12... | collective-permute-start | bytes 786440 | tf_op jit(solution)/shard_map/ppermute | solution.py:21
  67.1 42.5 %collective-permute-start.19 = (f32[4,128,128]{2,1,0:T(8,128)}, f32[4,128,128]{2,1,0:T(8,128)S(1)}, u32[]{:S(2)}, u32[]{:S(2)}) collective-permute-start(f32[4,128,128]{2,1,0:T(8,128)} %get-tuple-element.47), channel_id=1, source_target_pairs={{0,4},{2,6},{4,0},{6,2},{1,5},{3,7},{5,1},{7,3},{8,12},{10,14},{12... | collective-permute-start | bytes 786440 | tf_op jit(solution)/shard_map/ppermute | solution.py:21
  71.8 37.7 %collective-permute-start.20 = (f32[4,128,128]{2,1,0:T(8,128)}, f32[4,128,128]{2,1,0:T(8,128)S(1)}, u32[]{:S(2)}, u32[]{:S(2)}) collective-permute-start(f32[4,128,128]{2,1,0:T(8,128)} %get-tuple-element.48), channel_id=1, source_target_pairs={{0,6},{2,4},{4,2},{6,0},{1,7},{3,5},{5,3},{7,1},{8,14},{10,12},{12... | collective-permute-start | bytes 786440 | tf_op jit(solution)/shard_map/ppermute | solution.py:21
  116.7 12.3 %collective-permute-start.46 = (f32[2,4,2,64,128]{4,3,2,1,0:T(8,128)}, f32[2,4,2,64,128]{4,3,2,1,0:T(8,128)}, u32[]{:S(2)}, u32[]{:S(2)}) collective-permute-start(f32[2,4,2,64,128]{4,3,2,1,0:T(8,128)} %get-tuple-element.66), channel_id=1, source_target_pairs={{0,8},{8,0},{16,24},{24,16},{1,9},{9,1},{17,25},{25,17},{2,10},{10... | collective-permute-start | bytes 1572872 | tf_op jit(solution)/shard_map/ppermute | solution.py:21
  117.2 14.4 %collective-permute-start.41 = (f32[2,4,2,64,128]{4,3,2,1,0:T(8,128)S(1)}, f32[2,4,2,64,128]{4,3,2,1,0:T(8,128)}, u32[]{:S(2)}, u32[]{:S(2)}) collective-permute-start(f32[2,4,2,64,128]{4,3,2,1,0:T(8,128)S(1)} %get-tuple-element.64), channel_id=1, source_target_pairs={{0,8},{8,0},{16,24},{24,16},{1,9},{9,1},{17,25},{25,17},{2,10},{10... | collective-permute-start | bytes 1572872 | tf_op jit(solution)/shard_map/ppermute | solution.py:21
  121.4 56.4 %collective-permute-start.1 = (f32[16,128,128]{2,1,0:T(8,128)}, f32[16,128,128]{2,1,0:T(8,128)}, u32[]{:S(2)}, u32[]{:S(2)}) collective-permute-start(f32[16,128,128]{2,1,0:T(8,128)} %shard_map.59), channel_id=1, source_target_pairs={{0,16},{8,24},{16,0},{24,8},{1,17},{9,25},{17,1},{25,9},{2,18},{10... | collective-permute-start | bytes 3145736 | tf_op jit(solution)/shard_map/ppermute | solution.py:21
  127.3 51.1 %collective-permute-start = (f32[16,128,128]{2,1,0:T(8,128)}, f32[16,128,128]{2,1,0:T(8,128)}, u32[]{:S(2)}, u32[]{:S(2)}) collective-permute-start(f32[16,128,128]{2,1,0:T(8,128)} %get-tuple-element.35), channel_id=1, source_target_pairs={{0,8},{8,0},{16,24},{24,16},{1,9},{9,1},{17,25},{25,17},{2,10},{10... | collective-permute-start | bytes 3145736 | tf_op jit(solution)/shard_map/ppermute | solution.py:21
  127.6 56.3 %collective-permute-start.2 = (f32[16,128,128]{2,1,0:T(8,128)}, f32[16,128,128]{2,1,0:T(8,128)}, u32[]{:S(2)}, u32[]{:S(2)}) collective-permute-start(f32[16,128,128]{2,1,0:T(8,128)} %get-tuple-element.36), channel_id=1, source_target_pairs={{0,24},{8,16},{16,8},{24,0},{1,25},{9,17},{17,9},{25,1},{2,26},{10... | collective-permute-start | bytes 3145736 | tf_op jit(solution)/shard_map/ppermute | solution.py:21
  129.0 46.3 %collective-permute-start.28 = (f32[4,32,512]{2,1,0:T(8,128)S(1)}, f32[4,32,512]{2,1,0:T(8,128)S(1)}, u32[]{:S(2)}, u32[]{:S(2)}) collective-permute-start(f32[4,32,512]{2,1,0:T(8,128)S(1)} %fusion.3), channel_id=1, source_target_pairs={{0,16},{8,24},{16,0},{24,8},{1,17},{9,25},{17,1},{25,9},{2,18},{10... | collective-permute-start | bytes 786440 | tf_op jit(solution)/shard_map/ppermute | solution.py:21
  131.6 65.9 %collective-permute-start.36 = (f32[2,4,4,64,128]{4,3,2,1,0:T(8,128)}, f32[2,4,4,64,128]{4,3,2,1,0:T(8,128)S(1)}, u32[]{:S(2)}, u32[]{:S(2)}) collective-permute-start(f32[2,4,4,64,128]{4,3,2,1,0:T(8,128)} %copy-done.4), channel_id=1, source_target_pairs={{0,8},{8,0},{16,24},{24,16},{1,9},{9,1},{17,25},{25,17},{2,10},{10... | collective-permute-start | bytes 3145736 | tf_op jit(solution)/shard_map/ppermute | solution.py:21
  175.3 20.0 %collective-permute-start.47 = (f32[1,4,2,64,128]{4,3,2,1,0:T(8,128)S(1)}, f32[1,4,2,64,128]{4,3,2,1,0:T(8,128)S(1)}, u32[]{:S(2)}, u32[]{:S(2)}) collective-permute-start(f32[1,4,2,64,128]{4,3,2,1,0:T(8,128)S(1)} %slice_add_fusion.2), channel_id=1, source_target_pairs={{0,16},{8,24},{16,0},{24,8},{1,17},{9,25},{17,1},{25,9},{2,18},{10... | collective-permute-start | bytes 786440 | tf_op jit(solution)/shard_map/ppermute | solution.py:21
  177.8 18.6 %collective-permute-start.42 = (f32[1,4,2,64,128]{4,3,2,1,0:T(8,128)S(1)}, f32[1,4,2,64,128]{4,3,2,1,0:T(8,128)S(1)}, u32[]{:S(2)}, u32[]{:S(2)}) collective-permute-start(f32[1,4,2,64,128]{4,3,2,1,0:T(8,128)S(1)} %slice_add_fusion.4), channel_id=1, source_target_pairs={{0,16},{8,24},{16,0},{24,8},{1,17},{9,25},{17,1},{25,9},{2,18},{10... | collective-permute-start | bytes 786440 | tf_op jit(solution)/shard_map/ppermute | solution.py:21
  178.4 22.7 %collective-permute-start.29 = (f32[32,512]{1,0:T(8,128)S(1)}, f32[32,512]{1,0:T(8,128)S(1)}, u32[]{:S(2)}, u32[]{:S(2)}) collective-permute-start(f32[32,512]{1,0:T(8,128)S(1)} %get-tuple-element.79), channel_id=1, source_target_pairs={{0,2},{2,0},{4,6},{6,4},{1,3},{3,1},{5,7},{7,5},{8,10},{10,8},{12,... | collective-permute-start | bytes 196616 | tf_op jit(solution)/shard_map/ppermute | solution.py:21
  183.9 18.6 %collective-permute-start.31 = (f32[32,512]{1,0:T(8,128)S(1)}, f32[32,512]{1,0:T(8,128)S(1)}, u32[]{:S(2)}, u32[]{:S(2)}) collective-permute-start(f32[32,512]{1,0:T(8,128)S(1)} %get-tuple-element.80), channel_id=1, source_target_pairs={{0,6},{2,4},{4,2},{6,0},{1,7},{3,5},{5,3},{7,1},{8,14},{10,12},{12... | collective-permute-start | bytes 196616 | tf_op jit(solution)/shard_map/ppermute | solution.py:21
  197.5 27.1 %collective-permute-start.50 = (f32[2,64,128]{2,1,0:T(8,128)S(1)}, f32[2,64,128]{2,1,0:T(8,128)S(1)}, u32[]{:S(2)}, u32[]{:S(2)}) collective-permute-start(f32[2,64,128]{2,1,0:T(8,128)S(1)} %get-tuple-element.71), channel_id=1, source_target_pairs={{0,6},{2,4},{4,2},{6,0},{1,7},{3,5},{5,3},{7,1},{8,14},{10,12},{12... | collective-permute-start | bytes 196616 | tf_op jit(solution)/shard_map/ppermute | solution.py:21
  199.2 25.8 %collective-permute-start.49 = (f32[2,64,128]{2,1,0:T(8,128)S(1)}, f32[2,64,128]{2,1,0:T(8,128)S(1)}, u32[]{:S(2)}, u32[]{:S(2)}) collective-permute-start(f32[2,64,128]{2,1,0:T(8,128)S(1)} %get-tuple-element.72), channel_id=1, source_target_pairs={{0,4},{2,6},{4,0},{6,2},{1,5},{3,7},{5,1},{7,3},{8,12},{10,14},{12... | collective-permute-start | bytes 196616 | tf_op jit(solution)/shard_map/ppermute | solution.py:21
  201.1 21.7 %collective-permute-start.37 = (f32[1,4,4,64,128]{4,3,2,1,0:T(8,128)S(1)}, f32[1,4,4,64,128]{4,3,2,1,0:T(8,128)S(1)}, u32[]{:S(2)}, u32[]{:S(2)}) collective-permute-start(f32[1,4,4,64,128]{4,3,2,1,0:T(8,128)S(1)} %slice_add_fusion), channel_id=1, source_target_pairs={{0,16},{8,24},{16,0},{24,8},{1,17},{9,25},{17,1},{25,9},{2,18},{10... | collective-permute-start | bytes 1572872 | tf_op jit(solution)/shard_map/ppermute | solution.py:21
  202.5 17.8 %collective-permute-start.4 = (f32[1,128,512]{2,1,0:T(8,128)S(1)}, f32[1,128,512]{2,1,0:T(8,128)S(1)}, u32[]{:S(2)}, u32[]{:S(2)}) collective-permute-start(f32[1,128,512]{2,1,0:T(8,128)S(1)} %dynamic-slice_add_fusion), channel_id=1, source_target_pairs={{0,16},{8,24},{16,0},{24,8},{1,17},{9,25},{17,1},{25,9},{2,18},{10... | collective-permute-start | bytes 786440 | tf_op jit(solution)/shard_map/ppermute | solution.py:21
  207.6 19.0 %collective-permute-start.48 = (f32[2,64,128]{2,1,0:T(8,128)S(1)}, f32[2,64,128]{2,1,0:T(8,128)S(1)}, u32[]{:S(2)}, u32[]{:S(2)}) collective-permute-start(f32[2,64,128]{2,1,0:T(8,128)S(1)} %get-tuple-element.73), channel_id=1, source_target_pairs={{0,2},{2,0},{4,6},{6,4},{1,3},{3,1},{5,7},{7,5},{8,10},{10,8},{12,... | collective-permute-start | bytes 196616 | tf_op jit(solution)/shard_map/ppermute | solution.py:21
  (30 other events, 398.5 us)

commit v5 on v4

--- a/solution.py
+++ b/solution.py
@@ -42,13 +42,17 @@
 
 
 def params():
-    return pltpu.CompilerParams(vmem_limit_bytes=24 << 20)
+    return pltpu.CompilerParams(vmem_limit_bytes=48 << 20)
 
 
 def piece_sizes(own):
     sizes = (own // 4,) * 4
     assert all(n > 0 and n % 2 == 0 for n in sizes)
-    return sizes, ((0, 1), (2,), (3,))
+    return sizes, ((0,), (1,), (2,), (3,)), ((0, 1), (2,), (3,))
+
+
+def in_hbm(arrays):
+    return [pltpu.with_memory_space_constraint(a, pltpu.HBM) for a in arrays]
 
 
 def whole_spec(shape):
@@ -62,7 +66,7 @@
 
 
 def cut(where, flat, pieces):
-    unit = math.gcd(4, *[n for _, _, *counts in pieces for n in counts])
+    unit = math.gcd(*[n for _, _, *counts in pieces for n in counts if n])
     block = (unit,) + flat.shape[1:]
     steps = max(size for *_, size in pieces) // unit
     in_specs, out_specs, out_shape = [], [], []
@@ -224,11 +228,11 @@
     half = (nx // 2, ny, pairs, a_block, 2 * b_block)
     specs = [whole_spec(part.shape) for part in parts]
     specs += [whole_spec(fy[0].shape)] * 2 + [whole_spec(fxt.shape)]
-    args = [*parts, *fy, fxt]
+    args = [*in_hbm(parts), *fy, fxt]
     first = gram is None
     if not first:
         specs.append(whole_spec((width, width)))
-        args.append(gram)
+        args += in_hbm([gram])
     out_specs = [whole_spec(half)] * 2
     out_shape = [jax.ShapeDtypeStruct(half, F32)] * 2
     scratch = [pltpu.VMEM((n * x_local, width), F32)]
@@ -239,7 +243,7 @@
         scratch.append(pltpu.VMEM((width, width), F32))
     else:
         out_specs.append(whole_spec((width, width)))
-        out_shape.append(jax.ShapeDtypeStruct((width, width), F32))
+        out_shape.append(pltpu.HBM((width, width), F32))
     flops = 2 * n * x_local * (width * width + width * rank + rank * rank) * 3
     return pl.pallas_call(
         functools.partial(chunk_kernel, sizes, count, first, last),
@@ -309,34 +313,84 @@
         out_shape=[jax.ShapeDtypeStruct(half, F32)] * 2,
         compiler_params=params(),
         cost_estimate=pl.CostEstimate(flops=flops, bytes_accessed=1 << 23, transcendentals=0),
-    )(where, flat, *parts)
-
-
-def unpack_kernel(ny, own, starts, s_ref, *refs):
-    parts, out_ref = refs[:-1], refs[-1]
+    )(where, *in_hbm([flat, *parts]))
+
+
+def pack_kernel(ny, extra, s_ref, *refs):
+    outs, refs = refs[-ny:], refs[:-ny]
+    if extra:
+        xrows, refs = refs[-1], refs[:-1]
+    lanes = outs[0].shape[2]
+    for k in range(ny):
+        at = s_ref[1] ^ k
+        row = 0
+        for keep, got in zip(refs[::2], refs[1::2]):
+            outs[k][row : row + keep.shape[1]] = keep[at] + got[at]
+            row += keep.shape[1]
+        if extra:
+            size = xrows.shape[1]
+            for j in range(xrows.shape[2] // lanes):
+                block, start = divmod(j * size, outs[k].shape[1])
+                outs[k][row + block, start : start + size] = xrows[
+                    at, :, j * lanes : (j + 1) * lanes
+                ]
+
+
+def pack(sizes, where, halves, xrows=None):
+    ny = sizes[1]
+    args = [v for pair in halves for v in pair]
+    _, _, a_block, lanes = args[0].shape
+    count = sum(v.shape[1] for v in args[::2])
+    if xrows is not None:
+        args.append(xrows)
+        count += xrows.shape[1] * xrows.shape[2] // (a_block * lanes)
+    shape = (count, a_block, lanes)
+    return pl.pallas_call(
+        functools.partial(pack_kernel, ny, xrows is not None),
+        grid_spec=pltpu.PrefetchScalarGridSpec(
+            num_scalar_prefetch=1,
+            grid=(1,),
+            in_specs=[whole_spec(a.shape) for a in args],
+            out_specs=[whole_spec(shape)] * ny,
+        ),
+        out_shape=[jax.ShapeDtypeStruct(shape, F32)] * ny,
+        compiler_params=params(),
+        cost_estimate=pl.CostEstimate(flops=1000, bytes_accessed=1 << 20, transcendentals=0),
+    )(where, *args)
+
+
+def unpack_kernel(ny, own, starts, counts, terms, s_ref, *refs):
+    parts, (out_ref, gram_ref) = refs[:-2], refs[-2:]
     b_block = out_ref.shape[2]
     for c, start in enumerate(starts):
         for k in range(ny):
             part = parts[c * ny + k]
-            for j in range(part.shape[0]):
+            for j in range(counts[c] // 2):
                 base = (s_ref[1] ^ k) * own + start + 2 * j
                 out_ref[base] = part[j, :, :b_block]
                 out_ref[base + 1] = part[j, :, b_block:]
-
-
-def unpack(sizes, where, parts, starts, rows):
+    size, lanes = gram_ref.shape[0], 2 * b_block
+    for j in range(gram_ref.shape[1] // lanes):
+        block, start = divmod(j * size, out_ref.shape[1])
+        total = parts[0][counts[0] // 2 + block, start : start + size]
+        for k in range(1, ny):
+            total = total + parts[k][counts[0] // 2 + block, start : start + size]
+        gram_ref[:, j * lanes : (j + 1) * lanes] = total / terms
+
+
+def unpack(sizes, where, parts, starts, counts, rows, gram_shape, terms):
     ny = sizes[1]
     _, a_block, lanes = parts[0].shape
     shape = (rows, a_block, lanes // 2)
     return pl.pallas_call(
-        functools.partial(unpack_kernel, ny, rows // ny, starts),
+        functools.partial(unpack_kernel, ny, rows // ny, starts, counts, terms),
         grid_spec=pltpu.PrefetchScalarGridSpec(
             num_scalar_prefetch=1,
             grid=(1,),
             in_specs=[whole_spec(p.shape) for p in parts],
-            out_specs=whole_spec(shape),
-        ),
-        out_shape=jax.ShapeDtypeStruct(shape, F32),
+            out_specs=[whole_spec(shape), whole_spec(gram_shape)],
+        ),
+        out_shape=[jax.ShapeDtypeStruct(shape, F32), jax.ShapeDtypeStruct(gram_shape, F32)],
         compiler_params=params(),
         cost_estimate=pl.CostEstimate(flops=1000, bytes_accessed=3 << 20, transcendentals=0),
     )(where, *parts)
@@ -352,7 +406,7 @@
     rows = z_cells * s_local
     flat = slab.reshape((rows, x_local, y_local))
     own_y, own_x = rows // ny, rows // nx
-    counts, chunks = piece_sizes(own_y)
+    counts, chunks, sends = piece_sizes(own_y)
     starts = [sum(counts[:c]) for c in range(len(counts))]
     x_total, y_total, s_total = x_local * nx, y_local * ny, s_local * ns
 
@@ -378,7 +432,7 @@
     fxt = factor_x.T
 
     gram = None
-    core_parts = []
+    core_parts, reduced = [], []
     for c, members in enumerate(chunks):
         last = c == len(chunks) - 1
         parts = sum((along_y[p] for p in members), [])
@@ -395,14 +449,9 @@
             if 2 * bit < nx:
                 sent = keep[1::2] + got[1::2]
                 keep, got = keep[0::2], got[0::2]
-            keep = keep + got
+                keep = keep + got
             bit *= 2
-        keep = keep[0]
-        z_parts = [pick(keep, me_y ^ k, 0) for k in range(ny)]
-        core_parts += [swap(z_parts[k], "gy", k) if k else z_parts[0] for k in range(ny)]
-    core = unpack(sizes, where, core_parts, [starts[m[0]] for m in chunks], rows)
-    core = core.reshape((z_cells, s_local, a_block, b_block))
-
+        reduced.append((keep[0], got[0]))
     keep, sent = gram_x_terms(sizes, where, flat, along_x)
     got = swap(sent, "gx", 1)
     bit = 2
@@ -415,13 +464,21 @@
         got = swap(sent, "gx", bit)
         bit *= 2
     total = (keep[0] + got[0]).reshape((ny, ns, -1, x_total))
-    keep = pick(total, me_s, 1)
+    x_rows = pick(total, me_s, 1)
     for k in range(1, ns):
-        keep = keep + swap(pick(total, me_s ^ k, 1), "sa", k)
-    gram_x = pick(keep, me_y, 0)
-    for k in range(1, ny):
-        gram_x = gram_x + swap(pick(keep, me_y ^ k, 0), "gy", k)
-    gram_x = gram_x / (y_total * z_cells * s_total)
+        x_rows = x_rows + swap(pick(total, me_s ^ k, 1), "sa", k)
+
+    for c, members in enumerate(sends):
+        z_parts = pack(sizes, where, [reduced[m] for m in members], None if c else x_rows)
+        core_parts += [swap(z_parts[k], "gy", k) if k else z_parts[0] for k in range(ny)]
+    send_starts = [starts[chunks[m[0]][0]] for m in sends]
+    send_counts = [sum(counts[p] for m in members for p in chunks[m]) for members in sends]
+    gram_shape = x_rows.shape[1:]
+    terms = y_total * z_cells * s_total
+    core, gram_x = unpack(
+        sizes, where, core_parts, send_starts, send_counts, rows, gram_shape, terms
+    )
+    core = core.reshape((z_cells, s_local, a_block, b_block))
 
     keep, got = gkeep, ggot
     bit = 2

time: 246 us -> 202 us (0.82)
  waiting for transfers between devices: 119 us -> 71 us
  Pallas kernels: 41.2 us -> 48.7 us
  other arithmetic: 7.65 us -> 3.14 us
  starting transfers between devices: 72.2 us -> 74.7 us
    ppermute x51 -> x50, waiting for transfers between devices: 119 us -> 71 us  [swap(): return lax.ppermute(value, axis, [(i, i ^ offset) for i in range(size)])]
    pallas_call x3 -> x4, Pallas kernels: 12.2 us -> 19.7 us  [chunk_terms(): pl.pallas_call(functools.partial(chunk_kernel, sizes, count, first, last)...]
    ppermute x51 -> x50, starting transfers between devices: 72.2 us -> 74.7 us  [swap(): return lax.ppermute(value, axis, [(i, i ^ offset) for i in range(size)])]
  transfers between devices with their start and end apart: 51 -> 50, of which waited for: 13 -> 16; matrix products, arithmetic and copies ran while one was open for 3% -> 2% of each run, Pallas kernels for 14% -> 23%
where the time goes in v5:
time: 202 us
  starting transfers between devices  74.7 us (37%)
  waiting for transfers between devices  71 us (35%)
  Pallas kernels  48.7 us (24%)
  other arithmetic  3.14 us (2%)
  local copies, waits for them, and re-layouts  3.06 us (2%)
    ppermute x50, starting transfers between devices, swap(): return lax.ppermute(value, axis, [(i, i ^ offset) for i in range(size)])  74.7 us
    ppermute x50, waiting for transfers between devices, swap(): return lax.ppermute(value, axis, [(i, i ^ offset) for i in range(size)])  71 us
    pallas_call x4, Pallas kernels, chunk_terms(): pl.pallas_call(functools.partial(chunk_kernel, sizes, count, first, last)...  19.7 us
    pallas_call x5, Pallas kernels, cut(): pl.pallas_call(cut_kernel, grid_spec=pltpu.PrefetchScalarGridSpec(num_sca...  16.1 us
    pallas_call x1, Pallas kernels, gram_x_terms(): pl.pallas_call(functools.partial(gram_x_kernel, sizes), grid_spec=pltpu.P...  7 us
  transfers between devices with their start and end apart: 50, of which 16 were waited for; matrix products, arithmetic and copies ran while one was open for 2% of the time, Pallas kernels for 23%

profile of v5, /device:TPU:0, one launch (start us, length us, event | category | flops | bytes accessed | tf_op | source)
XLA Modules:
  0.0 201.7 jit_solution(12114928039969443177)
XLA Ops:
  1.4 5.1 %collective-permute-start.5 = (f32[32,256]{1,0:T(8,128)S(1)}, f32[32,256]{1,0:T(8,128)S(1)}, u32[]{:S(2)}, u32[]{:S(2)}) collective-permute-start(f32[32,256]{1,0:T(8,128)S(1)} %dynamic-slice_bitcast_fusion.4), channel_id=1, source_target_pairs={{0,6},{2,4},{4,2},{6,0},{1,7},{3,5},{5,3},{7,1},{8,14},{10,12},{12... | collective-permute-start | bytes 98312 | tf_op jit(solution)/shard_map/ppermute | solution.py:21
  7.6 2.7 %shard_map.59 = (f32[4,128,128]{2,1,0:T(8,128)}, f32[4,128,128]{2,1,0:T(8,128)}, f32[4,128,128]{2,1,0:T(8,128)}) custom-call(s32[3]{0:T(128)} %pad_add_fusion.s_ref, f32[64,128,128]{2,1,0:T(8,128)} %bitcast.78, f32[64,128,128]{2,1,0:T(8,128)} %bitcast.79, f32[64,128,128]{2,1,0:T(8,128)} %bitcast.80), custom_call_target="tpu_custom_call" | custom-call | flops 1000 | bytes 4194304 | tf_op jit(solution)/shard_map/pallas_call | solution.py:85
  11.9 1.6 collective-permute-start.7
  13.5 2.9 %collective-permute-start.1 = (f32[4,128,128]{2,1,0:T(8,128)}, f32[4,128,128]{2,1,0:T(8,128)S(1)}, u32[]{:S(2)}, u32[]{:S(2)}) collective-permute-start(f32[4,128,128]{2,1,0:T(8,128)} %get-tuple-element.54), channel_id=1, source_target_pairs={{0,4},{2,6},{4,0},{6,2},{1,5},{3,7},{5,1},{7,3},{8,12},{10,14},{12... | collective-permute-start | bytes 786440 | tf_op jit(solution)/shard_map/ppermute | solution.py:21
  16.6 3.0 %shard_map.58 = (f32[4,128,128]{2,1,0:T(8,128)}, f32[4,128,128]{2,1,0:T(8,128)}, f32[4,128,128]{2,1,0:T(8,128)}, f32[4,128,128]{2,1,0:T(8,128)}, f32[4,128,128]{2,1,0:T(8,128)}) custom-call(s32[3]{0:T(128)} %pad_add_fusion.s_ref, f32[64,128,128]{2,1,0:T(8,128)} %bitcast.81, f32[64,128,128]{2,1,0:T(8,128)} %bitcast.82, f32[64,128,128]{2,1,0:T(8,128)} %bitcast.83, ...), custom_call_target="tpu_custom_call" | custom-call | flops 1000 | bytes 4194304 | tf_op jit(solution)/shard_map/pallas_call | solution.py:85
  20.0 4.9 %collective-permute-done.8.refs_3_ = f32[3,32,256]{2,1,0:T(8,128)S(1)} collective-permute-done((f32[3,32,256]{2,1,0:T(8,128)S(1)}, f32[3,32,256]{2,1,0:T(8,128)S(1)}, u32[]{:S(2)}, u32[]{:S(2)}) %collective-permute-start.8) | collective-permute-done | bytes 98336 | tf_op jit(solution)/shard_map/ppermute | solution.py:21
  24.9 3.5 %collective-permute-start.12 = (f32[4,128,128]{2,1,0:T(8,128)}, f32[4,128,128]{2,1,0:T(8,128)S(1)}, u32[]{:S(2)}, u32[]{:S(2)}) collective-permute-start(f32[4,128,128]{2,1,0:T(8,128)} %get-tuple-element.62), channel_id=1, source_target_pairs={{0,4},{2,6},{4,0},{6,2},{1,5},{3,7},{5,1},{7,3},{8,12},{10,14},{12... | collective-permute-start | bytes 786440 | tf_op jit(solution)/shard_map/ppermute | solution.py:21
  28.7 3.6 %shard_map.67 = (f32[4,128,128]{2,1,0:T(8,128)}, f32[4,128,128]{2,1,0:T(8,128)}, f32[4,128,128]{2,1,0:T(8,128)}, f32[4,128,128]{2,1,0:T(8,128)}, f32[4,128,128]{...) custom-call(s32[3]{0:T(128)} %pad_add_fusion.s_ref, ...), custom_call_target="tpu_custom_call" | custom-call | flops 1000 | bytes 4194304 | tf_op jit(solution)/shard_map/pallas_call | solution.py:85
  32.3 2.8 %collective-permute-done.1.refs_2_ = f32[4,128,128]{2,1,0:T(8,128)S(1)} collective-permute-done((f32[4,128,128]{2,1,0:T(8,128)}, f32[4,128,128]{2,1,0:T(8,128)S(1)}, u32[]{:S(2)}, u32[]{:S(2)}) %collective-permute-start.1) | collective-permute-done | bytes 262176 | tf_op jit(solution)/shard_map/ppermute | solution.py:21
  35.1 18.4 %collective-permute-start.26 = (f32[4,128,128]{2,1,0:T(8,128)}, f32[4,128,128]{2,1,0:T(8,128)S(1)}, u32[]{:S(2)}, u32[]{:S(2)}) collective-permute-start(f32[4,128,128]{2,1,0:T(8,128)} %get-tuple-element.77), channel_id=1, source_target_pairs={{0,4},{2,6},{4,0},{6,2},{1,5},{3,7},{5,1},{7,3},{8,12},{10,14},{12... | collective-permute-start | bytes 786440 | tf_op jit(solution)/shard_map/ppermute | solution.py:21
  54.8 13.9 %collective-permute-done.12.refs_2_ = f32[4,128,128]{2,1,0:T(8,128)S(1)} collective-permute-done((f32[4,128,128]{2,1,0:T(8,128)}, f32[4,128,128]{2,1,0:T(8,128)S(1)}, u32[]{:S(2)}, u32[]{:S(2)}) %collective-permute-start.12) | collective-permute-done | bytes 262176 | tf_op jit(solution)/shard_map/ppermute | solution.py:21
  69.5 7.1 %collective-permute-start.34 = (f32[4,128,128]{2,1,0:T(8,128)}, f32[4,128,128]{2,1,0:T(8,128)S(1)}, u32[]{:S(2)}, u32[]{:S(2)}) collective-permute-start(f32[4,128,128]{2,1,0:T(8,128)} %get-tuple-element.88), channel_id=1, source_target_pairs={{0,4},{2,6},{4,0},{6,2},{1,5},{3,7},{5,1},{7,3},{8,12},{10,14},{12... | collective-permute-start | bytes 786440 | tf_op jit(solution)/shard_map/ppermute | solution.py:21
  76.6 3.6 %shard_map.63 = (f32[16,128,128]{2,1,0:T(8,128)}, f32[16,128,128]{2,1,0:T(8,128)}) custom-call(s32[3]{0:T(128)} %pad_add_fusion.s_ref, f32[64,128,128]{2,1,0:T(8,128)} %bitcast.94, f32[64,128,128]{2,1,0:T(8,128)} %bitcast.95), custom_call_target="tpu_custom_call" | custom-call | flops 1000 | bytes 4194304 | tf_op jit(solution)/shard_map/pallas_call | solution.py:85
  80.3 3.1 %shard_map.64 = f32[16,128,128]{2,1,0:T(8,128)} custom-call(s32[3]{0:T(128)} %pad_add_fusion.s_ref, f32[64,128,128]{2,1,0:T(8,128)} %bitcast.96), custom_call_target="tpu_custom_call" | custom-call | flops 1000 | bytes 4194304 | tf_op jit(solution)/shard_map/pallas_call | solution.py:85
  87.0 4.6 %shard_map.61 = (f32[2,4,2,64,128]{4,3,2,1,0:T(8,128)S(1)}, f32[2,4,2,64,128]{4,3,2,1,0:T(8,128)S(1)}, f32[512,512]{1,0:T(8,128)}) custom-call(s32[3]{0:T(128)S(1)} %copy-done.1, f32[4,128,128]{2,1,0:T(8,128)} %get-tuple-element.52.refs_0_, f32[4,128,128]{2,1,0:T(8,128)} %copy-done.5, f32[4,128,128]{2,1,0:T(8,128)} %copy-done.7, f32[4,128,128]{2,1,0:T(8,128)} %copy-done.8, ...), custom_call_target="tpu_custom_call" | custom-call | flops 1409286144 | bytes 4194304 | tf_op jit(solution)/shard_map/pallas_call | solution.py:248
  91.5 2.4 %collective-permute-start.35 = (f32[4,128,128]{2,1,0:T(8,128)}, f32[4,128,128]{2,1,0:T(8,128)}, u32[]{:S(2)}, u32[]{:S(2)}) collective-permute-start(f32[4,128,128]{2,1,0:T(8,128)} %get-tuple-element.89), channel_id=1, source_target_pairs={{0,6},{2,4},{4,2},{6,0},{1,7},{3,5},{5,3},{7,1},{8,14},{10,12},{12... | collective-permute-start | bytes 786440 | tf_op jit(solution)/shard_map/ppermute | solution.py:21
  93.9 2.5 %collective-permute-done.34.refs_2_ = f32[4,128,128]{2,1,0:T(8,128)S(1)} collective-permute-done((f32[4,128,128]{2,1,0:T(8,128)}, f32[4,128,128]{2,1,0:T(8,128)S(1)}, u32[]{:S(2)}, u32[]{:S(2)}) %collective-permute-start.34) | collective-permute-done | bytes 262176 | tf_op jit(solution)/shard_map/ppermute | solution.py:21
  97.1 5.0 %shard_map.62 = (f32[2,4,2,64,128]{4,3,2,1,0:T(8,128)S(1)}, f32[2,4,2,64,128]{4,3,2,1,0:T(8,128)S(1)}, f32[512,512]{1,0:T(8,128)}) custom-call(s32[3]{0:T(128)S(1)} %copy-done.1, f32[4,128,128]{2,1,0:T(8,128)} %get-tuple-element.60.refs_0_, f32[4,128,128]{2,1,0:T(8,128)} %copy-done.6, f32[4,128,128]{2,1,0:T(8,128)} %copy-done.9, f32[4,128,128]{2,1,0:T(8,128)} %copy-done.10, ...), custom_call_target="tpu_custom_call" | custom-call | flops 1409286144 | bytes 4194304 | tf_op jit(solution)/shard_map/pallas_call | solution.py:248
  102.1 5.4 %shard_map.68 = (f32[2,4,2,64,128]{4,3,2,1,0:T(8,128)S(1)}, f32[2,4,2,64,128]{4,3,2,1,0:T(8,128)}, f32[512,512]{1,0:T(8,128)}) custom-call(s32[3]{0:T(128)S(1)} %copy-done.1, f32[4,128,128]{2,1,0:T(8,128)} %get-tuple-element.75.refs_0_, f32[4,128,128]{2,1,0:T(8,128)} %copy-done.11, f32[4,128,128]{2,1,0:T(8,128)} %copy-done.12, f32[4,128,128]{2,1,0:T(8,128)} %copy-done.13, ...), custom_call_target="tpu_custom_call" | custom-call | flops 1409286144 | bytes 4194304 | tf_op jit(solution)/shard_map/pallas_call | solution.py:248
  107.5 4.7 %shard_map.70 = (f32[2,4,2,64,128]{4,3,2,1,0:T(8,128)S(1)}, f32[2,4,2,64,128]{4,3,2,1,0:T(8,128)S(1)}, f32[4,64,512]{2,1,0:T(8,128)S(1)}, f32[4,64,512]{2,1,0:T(8,128)S(1)}) custom-call(s32[3]{0:T(128)S(1)} %copy-done.1, f32[4,128,128]{2,1,0:T(8,128)} %get-tuple-element.86.refs_0_, f32[4,128,128]{2,1,0:T(8,128)} %copy-done.3, f32[4,128,128]{2,1,0:T(8,128)} %copy-done.4, ...), custom_call_target="tpu_custom_call" | custom-call | flops 1409286144 | bytes 4194304 | tf_op jit(solution)/shard_map/pallas_call | solution.py:248
  116.2 16.4 %collective-permute-done.18.refs_3_ = f32[16,128,128]{2,1,0:T(8,128)} collective-permute-done((f32[16,128,128]{2,1,0:T(8,128)}, f32[16,128,128]{2,1,0:T(8,128)}, u32[]{:S(2)}, u32[]{:S(2)}) %collective-permute-start.18) | collective-permute-done | bytes 1048608 | tf_op jit(solution)/shard_map/ppermute | solution.py:21
  134.0 7.0 %shard_map.65 = (f32[2,128,512]{2,1,0:T(8,128)S(1)}, f32[2,128,512]{2,1,0:T(8,128)S(1)}) custom-call(s32[3]{0:T(128)S(1)} %copy-done.1, f32[64,128,128]{2,1,0:T(8,128)} %bitcast.97, f32[16,128,128]{2,1,0:T(8,128)} %collective-permute-done.16.refs_1_, f32[16,128,128]{2,1,0:T(8,128)} %collective-permute-done.17.refs_2_, ...), custom_call_target="tpu_custom_call" | custom-call | flops 3221225472 | bytes 8388608 | tf_op jit(solution)/shard_map/pallas_call | solution.py:304
  144.8 6.2 %collective-permute-done.42 = f32[4,32,512]{2,1,0:T(8,128)S(1)} collective-permute-done((f32[4,32,512]{2,1,0:T(8,128)S(1)}, f32[4,32,512]{2,1,0:T(8,128)S(1)}, u32[]{:S(2)}, u32[]{:S(2)}) %collective-permute-start.42) | collective-permute-done | bytes 262176 | tf_op jit(solution)/shard_map/ppermute | solution.py:21
  151.1 2.4 %collective-permute-start.45 = (f32[32,512]{1,0:T(8,128)S(1)}, f32[32,512]{1,0:T(8,128)S(1)}, u32[]{:S(2)}, u32[]{:S(2)}) collective-permute-start(f32[32,512]{1,0:T(8,128)S(1)} %get-tuple-element.110), channel_id=1, source_target_pairs={{0,6},{2,4},{4,2},{6,0},{1,7},{3,5},{5,3},{7,1},{8,14},{10,12},{12... | collective-permute-start | bytes 196616 | tf_op jit(solution)/shard_map/ppermute | solution.py:21
  153.5 2.2 %collective-permute-done.20 = f32[1,128,512]{2,1,0:T(8,128)S(1)} collective-permute-done((f32[1,128,512]{2,1,0:T(8,128)S(1)}, f32[1,128,512]{2,1,0:T(8,128)S(1)}, u32[]{:S(2)}, u32[]{:S(2)}) %collective-permute-start.20) | collective-permute-done | bytes 262176 | tf_op jit(solution)/shard_map/ppermute | solution.py:21
  163.0 5.8 %collective-permute-done.37 = f32[1,4,2,64,128]{4,3,2,1,0:T(8,128)S(1)} collective-permute-done((f32[1,4,2,64,128]{4,3,2,1,0:T(8,128)S(1)}, f32[1,4,2,64,128]{4,3,2,1,0:T(8,128)S(1)}, u32[]{:S(2)}, u32[]{:S(2)}) %collective-permute-start.37) | collective-permute-done | bytes 262176 | tf_op jit(solution)/shard_map/ppermute | solution.py:21
  168.8 1.7 collective-permute-start.30
  176.9 1.6 collective-permute-start.23
  181.6 2.8 %collective-permute-done.48.refs_2_ = f32[32,512]{1,0:T(8,128)S(1)} collective-permute-done((f32[32,512]{1,0:T(8,128)S(1)}, f32[32,512]{1,0:T(8,128)S(1)}, u32[]{:S(2)}, u32[]{:S(2)}) %collective-permute-start.48) | collective-permute-done | bytes 65568 | tf_op jit(solution)/shard_map/ppermute | solution.py:21
  185.8 2.3 %collective-permute-start.40 = (f32[2,64,128]{2,1,0:T(8,128)S(1)}, f32[2,64,128]{2,1,0:T(8,128)S(1)}, u32[]{:S(2)}, u32[]{:S(2)}) collective-permute-start(f32[2,64,128]{2,1,0:T(8,128)S(1)} %get-tuple-element.96), channel_id=1, source_target_pairs={{0,6},{2,4},{4,2},{6,0},{1,7},{3,5},{5,3},{7,1},{8,14},{10,12},{12... | collective-permute-start | bytes 196616 | tf_op jit(solution)/shard_map/ppermute | solution.py:21
  189.4 10.0 %collective-permute-done.39.refs_10_ = f32[2,64,128]{2,1,0:T(8,128)S(1)} collective-permute-done((f32[2,64,128]{2,1,0:T(8,128)S(1)}, f32[2,64,128]{2,1,0:T(8,128)S(1)}, u32[]{:S(2)}, u32[]{:S(2)}) %collective-permute-start.39) | collective-permute-done | bytes 65568 | tf_op jit(solution)/shard_map/ppermute | solution.py:21
  199.5 2.2 %shard_map.72 = (f32[64,64,64]{2,1,0:T(8,128)}, f32[16,512]{1,0:T(8,128)}) custom-call(s32[3]{0:T(128)S(1)} %copy-done.1, f32[5,64,128]{2,1,0:T(8,128)S(1)} %get-tuple-element.71.refs_0_, f32[5,64,128]{2,1,0:T(8,128)S(1)} %collective-permute-done.22.refs_1_, f32[5,64,128]{2,1,0:T(8,128)S(1)} %collective-permute-done.23.refs_2_, ...), custom_call_target="tpu_custom_call" | custom-call | flops 1000 | bytes 3145728 | tf_op jit(solution)/shard_map/pallas_call | solution.py:385
  (129 shorter events, 39.2 us)
Async XLA Ops:
  1.4 10.4 %collective-permute-start.5 = (f32[32,256]{1,0:T(8,128)S(1)}, f32[32,256]{1,0:T(8,128)S(1)}, u32[]{:S(2)}, u32[]{:S(2)}) collective-permute-start(f32[32,256]{1,0:T(8,128)S(1)} %dynamic-slice_bitcast_fusion.4), channel_id=1, source_target_pairs={{0,6},{2,4},{4,2},{6,0},{1,7},{3,5},{5,3},{7,1},{8,14},{10,12},{12... | collective-permute-start | bytes 98312 | tf_op jit(solution)/shard_map/ppermute | solution.py:21
  10.4 18.1 %collective-permute-start = (f32[4,128,128]{2,1,0:T(8,128)}, f32[4,128,128]{2,1,0:T(8,128)S(1)}, u32[]{:S(2)}, u32[]{:S(2)}) collective-permute-start(f32[4,128,128]{2,1,0:T(8,128)} %get-tuple-element.53), channel_id=1, source_target_pairs={{0,2},{2,0},{4,6},{6,4},{1,3},{3,1},{5,7},{7,5},{8,10},{10,8},{12,... | collective-permute-start | bytes 786440 | tf_op jit(solution)/shard_map/ppermute | solution.py:21
  13.5 21.6 %collective-permute-start.1 = (f32[4,128,128]{2,1,0:T(8,128)}, f32[4,128,128]{2,1,0:T(8,128)S(1)}, u32[]{:S(2)}, u32[]{:S(2)}) collective-permute-start(f32[4,128,128]{2,1,0:T(8,128)} %get-tuple-element.54), channel_id=1, source_target_pairs={{0,4},{2,6},{4,0},{6,2},{1,5},{3,7},{5,1},{7,3},{8,12},{10,14},{12... | collective-permute-start | bytes 786440 | tf_op jit(solution)/shard_map/ppermute | solution.py:21
  16.4 18.6 %collective-permute-start.2 = (f32[4,128,128]{2,1,0:T(8,128)}, f32[4,128,128]{2,1,0:T(8,128)S(1)}, u32[]{:S(2)}, u32[]{:S(2)}) collective-permute-start(f32[4,128,128]{2,1,0:T(8,128)} %get-tuple-element.55), channel_id=1, source_target_pairs={{0,6},{2,4},{4,2},{6,0},{1,7},{3,5},{5,3},{7,1},{8,14},{10,12},{12... | collective-permute-start | bytes 786440 | tf_op jit(solution)/shard_map/ppermute | solution.py:21
  19.7 33.8 %collective-permute-start.11 = (f32[4,128,128]{2,1,0:T(8,128)}, f32[4,128,128]{2,1,0:T(8,128)S(1)}, u32[]{:S(2)}, u32[]{:S(2)}) collective-permute-start(f32[4,128,128]{2,1,0:T(8,128)} %get-tuple-element.61), channel_id=1, source_target_pairs={{0,2},{2,0},{4,6},{6,4},{1,3},{3,1},{5,7},{7,5},{8,10},{10,8},{12,... | collective-permute-start | bytes 786440 | tf_op jit(solution)/shard_map/ppermute | solution.py:21
  24.9 43.9 %collective-permute-start.12 = (f32[4,128,128]{2,1,0:T(8,128)}, f32[4,128,128]{2,1,0:T(8,128)S(1)}, u32[]{:S(2)}, u32[]{:S(2)}) collective-permute-start(f32[4,128,128]{2,1,0:T(8,128)} %get-tuple-element.62), channel_id=1, source_target_pairs={{0,4},{2,6},{4,0},{6,2},{1,5},{3,7},{5,1},{7,3},{8,12},{10,14},{12... | collective-permute-start | bytes 786440 | tf_op jit(solution)/shard_map/ppermute | solution.py:21
  28.4 40.3 %collective-permute-start.13 = (f32[4,128,128]{2,1,0:T(8,128)}, f32[4,128,128]{2,1,0:T(8,128)S(1)}, u32[]{:S(2)}, u32[]{:S(2)}) collective-permute-start(f32[4,128,128]{2,1,0:T(8,128)} %get-tuple-element.63), channel_id=1, source_target_pairs={{0,6},{2,4},{4,2},{6,0},{1,7},{3,5},{5,3},{7,1},{8,14},{10,12},{12... | collective-permute-start | bytes 786440 | tf_op jit(solution)/shard_map/ppermute | solution.py:21
  35.1 49.2 %collective-permute-start.25 = (f32[4,128,128]{2,1,0:T(8,128)}, f32[4,128,128]{2,1,0:T(8,128)S(1)}, u32[]{:S(2)}, u32[]{:S(2)}) collective-permute-start(f32[4,128,128]{2,1,0:T(8,128)} %get-tuple-element.76), channel_id=1, source_target_pairs={{0,2},{2,0},{4,6},{6,4},{1,3},{3,1},{5,7},{7,5},{8,10},{10,8},{12,... | collective-permute-start | bytes 786440 | tf_op jit(solution)/shard_map/ppermute | solution.py:21
  35.1 50.6 %collective-permute-start.26 = (f32[4,128,128]{2,1,0:T(8,128)}, f32[4,128,128]{2,1,0:T(8,128)S(1)}, u32[]{:S(2)}, u32[]{:S(2)}) collective-permute-start(f32[4,128,128]{2,1,0:T(8,128)} %get-tuple-element.77), channel_id=1, source_target_pairs={{0,4},{2,6},{4,0},{6,2},{1,5},{3,7},{5,1},{7,3},{8,12},{10,14},{12... | collective-permute-start | bytes 786440 | tf_op jit(solution)/shard_map/ppermute | solution.py:21
  53.4 32.8 %collective-permute-start.27 = (f32[4,128,128]{2,1,0:T(8,128)}, f32[4,128,128]{2,1,0:T(8,128)S(1)}, u32[]{:S(2)}, u32[]{:S(2)}) collective-permute-start(f32[4,128,128]{2,1,0:T(8,128)} %get-tuple-element.78), channel_id=1, source_target_pairs={{0,6},{2,4},{4,2},{6,0},{1,7},{3,5},{5,3},{7,1},{8,14},{10,12},{12... | collective-permute-start | bytes 786440 | tf_op jit(solution)/shard_map/ppermute | solution.py:21
  68.8 22.8 %collective-permute-start.33 = (f32[4,128,128]{2,1,0:T(8,128)}, f32[4,128,128]{2,1,0:T(8,128)S(1)}, u32[]{:S(2)}, u32[]{:S(2)}) collective-permute-start(f32[4,128,128]{2,1,0:T(8,128)} %get-tuple-element.87), channel_id=1, source_target_pairs={{0,2},{2,0},{4,6},{6,4},{1,3},{3,1},{5,7},{7,5},{8,10},{10,8},{12,... | collective-permute-start | bytes 786440 | tf_op jit(solution)/shard_map/ppermute | solution.py:21
  69.5 26.8 %collective-permute-start.34 = (f32[4,128,128]{2,1,0:T(8,128)}, f32[4,128,128]{2,1,0:T(8,128)S(1)}, u32[]{:S(2)}, u32[]{:S(2)}) collective-permute-start(f32[4,128,128]{2,1,0:T(8,128)} %get-tuple-element.88), channel_id=1, source_target_pairs={{0,4},{2,6},{4,0},{6,2},{1,5},{3,7},{5,1},{7,3},{8,12},{10,14},{12... | collective-permute-start | bytes 786440 | tf_op jit(solution)/shard_map/ppermute | solution.py:21
  84.3 30.8 %collective-permute-start.16 = (f32[16,128,128]{2,1,0:T(8,128)}, f32[16,128,128]{2,1,0:T(8,128)}, u32[]{:S(2)}, u32[]{:S(2)}) collective-permute-start(f32[16,128,128]{2,1,0:T(8,128)} %get-tuple-element.67), channel_id=1, source_target_pairs={{0,8},{8,0},{16,24},{24,16},{1,9},{9,1},{17,25},{25,17},{2,10},{10... | collective-permute-start | bytes 3145736 | tf_op jit(solution)/shard_map/ppermute | solution.py:21
  85.7 30.0 %collective-permute-start.17 = (f32[16,128,128]{2,1,0:T(8,128)}, f32[16,128,128]{2,1,0:T(8,128)}, u32[]{:S(2)}, u32[]{:S(2)}) collective-permute-start(f32[16,128,128]{2,1,0:T(8,128)} %shard_map.64), channel_id=1, source_target_pairs={{0,16},{8,24},{16,0},{24,8},{1,17},{9,25},{17,1},{25,9},{2,18},{10... | collective-permute-start | bytes 3145736 | tf_op jit(solution)/shard_map/ppermute | solution.py:21
  86.3 46.3 %collective-permute-start.18 = (f32[16,128,128]{2,1,0:T(8,128)}, f32[16,128,128]{2,1,0:T(8,128)}, u32[]{:S(2)}, u32[]{:S(2)}) collective-permute-start(f32[16,128,128]{2,1,0:T(8,128)} %get-tuple-element.68), channel_id=1, source_target_pairs={{0,24},{8,16},{16,8},{24,0},{1,25},{9,17},{17,9},{25,1},{2,26},{10... | collective-permute-start | bytes 3145736 | tf_op jit(solution)/shard_map/ppermute | solution.py:21
  91.5 15.9 %collective-permute-start.35 = (f32[4,128,128]{2,1,0:T(8,128)}, f32[4,128,128]{2,1,0:T(8,128)}, u32[]{:S(2)}, u32[]{:S(2)}) collective-permute-start(f32[4,128,128]{2,1,0:T(8,128)} %get-tuple-element.89), channel_id=1, source_target_pairs={{0,6},{2,4},{4,2},{6,0},{1,7},{3,5},{5,3},{7,1},{8,14},{10,12},{12... | collective-permute-start | bytes 786440 | tf_op jit(solution)/shard_map/ppermute | solution.py:21
  96.4 15.9 %collective-permute-start.9 = (f32[2,4,2,64,128]{4,3,2,1,0:T(8,128)S(1)}, f32[2,4,2,64,128]{4,3,2,1,0:T(8,128)}, u32[]{:S(2)}, u32[]{:S(2)}) collective-permute-start(f32[2,4,2,64,128]{4,3,2,1,0:T(8,128)S(1)} %get-tuple-element.59), channel_id=1, source_target_pairs={{0,8},{8,0},{16,24},{24,16},{1,9},{9,1},{17,25},{25,17},{2,10},{10... | collective-permute-start | bytes 1572872 | tf_op jit(solution)/shard_map/ppermute | solution.py:21
  112.2 29.5 %collective-permute-start.14 = (f32[2,4,2,64,128]{4,3,2,1,0:T(8,128)S(1)}, f32[2,4,2,64,128]{4,3,2,1,0:T(8,128)S(1)}, u32[]{:S(2)}, u32[]{:S(2)}) collective-permute-start(f32[2,4,2,64,128]{4,3,2,1,0:T(8,128)S(1)} %get-tuple-element.66), channel_id=1, source_target_pairs={{0,8},{8,0},{16,24},{24,16},{1,9},{9,1},{17,25},{25,17},{2,10},{10... | collective-permute-start | bytes 1572872 | tf_op jit(solution)/shard_map/ppermute | solution.py:21
  113.9 27.2 %collective-permute-start.41 = (f32[4,64,512]{2,1,0:T(8,128)S(1)}, f32[4,64,512]{2,1,0:T(8,128)S(1)}, u32[]{:S(2)}, u32[]{:S(2)}) collective-permute-start(f32[4,64,512]{2,1,0:T(8,128)S(1)} %get-tuple-element.99), channel_id=1, source_target_pairs={{0,8},{8,0},{16,24},{24,16},{1,9},{9,1},{17,25},{25,17},{2,10},{10... | collective-permute-start | bytes 1572872 | tf_op jit(solution)/shard_map/ppermute | solution.py:21
  115.1 28.2 %collective-permute-start.36 = (f32[2,4,2,64,128]{4,3,2,1,0:T(8,128)S(1)}, f32[2,4,2,64,128]{4,3,2,1,0:T(8,128)S(1)}, u32[]{:S(2)}, u32[]{:S(2)}) collective-permute-start(f32[2,4,2,64,128]{4,3,2,1,0:T(8,128)S(1)} %get-tuple-element.92), channel_id=1, source_target_pairs={{0,8},{8,0},{16,24},{24,16},{1,9},{9,1},{17,25},{25,17},{2,10},{10... | collective-permute-start | bytes 1572872 | tf_op jit(solution)/shard_map/ppermute | solution.py:21
  115.6 56.8 %collective-permute-start.10 = (f32[1,4,2,64,128]{4,3,2,1,0:T(8,128)S(1)}, f32[1,4,2,64,128]{4,3,2,1,0:T(8,128)S(1)}, u32[]{:S(2)}, u32[]{:S(2)}) collective-permute-start(f32[1,4,2,64,128]{4,3,2,1,0:T(8,128)S(1)} %get-tuple-element.107), channel_id=1, source_target_pairs={{0,16},{8,24},{16,0},{24,8},{1,17},{9,25},{17,1},{25,9},{2,18},{10... | collective-permute-start | bytes 786440 | tf_op jit(solution)/shard_map/ppermute | solution.py:21
  132.6 29.2 %collective-permute-start.29 = (f32[1,4,2,64,128]{4,3,2,1,0:T(8,128)S(1)}, f32[1,4,2,64,128]{4,3,2,1,0:T(8,128)S(1)}, u32[]{:S(2)}, u32[]{:S(2)}) collective-permute-start(f32[1,4,2,64,128]{4,3,2,1,0:T(8,128)S(1)} %get-tuple-element.103), channel_id=1, source_target_pairs={{0,16},{8,24},{16,0},{24,8},{1,17},{9,25},{17,1},{25,9},{2,18},{10... | collective-permute-start | bytes 786440 | tf_op jit(solution)/shard_map/ppermute | solution.py:21
  143.5 12.2 %collective-permute-start.20 = (f32[1,128,512]{2,1,0:T(8,128)S(1)}, f32[1,128,512]{2,1,0:T(8,128)S(1)}, u32[]{:S(2)}, u32[]{:S(2)}) collective-permute-start(f32[1,128,512]{2,1,0:T(8,128)S(1)} %dynamic-slice_add_fusion), channel_id=1, source_target_pairs={{0,16},{8,24},{16,0},{24,8},{1,17},{9,25},{17,1},{25,9},{2,18},{10... | collective-permute-start | bytes 786440 | tf_op jit(solution)/shard_map/ppermute | solution.py:21
  157.3 16.7 %collective-permute-start.15 = (f32[1,4,2,64,128]{4,3,2,1,0:T(8,128)S(1)}, f32[1,4,2,64,128]{4,3,2,1,0:T(8,128)S(1)}, u32[]{:S(2)}, u32[]{:S(2)}) collective-permute-start(f32[1,4,2,64,128]{4,3,2,1,0:T(8,128)S(1)} %get-tuple-element.105), channel_id=1, source_target_pairs={{0,16},{8,24},{16,0},{24,8},{1,17},{9,25},{17,1},{25,9},{2,18},{10... | collective-permute-start | bytes 786440 | tf_op jit(solution)/shard_map/ppermute | solution.py:21
  158.8 10.0 %collective-permute-start.37 = (f32[1,4,2,64,128]{4,3,2,1,0:T(8,128)S(1)}, f32[1,4,2,64,128]{4,3,2,1,0:T(8,128)S(1)}, u32[]{:S(2)}, u32[]{:S(2)}) collective-permute-start(f32[1,4,2,64,128]{4,3,2,1,0:T(8,128)S(1)} %get-tuple-element.101), channel_id=1, source_target_pairs={{0,16},{8,24},{16,0},{24,8},{1,17},{9,25},{17,1},{25,9},{2,18},{10... | collective-permute-start | bytes 786440 | tf_op jit(solution)/shard_map/ppermute | solution.py:21
  160.3 14.5 %collective-permute-start.21 = (f32[4,16,512]{2,1,0:T(8,128)S(1)}, f32[4,16,512]{2,1,0:T(8,128)S(1)}, u32[]{:S(2)}, u32[]{:S(2)}) collective-permute-start(f32[4,16,512]{2,1,0:T(8,128)S(1)} %dynamic-slice_bitcast_fusion), channel_id=1, source_target_pairs={{0,1},{1,0},{2,3},{3,2},{4,5},{5,4},{6,7},{7,6},{8,9},{9,8},{10,11... | collective-permute-start | bytes 393224 | tf_op jit(solution)/shard_map/ppermute | solution.py:21
  161.8 9.3 %collective-permute-start.46 = (f32[32,512]{1,0:T(8,128)S(1)}, f32[32,512]{1,0:T(8,128)S(1)}, u32[]{:S(2)}, u32[]{:S(2)}) collective-permute-start(f32[32,512]{1,0:T(8,128)S(1)} %fusion.8), channel_id=1, source_target_pairs={{0,1},{1,0},{2,3},{3,2},{4,5},{5,4},{6,7},{7,6},{8,9},{9,8},{10,11... | collective-permute-start | bytes 196616 | tf_op jit(solution)/shard_map/ppermute | solution.py:21
  175.5 24.0 %collective-permute-start.22 = (f32[5,64,128]{2,1,0:T(8,128)S(1)}, f32[5,64,128]{2,1,0:T(8,128)S(1)}, u32[]{:S(2)}, u32[]{:S(2)}) collective-permute-start(f32[5,64,128]{2,1,0:T(8,128)S(1)} %get-tuple-element.72), channel_id=1, source_target_pairs={{0,2},{2,0},{4,6},{6,4},{1,3},{3,1},{5,7},{7,5},{8,10},{10,8},{12,... | collective-permute-start | bytes 491528 | tf_op jit(solution)/shard_map/ppermute | solution.py:21
  176.9 22.6 %collective-permute-start.23 = (f32[5,64,128]{2,1,0:T(8,128)S(1)}, f32[5,64,128]{2,1,0:T(8,128)S(1)}, u32[]{:S(2)}, u32[]{:S(2)}) collective-permute-start(f32[5,64,128]{2,1,0:T(8,128)S(1)} %get-tuple-element.73), channel_id=1, source_target_pairs={{0,4},{2,6},{4,0},{6,2},{1,5},{3,7},{5,1},{7,3},{8,12},{10,14},{12... | collective-permute-start | bytes 491528 | tf_op jit(solution)/shard_map/ppermute | solution.py:21
  178.7 20.8 %collective-permute-start.24 = (f32[5,64,128]{2,1,0:T(8,128)S(1)}, f32[5,64,128]{2,1,0:T(8,128)S(1)}, u32[]{:S(2)}, u32[]{:S(2)}) collective-permute-start(f32[5,64,128]{2,1,0:T(8,128)S(1)} %get-tuple-element.74), channel_id=1, source_target_pairs={{0,6},{2,4},{4,2},{6,0},{1,7},{3,5},{5,3},{7,1},{8,14},{10,12},{12... | collective-permute-start | bytes 491528 | tf_op jit(solution)/shard_map/ppermute | solution.py:21
  184.4 15.0 %collective-permute-start.39 = (f32[2,64,128]{2,1,0:T(8,128)S(1)}, f32[2,64,128]{2,1,0:T(8,128)S(1)}, u32[]{:S(2)}, u32[]{:S(2)}) collective-permute-start(f32[2,64,128]{2,1,0:T(8,128)S(1)} %get-tuple-element.95), channel_id=1, source_target_pairs={{0,4},{2,6},{4,0},{6,2},{1,5},{3,7},{5,1},{7,3},{8,12},{10,14},{12... | collective-permute-start | bytes 196616 | tf_op jit(solution)/shard_map/ppermute | solution.py:21
  185.8 13.6 %collective-permute-start.40 = (f32[2,64,128]{2,1,0:T(8,128)S(1)}, f32[2,64,128]{2,1,0:T(8,128)S(1)}, u32[]{:S(2)}, u32[]{:S(2)}) collective-permute-start(f32[2,64,128]{2,1,0:T(8,128)S(1)} %get-tuple-element.96), channel_id=1, source_target_pairs={{0,6},{2,4},{4,2},{6,0},{1,7},{3,5},{5,3},{7,1},{8,14},{10,12},{12... | collective-permute-start | bytes 196616 | tf_op jit(solution)/shard_map/ppermute | solution.py:21
  (32 other events, 264.0 us)

commit v6 on v5

--- a/solution.py
+++ b/solution.py
@@ -19,6 +19,10 @@
 def swap(value, axis, offset):
     size = lax.axis_size(axis)
     return lax.ppermute(value, axis, [(i, i ^ offset) for i in range(size)])
+
+
+def far_first(size):
+    return [k for k in range(1, size) if k >= size // 2] + [k for k in range(1, size // 2)]
 
 
 def early_shift(size):
@@ -414,7 +418,9 @@
     x_keys = [(0, k, own_x, 0, own_x) for k in range(1, nx)]
     own_keys = [key[0] for key in keys]
     early = early_shift(nx)
-    groups = [keys[0][1:], [x_keys[early - 1]], keys[1][1:] + own_keys[:2]]
+    first = far_first(ny)[0]
+    groups = [[keys[0][first]], [x_keys[early - 1]] + [key for key in keys[0][1:] if key[1] != first]]
+    groups += [keys[1][1:] + own_keys[:2]]
     groups += [keys[2] + keys[3], [key for key in x_keys if key[1] != early]]
     pieces = {}
     for group in groups:
@@ -463,10 +469,14 @@
         keep = pick(keep, mybit, 1) + pick(got, mybit, 1)
         got = swap(sent, "gx", bit)
         bit *= 2
-    total = (keep[0] + got[0]).reshape((ny, ns, -1, x_total))
-    x_rows = pick(total, me_s, 1)
+    halves = [v[0].reshape((ny, ns, -1, x_total)) for v in (keep, got)]
+
+    def sa_rows(k):
+        return pick(halves[0], me_s ^ k, 1) + pick(halves[1], me_s ^ k, 1)
+
+    x_rows = sa_rows(0)
     for k in range(1, ns):
-        x_rows = x_rows + swap(pick(total, me_s ^ k, 1), "sa", k)
+        x_rows = x_rows + swap(sa_rows(k), "sa", k)
 
     for c, members in enumerate(sends):
         z_parts = pack(sizes, where, [reduced[m] for m in members], None if c else x_rows)
@@ -490,10 +500,13 @@
         keep = pick(keep, mybit, 1) + pick(got, mybit, 1)
         got = swap(sent, "gx", bit)
         bit *= 2
-    total = keep + got
-    row = pick(total, me_y, 0)
+
+    def gy_rows(k):
+        return pick(keep, me_y ^ k, 0) + pick(got, me_y ^ k, 0)
+
+    row = gy_rows(0)
     for k in range(1, ny):
-        row = row + swap(pick(total, me_y ^ k, 0), "gy", k)
+        row = row + swap(gy_rows(k), "gy", k)
     summed = row
     for k in range(1, ns):
         summed = summed + swap(row, "sa", k)

time: 202 us -> 197 us (0.975)
  waiting for transfers between devices: 71 us -> 67.4 us
    ppermute x50, waiting for transfers between devices: 71 us -> 67.4 us  [swap(): return lax.ppermute(value, axis, [(i, i ^ offset) for i in range(size)])]
    add x4, other arithmetic: 2.32 us -> 0.25 us  [local_step(): sent = keep[1::2] + got[1::2]]
  transfers between devices with their start and end apart: 50 -> 50, of which waited for: 16 -> 11; matrix products, arithmetic and copies ran while one was open for 2% -> 1% of each run, Pallas kernels for 23% -> 24%
where the time goes in v6:
time: 197 us
  starting transfers between devices  74 us (38%)
  waiting for transfers between devices  67.4 us (34%)
  Pallas kernels  49.2 us (25%)
  other arithmetic  2.76 us (1%)
  local copies, waits for them, and re-layouts  2.27 us (1%)
    ppermute x50, starting transfers between devices, swap(): return lax.ppermute(value, axis, [(i, i ^ offset) for i in range(size)])  74 us
    ppermute x50, waiting for transfers between devices, swap(): return lax.ppermute(value, axis, [(i, i ^ offset) for i in range(size)])  67.4 us
    pallas_call x4, Pallas kernels, chunk_terms(): pl.pallas_call(functools.partial(chunk_kernel, sizes, count, first, last)...  19.3 us
    pallas_call x5, Pallas kernels, cut(): pl.pallas_call(cut_kernel, grid_spec=pltpu.PrefetchScalarGridSpec(num_sca...  17 us
    pallas_call x1, Pallas kernels, gram_x_terms(): pl.pallas_call(functools.partial(gram_x_kernel, sizes), grid_spec=pltpu.P...  7 us
  transfers between devices with their start and end apart: 50, of which 11 were waited for; matrix products, arithmetic and copies ran while one was open for 1% of the time, Pallas kernels for 24%

profile of v6, /device:TPU:0, one launch (start us, length us, event | category | flops | bytes accessed | tf_op | source)
XLA Modules:
  0.0 196.7 jit_solution(8892621783201999543)
XLA Ops:
  1.4 5.1 %collective-permute-start.5 = (f32[32,256]{1,0:T(8,128)S(1)}, f32[32,256]{1,0:T(8,128)S(1)}, u32[]{:S(2)}, u32[]{:S(2)}) collective-permute-start(f32[32,256]{1,0:T(8,128)S(1)} %dynamic-slice_bitcast_fusion), channel_id=1, source_target_pairs={{0,6},{2,4},{4,2},{6,0},{1,7},{3,5},{5,3},{7,1},{8,14},{10,12},{12... | collective-permute-start | bytes 98312 | tf_op jit(solution)/shard_map/ppermute | solution.py:21
  7.7 4.5 %shard_map.59 = (f32[16,128,128]{2,1,0:T(8,128)}, f32[4,128,128]{2,1,0:T(8,128)}, f32[4,128,128]{2,1,0:T(8,128)}) custom-call(s32[3]{0:T(128)} %pad_add_fusion.s_ref, f32[64,128,128]{2,1,0:T(8,128)} %bitcast.95, f32[64,128,128]{2,1,0:T(8,128)} %bitcast.96, f32[64,128,128]{2,1,0:T(8,128)} %bitcast.97), custom_call_target="tpu_custom_call" | custom-call | flops 1000 | bytes 4194304 | tf_op jit(solution)/shard_map/pallas_call | solution.py:89
  13.6 2.3 %shard_map.60 = f32[4,128,128]{2,1,0:T(8,128)} custom-call(s32[3]{0:T(128)} %pad_add_fusion.s_ref, f32[64,128,128]{2,1,0:T(8,128)} %bitcast.98), custom_call_target="tpu_custom_call" | custom-call | flops 1000 | bytes 4194304 | tf_op jit(solution)/shard_map/pallas_call | solution.py:89
  15.9 2.9 %collective-permute-start.1 = (f32[4,128,128]{2,1,0:T(8,128)}, f32[4,128,128]{2,1,0:T(8,128)S(1)}, u32[]{:S(2)}, u32[]{:S(2)}) collective-permute-start(f32[4,128,128]{2,1,0:T(8,128)} %shard_map.60), channel_id=1, source_target_pairs={{0,4},{2,6},{4,0},{6,2},{1,5},{3,7},{5,1},{7,3},{8,12},{10,14},{12... | collective-permute-start | bytes 786440 | tf_op jit(solution)/shard_map/ppermute | solution.py:21
  19.0 1.8 collective-permute-start.7
  20.8 3.0 %shard_map.58 = (f32[4,128,128]{2,1,0:T(8,128)}, f32[4,128,128]{2,1,0:T(8,128)}, f32[4,128,128]{2,1,0:T(8,128)}, f32[4,128,128]{2,1,0:T(8,128)}, f32[4,128,128]{2,1,0:T(8,128)}) custom-call(s32[3]{0:T(128)} %pad_add_fusion.s_ref, f32[64,128,128]{2,1,0:T(8,128)} %bitcast.99, f32[64,128,128]{2,1,0:T(8,128)} %bitcast.100, f32[64,128,128]{2,1,0:T(8,128)} %bitcast.101, ...), custom_call_target="tpu_custom_call" | custom-call | flops 1000 | bytes 4194304 | tf_op jit(solution)/shard_map/pallas_call | solution.py:89
  25.1 3.6 %shard_map.67 = (f32[4,128,128]{2,1,0:T(8,128)}, f32[4,128,128]{2,1,0:T(8,128)}, f32[4,128,128]{2,1,0:T(8,128)}, f32[4,128,128]{2,1,0:T(8,128)}, f32[4,128,128]{...) custom-call(s32[3]{0:T(128)} %pad_add_fusion.s_ref, ...), custom_call_target="tpu_custom_call" | custom-call | flops 1000 | bytes 4194304 | tf_op jit(solution)/shard_map/pallas_call | solution.py:89
  29.3 3.8 %collective-permute-start.12 = (f32[4,128,128]{2,1,0:T(8,128)S(1)}, f32[4,128,128]{2,1,0:T(8,128)S(1)}, u32[]{:S(2)}, u32[]{:S(2)}) collective-permute-start(f32[4,128,128]{2,1,0:T(8,128)S(1)} %copy-done.17), channel_id=1, source_target_pairs={{0,4},{2,6},{4,0},{6,2},{1,5},{3,7},{5,1},{7,3},{8,12},{10,14},{12... | collective-permute-start | bytes 786440 | tf_op jit(solution)/shard_map/ppermute | solution.py:21
  33.4 4.1 %collective-permute-done.1.refs_2_ = f32[4,128,128]{2,1,0:T(8,128)S(1)} collective-permute-done((f32[4,128,128]{2,1,0:T(8,128)}, f32[4,128,128]{2,1,0:T(8,128)S(1)}, u32[]{:S(2)}, u32[]{:S(2)}) %collective-permute-start.1) | collective-permute-done | bytes 262176 | tf_op jit(solution)/shard_map/ppermute | solution.py:21
  38.2 18.0 %collective-permute-start.26 = (f32[4,128,128]{2,1,0:T(8,128)}, f32[4,128,128]{2,1,0:T(8,128)S(1)}, u32[]{:S(2)}, u32[]{:S(2)}) collective-permute-start(f32[4,128,128]{2,1,0:T(8,128)} %get-tuple-element.77), channel_id=1, source_target_pairs={{0,4},{2,6},{4,0},{6,2},{1,5},{3,7},{5,1},{7,3},{8,12},{10,14},{12... | collective-permute-start | bytes 786440 | tf_op jit(solution)/shard_map/ppermute | solution.py:21
  57.9 3.6 %shard_map.64 = (f32[16,128,128]{2,1,0:T(8,128)}, f32[16,128,128]{2,1,0:T(8,128)}) custom-call(s32[3]{0:T(128)} %pad_add_fusion.s_ref, f32[64,128,128]{2,1,0:T(8,128)} %bitcast.112, f32[64,128,128]{2,1,0:T(8,128)} %bitcast.113), custom_call_target="tpu_custom_call" | custom-call | flops 1000 | bytes 4194304 | tf_op jit(solution)/shard_map/pallas_call | solution.py:89
  61.5 9.5 %collective-permute-done.12.refs_2_ = f32[4,128,128]{2,1,0:T(8,128)S(1)} collective-permute-done((f32[4,128,128]{2,1,0:T(8,128)S(1)}, f32[4,128,128]{2,1,0:T(8,128)S(1)}, u32[]{:S(2)}, u32[]{:S(2)}) %collective-permute-start.12) | collective-permute-done | bytes 262176 | tf_op jit(solution)/shard_map/ppermute | solution.py:21
  72.8 9.4 %collective-permute-done.26.refs_2_ = f32[4,128,128]{2,1,0:T(8,128)S(1)} collective-permute-done((f32[4,128,128]{2,1,0:T(8,128)}, f32[4,128,128]{2,1,0:T(8,128)S(1)}, u32[]{:S(2)}, u32[]{:S(2)}) %collective-permute-start.26) | collective-permute-done | bytes 262176 | tf_op jit(solution)/shard_map/ppermute | solution.py:21
  82.2 5.6 %collective-permute-start.34 = (f32[4,128,128]{2,1,0:T(8,128)S(1)}, f32[4,128,128]{2,1,0:T(8,128)}, u32[]{:S(2)}, u32[]{:S(2)}) collective-permute-start(f32[4,128,128]{2,1,0:T(8,128)S(1)} %copy-done.6), channel_id=1, source_target_pairs={{0,4},{2,6},{4,0},{6,2},{1,5},{3,7},{5,1},{7,3},{8,12},{10,14},{12... | collective-permute-start | bytes 786440 | tf_op jit(solution)/shard_map/ppermute | solution.py:21
  88.6 4.6 %shard_map.62 = (f32[2,4,2,64,128]{4,3,2,1,0:T(8,128)S(1)}, f32[2,4,2,64,128]{4,3,2,1,0:T(8,128)S(1)}, f32[512,512]{1,0:T(8,128)}) custom-call(s32[3]{0:T(128)S(1)} %copy-done.1, f32[4,128,128]{2,1,0:T(8,128)} %get-tuple-element.52.refs_0_, f32[4,128,128]{2,1,0:T(8,128)} %copy-done.11, f32[4,128,128]{2,1,0:T(8,128)} %copy-done.13, ...), custom_call_target="tpu_custom_call" | custom-call | flops 1409286144 | bytes 4194304 | tf_op jit(solution)/shard_map/pallas_call | solution.py:252
  93.4 6.2 %collective-permute-done.34.refs_2_ = f32[4,128,128]{2,1,0:T(8,128)} collective-permute-done((f32[4,128,128]{2,1,0:T(8,128)S(1)}, f32[4,128,128]{2,1,0:T(8,128)}, u32[]{:S(2)}, u32[]{:S(2)}) %collective-permute-start.34) | collective-permute-done | bytes 262176 | tf_op jit(solution)/shard_map/ppermute | solution.py:21
  100.0 5.0 %shard_map.63 = (f32[2,4,2,64,128]{4,3,2,1,0:T(8,128)S(1)}, f32[2,4,2,64,128]{4,3,2,1,0:T(8,128)S(1)}, f32[512,512]{1,0:T(8,128)}) custom-call(s32[3]{0:T(128)S(1)} %copy-done.1, f32[4,128,128]{2,1,0:T(8,128)} %get-tuple-element.59.refs_0_, f32[4,128,128]{2,1,0:T(8,128)} %copy-done.3, f32[4,128,128]{2,1,0:T(8,128)} %copy-done.5, f32[4,128,128]{2,1,0:T(8,128)} %copy-done.7, ...), custom_call_target="tpu_custom_call" | custom-call | flops 1409286144 | bytes 4194304 | tf_op jit(solution)/shard_map/pallas_call | solution.py:252
  105.0 4.9 %shard_map.68 = (f32[2,4,2,64,128]{4,3,2,1,0:T(8,128)S(1)}, f32[2,4,2,64,128]{4,3,2,1,0:T(8,128)S(1)}, f32[512,512]{1,0:T(8,128)}) custom-call(s32[3]{0:T(128)S(1)} %copy-done.1, f32[4,128,128]{2,1,0:T(8,128)} %get-tuple-element.75.refs_0_, f32[4,128,128]{2,1,0:T(8,128)} %copy-done.8, f32[4,128,128]{2,1,0:T(8,128)} %copy-done.9, f32[4,128,128]{2,1,0:T(8,128)} %copy-done.10, ...), custom_call_target="tpu_custom_call" | custom-call | flops 1409286144 | bytes 4194304 | tf_op jit(solution)/shard_map/pallas_call | solution.py:252
  110.7 4.7 %shard_map.70 = (f32[2,4,2,64,128]{4,3,2,1,0:T(8,128)S(1)}, f32[2,4,2,64,128]{4,3,2,1,0:T(8,128)S(1)}, f32[4,64,512]{2,1,0:T(8,128)S(1)}, f32[4,64,512]{2,1,0:T(8,128)S(1)}) custom-call(s32[3]{0:T(128)S(1)} %copy-done.1, f32[4,128,128]{2,1,0:T(8,128)} %get-tuple-element.86.refs_0_, f32[4,128,128]{2,1,0:T(8,128)} %copy-done.12, ...), custom_call_target="tpu_custom_call" | custom-call | flops 1409286144 | bytes 4194304 | tf_op jit(solution)/shard_map/pallas_call | solution.py:252
  116.2 2.6 %collective-permute-done.18.refs_3_ = f32[16,128,128]{2,1,0:T(8,128)} collective-permute-done((f32[16,128,128]{2,1,0:T(8,128)}, f32[16,128,128]{2,1,0:T(8,128)}, u32[]{:S(2)}, u32[]{:S(2)}) %collective-permute-start.18) | collective-permute-done | bytes 1048608 | tf_op jit(solution)/shard_map/ppermute | solution.py:21
  120.2 7.0 %shard_map.65 = (f32[2,128,512]{2,1,0:T(8,128)S(1)}, f32[2,128,512]{2,1,0:T(8,128)S(1)}) custom-call(s32[3]{0:T(128)S(1)} %copy-done.1, f32[64,128,128]{2,1,0:T(8,128)} %bitcast.114, f32[16,128,128]{2,1,0:T(8,128)} %collective-permute-done.16.refs_1_, f32[16,128,128]{2,1,0:T(8,128)} %collective-permute-done.17.refs_2_, ...), custom_call_target="tpu_custom_call" | custom-call | flops 3221225472 | bytes 8388608 | tf_op jit(solution)/shard_map/pallas_call | solution.py:308
  130.6 11.7 %collective-permute-done.42 = f32[4,32,512]{2,1,0:T(8,128)S(1)} collective-permute-done((f32[4,32,512]{2,1,0:T(8,128)S(1)}, f32[4,32,512]{2,1,0:T(8,128)S(1)}, u32[]{:S(2)}, u32[]{:S(2)}) %collective-permute-start.42) | collective-permute-done | bytes 262176 | tf_op jit(solution)/shard_map/ppermute | solution.py:21
  142.3 2.4 %collective-permute-start.45 = (f32[32,512]{1,0:T(8,128)S(1)}, f32[32,512]{1,0:T(8,128)S(1)}, u32[]{:S(2)}, u32[]{:S(2)}) collective-permute-start(f32[32,512]{1,0:T(8,128)S(1)} %get-tuple-element.112), channel_id=1, source_target_pairs={{0,6},{2,4},{4,2},{6,0},{1,7},{3,5},{5,3},{7,1},{8,14},{10,12},{12... | collective-permute-start | bytes 196616 | tf_op jit(solution)/shard_map/ppermute | solution.py:21
  144.8 1.7 collective-permute-start.44
  147.4 2.2 %collective-permute-start.43 = (f32[32,512]{1,0:T(8,128)S(1)}, f32[32,512]{1,0:T(8,128)S(1)}, u32[]{:S(2)}, u32[]{:S(2)}) collective-permute-start(f32[32,512]{1,0:T(8,128)S(1)} %get-tuple-element.111), channel_id=1, source_target_pairs={{0,2},{2,0},{4,6},{6,4},{1,3},{3,1},{5,7},{7,5},{8,10},{10,8},{12,... | collective-permute-start | bytes 196616 | tf_op jit(solution)/shard_map/ppermute | solution.py:21
  155.0 8.0 %collective-permute-done.37 = f32[1,4,2,64,128]{4,3,2,1,0:T(8,128)S(1)} collective-permute-done((f32[1,4,2,64,128]{4,3,2,1,0:T(8,128)S(1)}, f32[1,4,2,64,128]{4,3,2,1,0:T(8,128)S(1)}, u32[]{:S(2)}, u32[]{:S(2)}) %collective-permute-start.37) | collective-permute-done | bytes 262176 | tf_op jit(solution)/shard_map/ppermute | solution.py:21
  163.8 3.0 %collective-permute-start.31 = (f32[2,64,128]{2,1,0:T(8,128)S(1)}, f32[2,64,128]{2,1,0:T(8,128)S(1)}, u32[]{:S(2)}, u32[]{:S(2)}) collective-permute-start(f32[2,64,128]{2,1,0:T(8,128)S(1)} %get-tuple-element.84), channel_id=1, source_target_pairs={{0,4},{2,6},{4,0},{6,2},{1,5},{3,7},{5,1},{7,3},{8,12},{10,14},{12... | collective-permute-start | bytes 196616 | tf_op jit(solution)/shard_map/ppermute | solution.py:21
  169.8 2.0 %collective-permute-start.22 = (f32[5,64,128]{2,1,0:T(8,128)S(1)}, f32[5,64,128]{2,1,0:T(8,128)S(1)}, u32[]{:S(2)}, u32[]{:S(2)}) collective-permute-start(f32[5,64,128]{2,1,0:T(8,128)S(1)} %get-tuple-element.72), channel_id=1, source_target_pairs={{0,2},{2,0},{4,6},{6,4},{1,3},{3,1},{5,7},{7,5},{8,10},{10,8},{12,... | collective-permute-start | bytes 491528 | tf_op jit(solution)/shard_map/ppermute | solution.py:21
  175.8 3.7 %collective-permute-done.48.refs_2_ = f32[32,512]{1,0:T(8,128)S(1)} collective-permute-done((f32[32,512]{1,0:T(8,128)S(1)}, f32[32,512]{1,0:T(8,128)S(1)}, u32[]{:S(2)}, u32[]{:S(2)}) %collective-permute-start.48) | collective-permute-done | bytes 65568 | tf_op jit(solution)/shard_map/ppermute | solution.py:21
  179.4 2.0 collective-permute-start.39
  183.8 10.6 %collective-permute-done.39.refs_10_ = f32[2,64,128]{2,1,0:T(8,128)S(1)} collective-permute-done((f32[2,64,128]{2,1,0:T(8,128)S(1)}, f32[2,64,128]{2,1,0:T(8,128)S(1)}, u32[]{:S(2)}, u32[]{:S(2)}) %collective-permute-start.39) | collective-permute-done | bytes 65568 | tf_op jit(solution)/shard_map/ppermute | solution.py:21
  194.5 2.2 %shard_map.72 = (f32[64,64,64]{2,1,0:T(8,128)}, f32[16,512]{1,0:T(8,128)}) custom-call(s32[3]{0:T(128)S(1)} %copy-done.1, f32[5,64,128]{2,1,0:T(8,128)S(1)} %get-tuple-element.71.refs_0_, f32[5,64,128]{2,1,0:T(8,128)S(1)} %collective-permute-done.22.refs_1_, f32[5,64,128]{2,1,0:T(8,128)S(1)} %collective-permute-done.23.refs_2_, ...), custom_call_target="tpu_custom_call" | custom-call | flops 1000 | bytes 3145728 | tf_op jit(solution)/shard_map/pallas_call | solution.py:389
  (138 shorter events, 34.1 us)
Async XLA Ops:
  1.4 17.5 %collective-permute-start.5 = (f32[32,256]{1,0:T(8,128)S(1)}, f32[32,256]{1,0:T(8,128)S(1)}, u32[]{:S(2)}, u32[]{:S(2)}) collective-permute-start(f32[32,256]{1,0:T(8,128)S(1)} %dynamic-slice_bitcast_fusion), channel_id=1, source_target_pairs={{0,6},{2,4},{4,2},{6,0},{1,7},{3,5},{5,3},{7,1},{8,14},{10,12},{12... | collective-permute-start | bytes 98312 | tf_op jit(solution)/shard_map/ppermute | solution.py:21
  6.5 12.4 %collective-permute-start.4 = (f32[32,256]{1,0:T(8,128)S(1)}, f32[32,256]{1,0:T(8,128)S(1)}, u32[]{:S(2)}, u32[]{:S(2)}) collective-permute-start(f32[32,256]{1,0:T(8,128)S(1)} %dynamic-slice_bitcast_fusion), channel_id=1, source_target_pairs={{0,4},{2,6},{4,0},{6,2},{1,5},{3,7},{5,1},{7,3},{8,12},{10,14},{12... | collective-permute-start | bytes 98312 | tf_op jit(solution)/shard_map/ppermute | solution.py:21
  6.5 12.4 %collective-permute-start.3 = (f32[32,256]{1,0:T(8,128)S(1)}, f32[32,256]{1,0:T(8,128)S(1)}, u32[]{:S(2)}, u32[]{:S(2)}) collective-permute-start(f32[32,256]{1,0:T(8,128)S(1)} %dynamic-slice_bitcast_fusion), channel_id=1, source_target_pairs={{0,2},{2,0},{4,6},{6,4},{1,3},{3,1},{5,7},{7,5},{8,10},{10,8},{12,... | collective-permute-start | bytes 98312 | tf_op jit(solution)/shard_map/ppermute | solution.py:21
  12.2 20.9 %collective-permute-start = (f32[4,128,128]{2,1,0:T(8,128)}, f32[4,128,128]{2,1,0:T(8,128)S(1)}, u32[]{:S(2)}, u32[]{:S(2)}) collective-permute-start(f32[4,128,128]{2,1,0:T(8,128)} %get-tuple-element.53), channel_id=1, source_target_pairs={{0,2},{2,0},{4,6},{6,4},{1,3},{3,1},{5,7},{7,5},{8,10},{10,8},{12,... | collective-permute-start | bytes 786440 | tf_op jit(solution)/shard_map/ppermute | solution.py:21
  15.9 21.5 %collective-permute-start.1 = (f32[4,128,128]{2,1,0:T(8,128)}, f32[4,128,128]{2,1,0:T(8,128)S(1)}, u32[]{:S(2)}, u32[]{:S(2)}) collective-permute-start(f32[4,128,128]{2,1,0:T(8,128)} %shard_map.60), channel_id=1, source_target_pairs={{0,4},{2,6},{4,0},{6,2},{1,5},{3,7},{5,1},{7,3},{8,12},{10,14},{12... | collective-permute-start | bytes 786440 | tf_op jit(solution)/shard_map/ppermute | solution.py:21
  18.9 18.6 %collective-permute-start.2 = (f32[4,128,128]{2,1,0:T(8,128)S(1)}, f32[4,128,128]{2,1,0:T(8,128)S(1)}, u32[]{:S(2)}, u32[]{:S(2)}) collective-permute-start(f32[4,128,128]{2,1,0:T(8,128)S(1)} %copy-done.15), channel_id=1, source_target_pairs={{0,6},{2,4},{4,2},{6,0},{1,7},{3,5},{5,3},{7,1},{8,14},{10,12},{12... | collective-permute-start | bytes 786440 | tf_op jit(solution)/shard_map/ppermute | solution.py:21
  23.8 32.4 %collective-permute-start.11 = (f32[4,128,128]{2,1,0:T(8,128)}, f32[4,128,128]{2,1,0:T(8,128)S(1)}, u32[]{:S(2)}, u32[]{:S(2)}) collective-permute-start(f32[4,128,128]{2,1,0:T(8,128)} %get-tuple-element.60), channel_id=1, source_target_pairs={{0,2},{2,0},{4,6},{6,4},{1,3},{3,1},{5,7},{7,5},{8,10},{10,8},{12,... | collective-permute-start | bytes 786440 | tf_op jit(solution)/shard_map/ppermute | solution.py:21
  29.3 41.7 %collective-permute-start.12 = (f32[4,128,128]{2,1,0:T(8,128)S(1)}, f32[4,128,128]{2,1,0:T(8,128)S(1)}, u32[]{:S(2)}, u32[]{:S(2)}) collective-permute-start(f32[4,128,128]{2,1,0:T(8,128)S(1)} %copy-done.17), channel_id=1, source_target_pairs={{0,4},{2,6},{4,0},{6,2},{1,5},{3,7},{5,1},{7,3},{8,12},{10,14},{12... | collective-permute-start | bytes 786440 | tf_op jit(solution)/shard_map/ppermute | solution.py:21
  33.1 37.9 %collective-permute-start.13 = (f32[4,128,128]{2,1,0:T(8,128)S(1)}, f32[4,128,128]{2,1,0:T(8,128)S(1)}, u32[]{:S(2)}, u32[]{:S(2)}) collective-permute-start(f32[4,128,128]{2,1,0:T(8,128)S(1)} %copy-done.16), channel_id=1, source_target_pairs={{0,6},{2,4},{4,2},{6,0},{1,7},{3,5},{5,3},{7,1},{8,14},{10,12},{12... | collective-permute-start | bytes 786440 | tf_op jit(solution)/shard_map/ppermute | solution.py:21
  37.5 35.0 %collective-permute-start.25 = (f32[4,128,128]{2,1,0:T(8,128)}, f32[4,128,128]{2,1,0:T(8,128)S(1)}, u32[]{:S(2)}, u32[]{:S(2)}) collective-permute-start(f32[4,128,128]{2,1,0:T(8,128)} %get-tuple-element.76), channel_id=1, source_target_pairs={{0,2},{2,0},{4,6},{6,4},{1,3},{3,1},{5,7},{7,5},{8,10},{10,8},{12,... | collective-permute-start | bytes 786440 | tf_op jit(solution)/shard_map/ppermute | solution.py:21
  38.2 44.0 %collective-permute-start.26 = (f32[4,128,128]{2,1,0:T(8,128)}, f32[4,128,128]{2,1,0:T(8,128)S(1)}, u32[]{:S(2)}, u32[]{:S(2)}) collective-permute-start(f32[4,128,128]{2,1,0:T(8,128)} %get-tuple-element.77), channel_id=1, source_target_pairs={{0,4},{2,6},{4,0},{6,2},{1,5},{3,7},{5,1},{7,3},{8,12},{10,14},{12... | collective-permute-start | bytes 786440 | tf_op jit(solution)/shard_map/ppermute | solution.py:21
  56.2 26.0 %collective-permute-start.27 = (f32[4,128,128]{2,1,0:T(8,128)}, f32[4,128,128]{2,1,0:T(8,128)S(1)}, u32[]{:S(2)}, u32[]{:S(2)}) collective-permute-start(f32[4,128,128]{2,1,0:T(8,128)} %get-tuple-element.78), channel_id=1, source_target_pairs={{0,6},{2,4},{4,2},{6,0},{1,7},{3,5},{5,3},{7,1},{8,14},{10,12},{12... | collective-permute-start | bytes 786440 | tf_op jit(solution)/shard_map/ppermute | solution.py:21
  71.0 44.6 %collective-permute-start.16 = (f32[16,128,128]{2,1,0:T(8,128)}, f32[16,128,128]{2,1,0:T(8,128)}, u32[]{:S(2)}, u32[]{:S(2)}) collective-permute-start(f32[16,128,128]{2,1,0:T(8,128)} %get-tuple-element.66), channel_id=1, source_target_pairs={{0,8},{8,0},{16,24},{24,16},{1,9},{9,1},{17,25},{25,17},{2,10},{10... | collective-permute-start | bytes 3145736 | tf_op jit(solution)/shard_map/ppermute | solution.py:21
  71.0 45.1 %collective-permute-start.17 = (f32[16,128,128]{2,1,0:T(8,128)}, f32[16,128,128]{2,1,0:T(8,128)}, u32[]{:S(2)}, u32[]{:S(2)}) collective-permute-start(f32[16,128,128]{2,1,0:T(8,128)} %get-tuple-element.67), channel_id=1, source_target_pairs={{0,16},{8,24},{16,0},{24,8},{1,17},{9,25},{17,1},{25,9},{2,18},{10... | collective-permute-start | bytes 3145736 | tf_op jit(solution)/shard_map/ppermute | solution.py:21
  72.5 46.3 %collective-permute-start.18 = (f32[16,128,128]{2,1,0:T(8,128)}, f32[16,128,128]{2,1,0:T(8,128)}, u32[]{:S(2)}, u32[]{:S(2)}) collective-permute-start(f32[16,128,128]{2,1,0:T(8,128)} %get-tuple-element.68), channel_id=1, source_target_pairs={{0,24},{8,16},{16,8},{24,0},{1,25},{9,17},{17,9},{25,1},{2,26},{10... | collective-permute-start | bytes 3145736 | tf_op jit(solution)/shard_map/ppermute | solution.py:21
  82.2 17.4 %collective-permute-start.34 = (f32[4,128,128]{2,1,0:T(8,128)S(1)}, f32[4,128,128]{2,1,0:T(8,128)}, u32[]{:S(2)}, u32[]{:S(2)}) collective-permute-start(f32[4,128,128]{2,1,0:T(8,128)S(1)} %copy-done.6), channel_id=1, source_target_pairs={{0,4},{2,6},{4,0},{6,2},{1,5},{3,7},{5,1},{7,3},{8,12},{10,14},{12... | collective-permute-start | bytes 786440 | tf_op jit(solution)/shard_map/ppermute | solution.py:21
  93.2 22.2 %collective-permute-start.9 = (f32[2,4,2,64,128]{4,3,2,1,0:T(8,128)S(1)}, f32[2,4,2,64,128]{4,3,2,1,0:T(8,128)S(1)}, u32[]{:S(2)}, u32[]{:S(2)}) collective-permute-start(f32[2,4,2,64,128]{4,3,2,1,0:T(8,128)S(1)} %get-tuple-element.58), channel_id=1, source_target_pairs={{0,8},{8,0},{16,24},{24,16},{1,9},{9,1},{17,25},{25,17},{2,10},{10... | collective-permute-start | bytes 1572872 | tf_op jit(solution)/shard_map/ppermute | solution.py:21
  110.0 18.2 %collective-permute-start.14 = (f32[2,4,2,64,128]{4,3,2,1,0:T(8,128)S(1)}, f32[2,4,2,64,128]{4,3,2,1,0:T(8,128)S(1)}, u32[]{:S(2)}, u32[]{:S(2)}) collective-permute-start(f32[2,4,2,64,128]{4,3,2,1,0:T(8,128)S(1)} %get-tuple-element.65), channel_id=1, source_target_pairs={{0,8},{8,0},{16,24},{24,16},{1,9},{9,1},{17,25},{25,17},{2,10},{10... | collective-permute-start | bytes 1572872 | tf_op jit(solution)/shard_map/ppermute | solution.py:21
  115.4 11.8 %collective-permute-start.28 = (f32[2,4,2,64,128]{4,3,2,1,0:T(8,128)S(1)}, f32[2,4,2,64,128]{4,3,2,1,0:T(8,128)S(1)}, u32[]{:S(2)}, u32[]{:S(2)}) collective-permute-start(f32[2,4,2,64,128]{4,3,2,1,0:T(8,128)S(1)} %get-tuple-element.81), channel_id=1, source_target_pairs={{0,8},{8,0},{16,24},{24,16},{1,9},{9,1},{17,25},{25,17},{2,10},{10... | collective-permute-start | bytes 1572872 | tf_op jit(solution)/shard_map/ppermute | solution.py:21
  115.6 14.9 %collective-permute-start.36 = (f32[2,4,2,64,128]{4,3,2,1,0:T(8,128)S(1)}, f32[2,4,2,64,128]{4,3,2,1,0:T(8,128)S(1)}, u32[]{:S(2)}, u32[]{:S(2)}) collective-permute-start(f32[2,4,2,64,128]{4,3,2,1,0:T(8,128)S(1)} %get-tuple-element.92), channel_id=1, source_target_pairs={{0,8},{8,0},{16,24},{24,16},{1,9},{9,1},{17,25},{25,17},{2,10},{10... | collective-permute-start | bytes 1572872 | tf_op jit(solution)/shard_map/ppermute | solution.py:21
  118.8 48.0 %collective-permute-start.10 = (f32[1,4,2,64,128]{4,3,2,1,0:T(8,128)S(1)}, f32[1,4,2,64,128]{4,3,2,1,0:T(8,128)S(1)}, u32[]{:S(2)}, u32[]{:S(2)}) collective-permute-start(f32[1,4,2,64,128]{4,3,2,1,0:T(8,128)S(1)} %get-tuple-element.109), channel_id=1, source_target_pairs={{0,16},{8,24},{16,0},{24,8},{1,17},{9,25},{17,1},{25,9},{2,18},{10... | collective-permute-start | bytes 786440 | tf_op jit(solution)/shard_map/ppermute | solution.py:21
  127.5 26.4 %collective-permute-start.29 = (f32[1,4,2,64,128]{4,3,2,1,0:T(8,128)S(1)}, f32[1,4,2,64,128]{4,3,2,1,0:T(8,128)S(1)}, u32[]{:S(2)}, u32[]{:S(2)}) collective-permute-start(f32[1,4,2,64,128]{4,3,2,1,0:T(8,128)S(1)} %get-tuple-element.103), channel_id=1, source_target_pairs={{0,16},{8,24},{16,0},{24,8},{1,17},{9,25},{17,1},{25,9},{2,18},{10... | collective-permute-start | bytes 786440 | tf_op jit(solution)/shard_map/ppermute | solution.py:21
  128.2 14.1 %collective-permute-start.42 = (f32[4,32,512]{2,1,0:T(8,128)S(1)}, f32[4,32,512]{2,1,0:T(8,128)S(1)}, u32[]{:S(2)}, u32[]{:S(2)}) collective-permute-start(f32[4,32,512]{2,1,0:T(8,128)S(1)} %fusion.4), channel_id=1, source_target_pairs={{0,16},{8,24},{16,0},{24,8},{1,17},{9,25},{17,1},{25,9},{2,18},{10... | collective-permute-start | bytes 786440 | tf_op jit(solution)/shard_map/ppermute | solution.py:21
  129.8 17.6 %collective-permute-start.20 = (f32[1,128,512]{2,1,0:T(8,128)S(1)}, f32[1,128,512]{2,1,0:T(8,128)S(1)}, u32[]{:S(2)}, u32[]{:S(2)}) collective-permute-start(f32[1,128,512]{2,1,0:T(8,128)S(1)} %get-tuple-element.106), channel_id=1, source_target_pairs={{0,16},{8,24},{16,0},{24,8},{1,17},{9,25},{17,1},{25,9},{2,18},{10... | collective-permute-start | bytes 786440 | tf_op jit(solution)/shard_map/ppermute | solution.py:21
  150.3 17.8 %collective-permute-start.15 = (f32[1,4,2,64,128]{4,3,2,1,0:T(8,128)S(1)}, f32[1,4,2,64,128]{4,3,2,1,0:T(8,128)S(1)}, u32[]{:S(2)}, u32[]{:S(2)}) collective-permute-start(f32[1,4,2,64,128]{4,3,2,1,0:T(8,128)S(1)} %get-tuple-element.107), channel_id=1, source_target_pairs={{0,16},{8,24},{16,0},{24,8},{1,17},{9,25},{17,1},{25,9},{2,18},{10... | collective-permute-start | bytes 786440 | tf_op jit(solution)/shard_map/ppermute | solution.py:21
  150.8 12.2 %collective-permute-start.37 = (f32[1,4,2,64,128]{4,3,2,1,0:T(8,128)S(1)}, f32[1,4,2,64,128]{4,3,2,1,0:T(8,128)S(1)}, u32[]{:S(2)}, u32[]{:S(2)}) collective-permute-start(f32[1,4,2,64,128]{4,3,2,1,0:T(8,128)S(1)} %get-tuple-element.101), channel_id=1, source_target_pairs={{0,16},{8,24},{16,0},{24,8},{1,17},{9,25},{17,1},{25,9},{2,18},{10... | collective-permute-start | bytes 786440 | tf_op jit(solution)/shard_map/ppermute | solution.py:21
  152.3 15.8 %collective-permute-start.21 = (f32[4,16,512]{2,1,0:T(8,128)}, f32[4,16,512]{2,1,0:T(8,128)}, u32[]{:S(2)}, u32[]{:S(2)}) collective-permute-start(f32[4,16,512]{2,1,0:T(8,128)} %fusion.5), channel_id=1, source_target_pairs={{0,1},{1,0},{2,3},{3,2},{4,5},{5,4},{6,7},{7,6},{8,9},{9,8},{10,11... | collective-permute-start | bytes 393224 | tf_op jit(solution)/shard_map/ppermute | solution.py:21
  169.8 24.7 %collective-permute-start.22 = (f32[5,64,128]{2,1,0:T(8,128)S(1)}, f32[5,64,128]{2,1,0:T(8,128)S(1)}, u32[]{:S(2)}, u32[]{:S(2)}) collective-permute-start(f32[5,64,128]{2,1,0:T(8,128)S(1)} %get-tuple-element.72), channel_id=1, source_target_pairs={{0,2},{2,0},{4,6},{6,4},{1,3},{3,1},{5,7},{7,5},{8,10},{10,8},{12,... | collective-permute-start | bytes 491528 | tf_op jit(solution)/shard_map/ppermute | solution.py:21
  171.8 22.7 %collective-permute-start.23 = (f32[5,64,128]{2,1,0:T(8,128)S(1)}, f32[5,64,128]{2,1,0:T(8,128)S(1)}, u32[]{:S(2)}, u32[]{:S(2)}) collective-permute-start(f32[5,64,128]{2,1,0:T(8,128)S(1)} %get-tuple-element.73), channel_id=1, source_target_pairs={{0,4},{2,6},{4,0},{6,2},{1,5},{3,7},{5,1},{7,3},{8,12},{10,14},{12... | collective-permute-start | bytes 491528 | tf_op jit(solution)/shard_map/ppermute | solution.py:21
  173.1 21.4 %collective-permute-start.24 = (f32[5,64,128]{2,1,0:T(8,128)S(1)}, f32[5,64,128]{2,1,0:T(8,128)S(1)}, u32[]{:S(2)}, u32[]{:S(2)}) collective-permute-start(f32[5,64,128]{2,1,0:T(8,128)S(1)} %get-tuple-element.74), channel_id=1, source_target_pairs={{0,6},{2,4},{4,2},{6,0},{1,7},{3,5},{5,3},{7,1},{8,14},{10,12},{12... | collective-permute-start | bytes 491528 | tf_op jit(solution)/shard_map/ppermute | solution.py:21
  179.4 15.1 %collective-permute-start.39 = (f32[2,64,128]{2,1,0:T(8,128)S(1)}, f32[2,64,128]{2,1,0:T(8,128)S(1)}, u32[]{:S(2)}, u32[]{:S(2)}) collective-permute-start(f32[2,64,128]{2,1,0:T(8,128)S(1)} %get-tuple-element.95), channel_id=1, source_target_pairs={{0,4},{2,6},{4,0},{6,2},{1,5},{3,7},{5,1},{7,3},{8,12},{10,14},{12... | collective-permute-start | bytes 196616 | tf_op jit(solution)/shard_map/ppermute | solution.py:21
  181.4 13.1 %collective-permute-start.40 = (f32[2,64,128]{2,1,0:T(8,128)S(1)}, f32[2,64,128]{2,1,0:T(8,128)S(1)}, u32[]{:S(2)}, u32[]{:S(2)}) collective-permute-start(f32[2,64,128]{2,1,0:T(8,128)S(1)} %get-tuple-element.96), channel_id=1, source_target_pairs={{0,6},{2,4},{4,2},{6,0},{1,7},{3,5},{5,3},{7,1},{8,14},{10,12},{12... | collective-permute-start | bytes 196616 | tf_op jit(solution)/shard_map/ppermute | solution.py:21
  (37 other events, 455.2 us)
